TPU v7x, 32 devices: a whole 2x2x4 slice. The times are simulated.
32 devices in a mesh: dp: 4 (over y, core), expert: 8 (over z, x).
Axes of the slice: x: 2, y: 2, z: 4, core: 2. Of those that a mesh axis runs over, the one named last changes fastest.
Arguments:
- tokens: bfloat16 [4096, 1024], P(('dp', 'expert')), may hold values from -6 to 6
- norm_gain: bfloat16 [1024], P('dp'), may hold values from 0.25 to 1.75
- qkv_weight: bfloat16 [1024, 3072], P('dp'), may hold values from -0.1875 to 0.1875
- out_weight: bfloat16 [1024, 1024], P('dp'), may hold values from -3 to 3
- centroids: bfloat16 [8, 1024], P(None, 'dp'), may hold values from -0.09375 to 0.09375
- expert_gain: bfloat16 [8, 2, 1024], P('expert', None, 'dp'), may hold values from 0.25 to 1.75
- expert_in: bfloat16 [8, 2, 4096, 1024], P('expert', None, 'dp'), may hold values from -0.1875 to 0.1875
- expert_out: bfloat16 [8, 2, 4096, 1024], P('expert', None, 'dp'), may hold values from -0.09375 to 0.09375
- routes: int32 [4096, 1], P(('dp', 'expert')), may hold values from 0 to 7; in each aligned block of 128 rows (0 to 127, 128 to 255, ...) at most 24 rows name the same one
- cotangent: bfloat16 [4096, 1024], P(('dp', 'expert')), may hold values from -6 to 6
Outputs:
- block_out: bfloat16 [4096, 1024], P(('dp', 'expert'))
- grad_tokens: float32 [4096, 1024], P(('dp', 'expert'))
- grad_norm_gain: float32 [1024], P('dp')
- grad_qkv: float32 [1024, 3072], P('dp')
- grad_out_weight: float32 [1024, 1024], P('dp')
- grad_centroids: float32 [8, 1024], P(None, 'dp')
- grad_expert_gain: float32 [8, 2, 1024], P('expert', None, 'dp')
- grad_expert_in: float32 [8, 2, 4096, 1024], P('expert', None, 'dp')
- grad_expert_out: float32 [8, 2, 4096, 1024], P('expert', None, 'dp')
Inputs may be any that keep to these rules, and one draw needn't show every extreme that they name: `routes`: in each aligned block of 128 rows (the rows of one device) no expert is named by more than 24 rows, a bound that some block reaches.
All inputs are finite; a program needn't handle non-finite values.
Results may differ from a plain program's by a relative error of at most 0.04.
Values may be sent and summed in bfloat16 or wider, within the bound.
A program may use at most 256 MiB of HBM per device.

v0:
```python
from functools import partial

import jax
import jax.numpy as jnp
from jax import lax
from jax.sharding import PartitionSpec as P

HEADS = 16
HEAD = 64
BLOCK = 256


EPS = 1e-05
NEGATIVE = -1e30
HIGH = lax.Precision.HIGHEST


def normalize(inputs, gain_row):
    centered = inputs - jnp.mean(inputs, axis=-1, keepdims=True)
    inverse = lax.rsqrt(jnp.mean(centered * centered, axis=-1, keepdims=True) + EPS)
    unit_rows = centered * inverse
    return (unit_rows, inverse, unit_rows * gain_row)


def norm_backward(grad_normed, unit_rows, inverse, gain_row):
    grad_unit = grad_normed * gain_row
    first_mean = jnp.mean(grad_unit, axis=-1, keepdims=True)
    second_mean = jnp.mean(grad_unit * unit_rows, axis=-1, keepdims=True)
    grad_input = inverse * (grad_unit - first_mean - unit_rows * second_mean)
    return (grad_input, jnp.sum(grad_normed * unit_rows, axis=0))


def split_heads(matrix):
    return matrix.reshape(matrix.shape[0], HEADS, HEAD)


def exact_gelu(inputs):
    return jax.nn.gelu(inputs, approximate=False)


def keep_state(current):
    return current


def row_product(left_rows, right_matrix, offset, amount):
    return jnp.dot(left_rows, right_matrix, preferred_element_type=jnp.float32)


def fetch_dense(norm_gain, qkv_weight, out_weight, centroids, expert_gain):
    return (
        lax.all_gather(norm_gain, "dp", axis=0, tiled=True),
        lax.all_gather(qkv_weight, "dp", axis=0, tiled=True),
        lax.all_gather(out_weight, "dp", axis=0, tiled=True),
        lax.all_gather(centroids, "dp", axis=1, tiled=True),
        lax.all_gather(expert_gain, "dp", axis=2, tiled=True),
    )


def spread_rows(rows_low):
    return lax.all_gather(rows_low, "dp", axis=0, tiled=True)


def sum_rows(term, amount):
    return lax.psum_scatter(
        term(jnp.int32(0), amount * lax.axis_size("dp")).astype(jnp.bfloat16),
        "dp",
        scatter_dimension=0,
        tiled=True,
    ).astype(jnp.float32)


def send_slots(rows_low, target, experts, capacity):
    buffer_rows = (
        jnp.zeros((experts * capacity, rows_low.shape[1]), rows_low.dtype).at[target].set(rows_low)
    )
    return buffer_rows.reshape(experts, capacity, rows_low.shape[1])


def on_device(
    tokens,
    norm_gain,
    qkv_weight,
    out_weight,
    centroids,
    expert_gain,
    expert_in,
    expert_out,
    routes,
    cotangent,
):
    model_width = tokens.shape[1]
    local_rows = tokens.shape[0]
    experts = lax.axis_size("expert")
    capacity = max(2, 3 * local_rows // (2 * experts))
    slot_total = experts * capacity
    first_pos = lax.axis_index("expert") * local_rows
    scale = HEAD ** (-0.5)
    gain_full, qkv_full, out_full, centroid_full, expert_gain_full = fetch_dense(
        norm_gain, qkv_weight, out_weight, centroids, expert_gain
    )
    inputs = tokens.astype(jnp.float32)
    unit_attn, inverse_attn, normed_attn = normalize(inputs, gain_full.astype(jnp.float32))
    normed_low = normed_attn.astype(jnp.bfloat16)
    projected = jnp.dot(normed_low, qkv_full, preferred_element_type=jnp.float32).astype(
        jnp.bfloat16
    )
    queries = projected[:, :model_width]
    keyset = projected[:, model_width : 2 * model_width]
    values = projected[:, 2 * model_width :]
    query_heads = split_heads(queries)
    key_heads = split_heads(keyset)
    value_heads = split_heads(values)
    query_block = (first_pos + jnp.arange(local_rows, dtype=jnp.int32)) // BLOCK
    last_block = (first_pos + local_rows - 1) // BLOCK
    start_state = (
        jnp.zeros((local_rows, HEADS, HEAD), jnp.float32),
        jnp.full((HEADS, local_rows), NEGATIVE, jnp.float32),
        jnp.zeros((HEADS, local_rows), jnp.float32),
    )
    key_piece = lax.all_gather(keyset, "expert", axis=0, tiled=True)
    value_piece = lax.all_gather(values, "expert", axis=0, tiled=True)
    amount = key_piece.shape[0]

    def update(current):
        accumulated, highest, totals = current
        scores = (
            jnp.einsum(
                "qhd,khd->hqk",
                query_heads,
                split_heads(key_piece),
                preferred_element_type=jnp.float32,
            )
            * scale
        )
        piece_block = jnp.arange(amount, dtype=jnp.int32) // BLOCK
        visible = (piece_block[None, :] <= query_block[:, None])[None]
        scores = jnp.where(visible, scores, NEGATIVE)
        new_high = jnp.maximum(highest, jnp.max(scores, axis=-1))
        factor = jnp.exp(highest - new_high)
        weights = jnp.where(visible, jnp.exp(scores - new_high[:, :, None]), 0.0)
        totals = jnp.sum(weights, axis=-1)
        accumulated = accumulated * factor.T[:, :, None] + jnp.einsum(
            "hqk,khd->qhd",
            weights.astype(jnp.bfloat16),
            split_heads(value_piece),
            preferred_element_type=jnp.float32,
        )
        return (accumulated, new_high, totals)

    accumulated, highest, totals = lax.cond(
        jnp.int32(0) // BLOCK <= last_block, update, keep_state, start_state
    )
    mixed_heads = accumulated / totals.T[:, :, None]
    log_total = (highest + jnp.log(totals)).T
    mixed_low = mixed_heads.reshape(local_rows, model_width).astype(jnp.bfloat16)
    residual = inputs + jnp.dot(mixed_low, out_full, preferred_element_type=jnp.float32)
    route_ids = routes[:, 0]
    chosen = route_ids[:, None] == jnp.arange(experts, dtype=jnp.int32)[None, :]
    centroid_rows = jnp.dot(
        chosen.astype(jnp.bfloat16), centroid_full, preferred_element_type=jnp.float32
    )
    gate_value = jax.nn.sigmoid(jnp.sum(residual * centroid_rows, axis=-1))
    chosen_int = chosen.astype(jnp.int32)
    slot_index = jnp.sum((jnp.cumsum(chosen_int, axis=0) - 1) * chosen_int, axis=-1)
    target = route_ids * capacity + slot_index
    arrived = lax.all_to_all(
        send_slots(residual.astype(jnp.bfloat16), target, experts, capacity),
        "expert",
        split_axis=0,
        concat_axis=0,
        tiled=True,
    )
    expert_state = arrived.reshape(slot_total, model_width).astype(jnp.float32)
    gains_here = expert_gain_full[0].astype(jnp.float32)
    total_change = jnp.zeros_like(expert_state)
    stored = []
    for sublayer in range(2):
        unit_rows, inverse, normed = normalize(expert_state, gains_here[sublayer])
        normed_rows = normed.astype(jnp.bfloat16)
        first_full, second_full = (expert_in[0, sublayer], expert_out[0, sublayer])
        left_rows = spread_rows(normed_rows)
        hidden_pre = jnp.einsum(
            "rd,fd->rf", left_rows, first_full, preferred_element_type=jnp.float32
        )
        hidden_act, slope_pull = jax.vjp(exact_gelu, hidden_pre)
        hidden_low = hidden_act.astype(jnp.bfloat16)
        change = sum_rows(partial(row_product, hidden_low, second_full), slot_total)
        expert_state = expert_state + change
        total_change = total_change + change
        stored.append((unit_rows, inverse, left_rows, hidden_low, slope_pull))
    branch_low = total_change.astype(jnp.bfloat16)
    returned = lax.all_to_all(
        branch_low.reshape(experts, capacity, model_width),
        "expert",
        split_axis=0,
        concat_axis=0,
        tiled=True,
    )
    branch_tok = returned.reshape(slot_total, model_width)[target].astype(jnp.float32)
    block_out = (residual + gate_value[:, None] * branch_tok).astype(jnp.bfloat16)
    gain_full, qkv_full, out_full, centroid_full, expert_gain_full = fetch_dense(
        norm_gain, qkv_weight, out_weight, centroids, expert_gain
    )
    gains_here = expert_gain_full[0].astype(jnp.float32)
    grad_out = cotangent.astype(jnp.float32)
    grad_logit = jnp.sum(grad_out * branch_tok, axis=-1) * gate_value * (1.0 - gate_value)
    grad_centroid = jnp.dot(
        chosen.astype(jnp.float32).T, grad_logit[:, None] * residual, precision=HIGH
    )
    grad_resid = grad_out + grad_logit[:, None] * centroid_rows
    grad_branch = (gate_value[:, None] * grad_out).astype(jnp.bfloat16)
    branch_grads = lax.all_to_all(
        send_slots(grad_branch, target, experts, capacity),
        "expert",
        split_axis=0,
        concat_axis=0,
        tiled=True,
    )
    grad_change = branch_grads.reshape(slot_total, model_width).astype(jnp.float32)
    grad_state = jnp.zeros_like(grad_change)
    gain_grads = [None, None]
    first_grads = [None, None]
    second_grads = [None, None]
    for sublayer in (1, 0):
        unit_rows, inverse, left_rows, hidden_low, slope_pull = stored[sublayer]
        grad_rows_low = (grad_change + grad_state).astype(jnp.bfloat16)
        first_full, second_full = (expert_in[0, sublayer], expert_out[0, sublayer])
        grad_rows = spread_rows(grad_rows_low)
        grad_hidden = jnp.einsum(
            "rd,fd->rf", grad_rows, second_full, preferred_element_type=jnp.float32
        )
        grad_pre = slope_pull(grad_hidden)[0].astype(jnp.bfloat16)
        grad_first = jnp.einsum(
            "rf,rd->fd", grad_pre, left_rows, preferred_element_type=jnp.float32
        )
        grad_second = jnp.einsum(
            "rf,rd->fd", hidden_low, grad_rows, preferred_element_type=jnp.float32
        )
        grad_normed = sum_rows(partial(row_product, grad_pre, first_full), slot_total)
        grad_input, gain_grad = norm_backward(grad_normed, unit_rows, inverse, gains_here[sublayer])
        grad_state = grad_state + grad_input
        gain_grads[sublayer] = gain_grad
        first_grads[sublayer] = grad_first
        second_grads[sublayer] = grad_second
    came_back = lax.all_to_all(
        grad_state.astype(jnp.bfloat16).reshape(experts, capacity, model_width),
        "expert",
        split_axis=0,
        concat_axis=0,
        tiled=True,
    )
    grad_resid = grad_resid + came_back.reshape(slot_total, model_width)[target].astype(jnp.float32)
    grad_attended = grad_resid.astype(jnp.bfloat16)
    grad_out_weight = jnp.einsum(
        "rd,re->de", mixed_low, grad_attended, preferred_element_type=jnp.float32
    )
    grad_mixed = jnp.einsum(
        "re,de->rd", grad_attended, out_full, preferred_element_type=jnp.float32
    ).astype(jnp.bfloat16)
    grad_heads = split_heads(grad_mixed)
    delta_rows = jnp.sum(grad_heads.astype(jnp.float32) * mixed_heads, axis=-1)
    zero_heads = jnp.zeros((local_rows, HEADS, HEAD), jnp.float32)
    running = (zero_heads, zero_heads, zero_heads)
    offset = jnp.int32(0)
    fold_key_piece = lax.all_gather(keyset, "expert", axis=0, tiled=True)
    fold_value_piece = lax.all_gather(values, "expert", axis=0, tiled=True)
    query_piece = lax.all_gather(queries, "expert", axis=0, tiled=True)
    grad_piece = lax.all_gather(grad_mixed, "expert", axis=0, tiled=True)
    log_piece = lax.all_gather(log_total.astype(jnp.bfloat16), "expert", axis=0, tiled=True).astype(
        jnp.float32
    )
    delta_piece = lax.all_gather(
        delta_rows.astype(jnp.bfloat16), "expert", axis=0, tiled=True
    ).astype(jnp.float32)
    fold_amount = fold_key_piece.shape[0]
    piece_block = jnp.arange(fold_amount, dtype=jnp.int32) // BLOCK

    def to_queries(current):
        grad_query, grad_key, grad_value = current
        piece_keys = split_heads(fold_key_piece)
        scores = (
            jnp.einsum("qhd,khd->hqk", query_heads, piece_keys, preferred_element_type=jnp.float32)
            * scale
        )
        visible = (piece_block[None, :] <= query_block[:, None])[None]
        weights = jnp.where(visible, jnp.exp(scores - log_total.T[:, :, None]), 0.0)
        grad_weights = jnp.einsum(
            "qhd,khd->hqk",
            grad_heads,
            split_heads(fold_value_piece),
            preferred_element_type=jnp.float32,
        )
        grad_scores = (weights * (grad_weights - delta_rows.T[:, :, None])).astype(jnp.bfloat16)
        grad_query = (
            jnp.einsum("hqk,khd->qhd", grad_scores, piece_keys, preferred_element_type=jnp.float32)
            * scale
        )
        return (grad_query, grad_key, grad_value)

    def to_keys(current):
        grad_query, grad_key, grad_value = current
        piece_queries = split_heads(query_piece)
        piece_grads = split_heads(grad_piece)
        scores = (
            jnp.einsum("qhd,khd->hqk", piece_queries, key_heads, preferred_element_type=jnp.float32)
            * scale
        )
        visible = (query_block[None, :] <= piece_block[:, None])[None]
        weights = jnp.where(visible, jnp.exp(scores - log_piece.T[:, :, None]), 0.0)
        grad_weights = jnp.einsum(
            "qhd,khd->hqk", piece_grads, value_heads, preferred_element_type=jnp.float32
        )
        grad_scores = (weights * (grad_weights - delta_piece.T[:, :, None])).astype(jnp.bfloat16)
        grad_key = (
            grad_key
            + jnp.einsum(
                "hqk,qhd->khd", grad_scores, piece_queries, preferred_element_type=jnp.float32
            )
            * scale
        )
        grad_value = grad_value + jnp.einsum(
            "hqk,qhd->khd",
            weights.astype(jnp.bfloat16),
            piece_grads,
            preferred_element_type=jnp.float32,
        )
        return (grad_query, grad_key, grad_value)

    running = lax.cond(offset // BLOCK <= last_block, to_queries, keep_state, running)
    grad_query, grad_key, grad_value = lax.cond(
        query_block[0] <= (offset + fold_amount - 1) // BLOCK, to_keys, keep_state, running
    )
    grad_qkv_rows = jnp.concatenate(
        [
            grad_query.reshape(local_rows, model_width),
            grad_key.reshape(local_rows, model_width),
            grad_value.reshape(local_rows, model_width),
        ],
        axis=1,
    ).astype(jnp.bfloat16)
    grad_qkv = jnp.einsum(
        "rd,re->de", normed_low, grad_qkv_rows, preferred_element_type=jnp.float32
    )
    grad_normed_attn = jnp.einsum(
        "re,de->rd", grad_qkv_rows, qkv_full, preferred_element_type=jnp.float32
    )
    grad_input_attn, attn_gain_grad = norm_backward(
        grad_normed_attn, unit_attn, inverse_attn, gain_full.astype(jnp.float32)
    )
    grad_tokens = grad_resid + grad_input_attn
    expert_gain_grad = jnp.stack(gain_grads)[None]
    gain_share, qkv_share, out_share, centroid_share, expert_gain_share = (
        lax.psum_scatter(
            attn_gain_grad.astype(jnp.bfloat16), "dp", scatter_dimension=0, tiled=True
        ).astype(jnp.float32),
        lax.psum_scatter(
            grad_qkv.astype(jnp.bfloat16), "dp", scatter_dimension=0, tiled=True
        ).astype(jnp.float32),
        lax.psum_scatter(
            grad_out_weight.astype(jnp.bfloat16), "dp", scatter_dimension=0, tiled=True
        ).astype(jnp.float32),
        lax.psum_scatter(
            grad_centroid.astype(jnp.bfloat16), "dp", scatter_dimension=1, tiled=True
        ).astype(jnp.float32),
        lax.psum_scatter(
            expert_gain_grad.astype(jnp.bfloat16), "dp", scatter_dimension=2, tiled=True
        ).astype(jnp.float32),
    )
    gain_total, qkv_total, out_total, centroid_total = (
        lax.psum(gain_share.astype(jnp.bfloat16), "expert").astype(jnp.float32),
        lax.psum(qkv_share.astype(jnp.bfloat16), "expert").astype(jnp.float32),
        lax.psum(out_share.astype(jnp.bfloat16), "expert").astype(jnp.float32),
        lax.psum(centroid_share.astype(jnp.bfloat16), "expert").astype(jnp.float32),
    )
    grad_expert_in = jnp.stack(first_grads)[None]
    grad_expert_out = jnp.stack(second_grads)[None]
    return (
        block_out,
        grad_tokens,
        gain_total,
        qkv_total,
        out_total,
        centroid_total,
        expert_gain_share,
        grad_expert_in,
        grad_expert_out,
    )


def solution(mesh):
    in_specs = (
        P(("dp", "expert"), None),
        P("dp"),
        P("dp", None),
        P("dp", None),
        P(None, "dp"),
        P("expert", None, "dp"),
        P("expert", None, "dp", None),
        P("expert", None, "dp", None),
        P(("dp", "expert"), None),
        P(("dp", "expert"), None),
    )
    out_specs = (
        P(("dp", "expert"), None),
        P(("dp", "expert"), None),
        P("dp"),
        P("dp", None),
        P("dp", None),
        P(None, "dp"),
        P("expert", None, "dp"),
        P("expert", None, "dp", None),
        P("expert", None, "dp", None),
    )
    return jax.shard_map(
        on_device, mesh=mesh, in_specs=in_specs, out_specs=out_specs, check_vma=False
    )
```

profile of v0, /device:TPU:0, one launch (start us, length us, event | category | flops | bytes accessed | tf_op | source)
XLA Modules:
  0.0 861.3 jit_solution(7556661330962708018)
XLA Ops:
  16.9 41.8 %all-gather.12.cloned.1.call-done = bf16[1024,3072]{1,0:T(8,128)(2,1)} async-done(((bf16[256,3072]{1,0:T(8,128)(2,1)}), bf16[1024,3072]{1,0:T(8,128)(2,1)}) %all-gather.12.cloned.1.call-update) | async-done | bytes 6291472 | tf_op jit(solution)/shard_map/all_gather | solution.py:52
  72.3 40.4 %all-gather.14.cloned.1.call-done = bf16[1024,1024]{1,0:T(8,128)(2,1)} async-done(((bf16[128,1024]{1,0:T(8,128)(2,1)}), bf16[1024,1024]{1,0:T(8,128)(2,1)}) %all-gather.14.cloned.1.call-update) | async-done | bytes 2097168 | tf_op jit(solution)/shard_map/all_gather | solution.py:120
  112.8 50.4 %all-gather.16.cloned.1.call-done = bf16[1024,1024]{1,0:T(8,128)(2,1)} async-done(((bf16[128,1024]{1,0:T(8,128)(2,1)}), bf16[1024,1024]{1,0:T(8,128)(2,1)}) %all-gather.16.cloned.1.call-update) | async-done | bytes 2097168 | tf_op jit(solution)/shard_map/all_gather | solution.py:121
  163.1 19.1 %conditional.3 = (f32[128,16,64]{0,2,1:T(8,128)S(1)}, f32[16,128]{1,0:T(8,128)}, f32[16,128]{1,0:T(8,128)}, f32[16,128]{1,0:T(8,128)S(1)}) conditional(s32[]{:T(128)} %convert_element_type.204, () %tuple.38, (s32[128]{0:T(128)}, bf16[1024,1024]{1,0:T(8,128)(2,1)}, bf16[128,16,64]{0,2,1:T(8,128)(2,1)}, bf16[1024,1024]{1,0:T(8,128)(2,1)}) %tuple.128), branch_computations={%region_2.3_spmd, %region_3.6_spmd} | conditional | flops 564406272 | bytes 56975988 | solution.py:150
  209.2 17.7 %all-gather.20.cloned.1.call-done = bf16[768,1024]{1,0:T(8,128)(2,1)} async-done(((bf16[192,1024]{1,0:T(8,128)(2,1)}), bf16[768,1024]{1,0:T(8,128)(2,1)}) %all-gather.20.cloned.1.call-update) | async-done | bytes 1572880 | tf_op jit(solution)/shard_map/all_gather | solution.py:60
  226.8 11.7 %multiply_convert_fusion.11 = (bf16[768,1024]{1,0:T(8,128)(2,1)S(1)}, f32[768,1024]{1,0:T(8,128)}, f32[768,1024]{1,0:T(8,128)}) fusion(bf16[768,1024]{1,0:T(8,128)(2,1)} %all-gather.20.cloned.1.call-done, bf16[1,2,1024,1024]{3,2,1,0:T(8,128)(2,1)} %param.22), kind=kOutput, calls=%fused_computation.73 | convolution fusion | flops 1661730816 | bytes 11534336 | tf_op jit(solution)/shard_map/rd,fd->rf/dot_general | solution.py:182
  241.6 28.1 %reduce-scatter.11.cloned.1.call-done = bf16[192,1024]{1,0:T(8,128)(2,1)} async-done(((bf16[768,1024]{1,0:T(8,128)(2,1)}), bf16[192,1024]{1,0:T(8,128)(2,1)}) %reduce-scatter.11.cloned.1.call-update) | async-done | bytes 393232 | tf_op jit(solution)/shard_map/reduce_scatter | solution.py:64
  272.1 19.7 %all-gather.22.cloned.1.call-done = bf16[768,1024]{1,0:T(8,128)(2,1)} async-done(((bf16[192,1024]{1,0:T(8,128)(2,1)}), bf16[768,1024]{1,0:T(8,128)(2,1)}) %all-gather.22.cloned.1.call-update) | async-done | bytes 1572880 | tf_op jit(solution)/shard_map/all_gather | solution.py:60
  291.9 11.7 %multiply_convert_fusion.10 = (bf16[768,1024]{1,0:T(8,128)(2,1)S(1)}, f32[768,1024]{1,0:T(8,128)}, f32[768,1024]{1,0:T(8,128)}) fusion(bf16[768,1024]{1,0:T(8,128)(2,1)} %all-gather.22.cloned.1.call-done, bf16[1,2,1024,1024]{3,2,1,0:T(8,128)(2,1)} %param.22), kind=kOutput, calls=%fused_computation.60 | convolution fusion | flops 1661730816 | bytes 11534336 | tf_op jit(solution)/shard_map/rd,fd->rf/dot_general | solution.py:182
  307.8 28.1 %reduce-scatter.13.cloned.1.call-done = bf16[192,1024]{1,0:T(8,128)(2,1)} async-done(((bf16[768,1024]{1,0:T(8,128)(2,1)}), bf16[192,1024]{1,0:T(8,128)(2,1)}) %reduce-scatter.13.cloned.1.call-update) | async-done | bytes 393232 | tf_op jit(solution)/shard_map/reduce_scatter | solution.py:64
  358.2 15.4 %all_to_all.20 = bf16[8,24,1024]{2,1,0:T(8,128)(2,1)} all-to-all(bf16[8,24,1024]{2,1,0:T(8,128)(2,1)S(1)} %bitcast.169), channel_id=1, replica_groups=mesh['dp'=4,'expert'=8] {'expert'}, dimensions={0} | all-to-all | bytes 786432 | tf_op jit(solution)/shard_map/all_to_all | solution.py:212
  373.7 17.4 %all-gather.24.cloned.1.call-done = bf16[768,1024]{1,0:T(8,128)(2,1)} async-done(((bf16[192,1024]{1,0:T(8,128)(2,1)}), bf16[768,1024]{1,0:T(8,128)(2,1)}) %all-gather.24.cloned.1.call-update) | async-done | bytes 1572880 | tf_op jit(solution)/shard_map/all_gather | solution.py:60
  402.1 28.2 %reduce-scatter.15.cloned.1.call-done = bf16[192,1024]{1,0:T(8,128)(2,1)} async-done(((bf16[768,1024]{1,0:T(8,128)(2,1)}), bf16[192,1024]{1,0:T(8,128)(2,1)}) %reduce-scatter.15.cloned.1.call-update) | async-done | bytes 393232 | tf_op jit(solution)/shard_map/reduce_scatter | solution.py:64
  434.4 19.7 %all-gather.26.cloned.1.call-done = bf16[768,1024]{1,0:T(8,128)(2,1)} async-done(((bf16[192,1024]{1,0:T(8,128)(2,1)}), bf16[768,1024]{1,0:T(8,128)(2,1)}) %all-gather.26.cloned.1.call-update) | async-done | bytes 1572880 | tf_op jit(solution)/shard_map/all_gather | solution.py:60
  465.8 27.4 %reduce-scatter.17.cloned.1.call-done = bf16[192,1024]{1,0:T(8,128)(2,1)} async-done(((bf16[768,1024]{1,0:T(8,128)(2,1)}), bf16[192,1024]{1,0:T(8,128)(2,1)}) %reduce-scatter.17.cloned.1.call-update) | async-done | bytes 393232 | tf_op jit(solution)/shard_map/reduce_scatter | solution.py:64
  497.1 25.4 %all_to_all.21 = bf16[8,24,1024]{2,1,0:T(8,128)(2,1)S(1)} all-to-all(bf16[8,24,1024]{2,1,0:T(8,128)(2,1)S(1)} %bitcast.168), channel_id=1, replica_groups=mesh['dp'=4,'expert'=8] {'expert'}, dimensions={0} | all-to-all | bytes 786432 | tf_op jit(solution)/shard_map/all_to_all | solution.py:245
  532.0 26.3 %all_gather.63 = bf16[1024,16]{0,1:T(8,128)(2,1)S(1)} all-gather(bf16[128,16]{0,1:T(8,128)(2,1)S(1)} %get-tuple-element.167), channel_id=1, replica_groups=mesh['dp'=4,'expert'=8] {'expert'}, dimensions={0}, use_global_device_ids=true | all-gather | bytes 36864 | tf_op jit(solution)/shard_map/all_gather | solution.py:269
  560.2 26.3 %all_gather.65 = bf16[1024,16]{0,1:T(8,128)(2,1)S(1)} all-gather(bf16[128,16]{0,1:T(8,128)(2,1)S(1)} %convert_element_type.247), channel_id=1, replica_groups=mesh['dp'=4,'expert'=8] {'expert'}, dimensions={0}, use_global_device_ids=true | all-gather | bytes 36864 | tf_op jit(solution)/shard_map/all_gather | solution.py:272
  587.2 20.9 %conditional.4 = (bf16[128,1024]{0,1:T(8,128)(2,1)S(1)}) conditional(s32[]{:T(128)} %convert_element_type.204, () %tuple.40, (s32[1024]{0:T(1024)S(1)}, s32[128]{0:T(128)}, bf16[1024,1024]{1,0:T(8,128)(2,1)S(1)}, bf16[128,16,64]{0,2,1:T(8,128)(2,1)S(1)}, f32[16,128]{1,0:T(8,128)S(1)}, /*index=5*/bf16[1024,1024]{1,0:T(8,128)(2,1)}, ...), branch_computations={%region_25.26_spmd, %region_26.27_spmd} | conditional | flops 818282496 | bytes 41964096 | solution.py:329
  608.8 28.7 %conditional.5 = (bf16[128,1024]{0,1:T(8,128)(2,1)S(1)}, bf16[128,1024]{0,1:T(8,128)(2,1)S(1)}) conditional(s32[]{:T(128)} %bitcast.41, () %tuple.42, (s32[128]{0:T(128)}, s32[1024]{0:T(1024)S(1)}, bf16[1024,1024]{1,0:T(8,128)(2,1)}, bf16[128,1024]{1,0:T(8,128)(2,1)S(1)}, f32[1024,16]{0,1:T(8,128)S(1)}, /*index=5*/bf16[1024,1024]{1,0:T(8,128)(2,1)}, ...), branch_computations={%region_27.28_spmd, %region_28.29_spmd} | conditional | flops 1095237632 | bytes 45683328 | solution.py:330
  663.1 35.6 %reduce-scatter.19.cloned.1.call-done = bf16[256,3072]{1,0:T(8,128)(2,1)} async-done(((bf16[1024,3072]{1,0:T(8,128)(2,1)}), bf16[256,3072]{1,0:T(8,128)(2,1)}) %reduce-scatter.19.cloned.1.call-update) | async-done | bytes 1572880 | tf_op jit(solution)/shard_map/reduce_scatter | solution.py:356
  706.4 15.2 %reduce-scatter.25.cloned.1.call-done = bf16[256,2]{1,0:T(8,128)(2,1)} async-done(((bf16[1024,2]{1,0:T(8,128)(2,1)}), bf16[256,2]{1,0:T(8,128)(2,1)}) %reduce-scatter.25.cloned.1.call-update) | async-done | bytes 1040
  743.5 22.6 %all-reduce.1 = (bf16[256]{0:T(256)(128)(2,1)S(1)}, bf16[8,256]{1,0:T(8,128)(2,1)S(1)}) all-reduce(bf16[256]{0:T(256)(128)(2,1)S(1)} %dynamic-slice.1, bf16[8,256]{1,0:T(8,128)(2,1)} %reduce-scatter.23.cloned.1.call-done), channel_id=1, replica_groups=mesh['dp'=4,'expert'=8] {'expert'}, use_global_device_ids=true, to_apply=%region_33.34 | all-reduce | flops 2304 | bytes 9216 | tf_op jit(solution)/shard_map/psum | solution.py:370
  768.3 81.4 %all-reduce.5.cloned.1.call-done = (bf16[256,3072]{1,0:T(8,128)(2,1)}, bf16[256,1024]{1,0:T(8,128)(2,1)}) async-done(((bf16[256,3072]{1,0:T(8,128)(2,1)}, bf16[256,1024]{1,0:T(8,128)(2,1)}), (bf16[256,3072]{1,0:T(8,128)(2,1)}, bf16[256,1024]{1,0:T(8,128)(2,1)})) %all-reduce.5.cloned.1.call-update) | async-done | bytes 2097168 | tf_op jit(solution)/shard_map/psum | solution.py:371
  (305 shorter events, 253.6 us)
Async XLA Ops:
  7.2 51.6 %all-gather.12.cloned.1.call-start = ((), (), s32[]{:S(2)}) async-start(), calls=%async_computation.12 | async-start | bytes 7864320 | tf_op jit(solution)/shard_map/all_gather | solution.py:52
  7.9 104.9 %all-gather.14.cloned.1.call-start = ((), (), s32[]{:S(2)}) async-start(), calls=%async_computation.13 | async-start | bytes 2359296 | tf_op jit(solution)/shard_map/all_gather | solution.py:120
  63.6 99.5 %all-gather.16.cloned.1.call-start = ((), (), s32[]{:S(2)}) async-start(), calls=%async_computation.14 | async-start | bytes 2359296 | tf_op jit(solution)/shard_map/all_gather | solution.py:121
  64.3 121.3 %all-gather.18.cloned.1.call-start = ((), (), s32[]{:S(2)}) async-start(), calls=%async_computation.15 | async-start | bytes 2621440 | tf_op jit(solution)/shard_map/all_gather | solution.py:53
  189.7 17.6 %all-to-all-start = ((bf16[8,24,1024]{2,1,0:T(8,128)(2,1)}), bf16[8,24,1024]{2,1,0:T(8,128)(2,1)S(1)}, u32[]{:S(2)}, u32[]{:S(2)}) async-start(bf16[8,24,1024]{2,1,0:T(8,128)(2,1)} %bitcast.26), calls=%async_computation | async-start | bytes 786432 | tf_op jit(solution)/shard_map/all_to_all | solution.py:166
  195.2 31.6 %all-gather.20.cloned.1.call-start = ((), (), s32[]{:S(2)}) async-start(), calls=%async_computation.16 | async-start | bytes 1966080 | tf_op jit(solution)/shard_map/all_gather | solution.py:60
  207.5 285.6 %copy-start.39 = (f32[192]{0:T(256)}, f32[192]{0:T(256)S(1)}, u32[]{:S(2)}) copy-start(f32[192]{0:T(256)S(1)} %div.108) | copy-start | bytes 2308
  207.9 285.3 %copy-start.40 = (f32[192]{0:T(256)}, f32[192]{0:T(256)S(1)}, u32[]{:S(2)}) copy-start(f32[192]{0:T(256)S(1)} %rsqrt.29) | copy-start | bytes 2308
  208.9 60.8 %reduce-scatter.11.cloned.1.call-start = ((), (), s32[]{:S(2)}) async-start(), calls=%async_computation.17 | async-start | bytes 1966080 | tf_op jit(solution)/shard_map/reduce_scatter | solution.py:64
  241.5 50.3 %all-gather.22.cloned.1.call-start = ((), (), s32[]{:S(2)}) async-start(), calls=%async_computation.18 | async-start | bytes 1966080 | tf_op jit(solution)/shard_map/all_gather | solution.py:60
  271.1 161.1 %copy-start.36 = (f32[192]{0:T(256)}, f32[192]{0:T(256)S(1)}, u32[]{:S(2)}) copy-start(f32[192]{0:T(256)S(1)} %add_rsqrt_fusion.1) | copy-start | bytes 2308
  272.1 63.8 %reduce-scatter.13.cloned.1.call-start = ((), (), s32[]{:S(2)}) async-start(), calls=%async_computation.19 | async-start | bytes 1966080 | tf_op jit(solution)/shard_map/reduce_scatter | solution.py:64
  337.8 17.5 %all-to-all-start.1 = ((bf16[8,24,1024]{2,1,0:T(8,128)(2,1)}), bf16[8,24,1024]{2,1,0:T(8,128)(2,1)S(1)}, u32[]{:S(2)}, u32[]{:S(2)}) async-start(bf16[8,24,1024]{2,1,0:T(8,128)(2,1)} %bitcast.34), calls=%async_computation.3 | async-start | bytes 786432 | tf_op jit(solution)/shard_map/all_to_all | solution.py:192
  343.7 47.5 %all-gather.24.cloned.1.call-start = ((), (), s32[]{:S(2)}) async-start(), calls=%async_computation.20 | async-start | bytes 1966080 | tf_op jit(solution)/shard_map/all_gather | solution.py:60
  373.7 56.5 %reduce-scatter.15.cloned.1.call-start = ((), (), s32[]{:S(2)}) async-start(), calls=%async_computation.21 | async-start | bytes 1966080 | tf_op jit(solution)/shard_map/reduce_scatter | solution.py:64
  402.0 52.2 %all-gather.26.cloned.1.call-start = ((), (), s32[]{:S(2)}) async-start(), calls=%async_computation.22 | async-start | bytes 1966080 | tf_op jit(solution)/shard_map/all_gather | solution.py:60
  434.4 58.8 %reduce-scatter.17.cloned.1.call-start = ((), (), s32[]{:S(2)}) async-start(), calls=%async_computation.23 | async-start | bytes 1966080 | tf_op jit(solution)/shard_map/reduce_scatter | solution.py:64
  465.0 143.2 %all-gather.28.cloned.1.call-start = ((), (), s32[]{:S(2)}) async-start(), calls=%async_computation.24 | async-start | bytes 2359296 | tf_op jit(solution)/shard_map/all_gather | solution.py:267
  465.7 142.4 %all-gather.30.cloned.1.call-start = ((), (), s32[]{:S(2)}) async-start(), calls=%async_computation.25 | async-start | bytes 2359296 | tf_op jit(solution)/shard_map/all_gather | solution.py:268
  527.2 135.9 %reduce-scatter.21.cloned.1.call-start = ((), (), s32[]{:S(2)}) async-start(), calls=%async_computation.27 | async-start | bytes 2621440 | tf_op jit(solution)/shard_map/reduce_scatter | solution.py:359
  530.6 168.1 %reduce-scatter.19.cloned.1.call-start = ((), (), s32[]{:S(2)}) async-start(), calls=%async_computation.26 | async-start | bytes 7864320 | tf_op jit(solution)/shard_map/reduce_scatter | solution.py:356
  643.2 78.5 %reduce-scatter.25.cloned.1.call-start = ((), (), s32[]{:S(2)}) async-start(), calls=%async_computation.29 | async-start | bytes 327680
  647.1 96.3 %reduce-scatter.23.cloned.1.call-start = ((), (), s32[]{:S(2)}) async-start(), calls=%async_computation.28 | async-start | bytes 20480 | tf_op jit(solution)/shard_map/reduce_scatter | solution.py:362
  648.2 201.5 %all-reduce.5.cloned.1.call-start = ((), (), s32[]{:S(2)}) async-start(), calls=%async_computation.30 | async-start | bytes 4194304 | tf_op jit(solution)/shard_map/psum | solution.py:371
  (69 other events, 1443.4 us)
Sparse Core Ops, SparseCore 0:
  9.5 49.1 all-gather.11
  63.7 48.9 all-gather.13
  115.5 47.6 all-gather.15
  164.5 21.0 all-gather.17
  209.0 17.7 all-gather.19
  241.7 27.9 reduce-scatter.10
  272.2 19.6 all-gather.21
  307.9 27.9 reduce-scatter.12
  373.8 17.3 all-gather.23
  402.1 28.0 reduce-scatter.14
  434.5 19.6 all-gather.25
  465.1 28.0 reduce-scatter.16
  495.3 53.8 all-gather.27
  551.1 47.9 all-gather.29
  602.1 29.7 reduce-scatter.20
  643.3 55.3 reduce-scatter.18
  701.6 20.0 reduce-scatter.24
  723.9 19.4 reduce-scatter.22
  747.1 102.5 all-reduce.4
where the time goes:
time: 871 us; the launch traced here: 861 us
  waiting for transfers between devices  484 us (56%)
  blocking collectives  138 us (16%)
  matrix products  126 us (14%)
  other arithmetic  49.5 us (6%)
  local copies, waits for them, and re-layouts  33.4 us (4%)
  between operations  16.6 us (2%)
  starting transfers between devices  12.7 us (1%)
    reduce_scatter x4, waiting for transfers between devices, sum_rows(): lax.psum_scatter(term(jnp.int32(0), amount * lax.axis_size('dp')).astype(...  112 us
    psum x1, waiting for transfers between devices, on_device(): lax.psum(qkv_share.astype(jnp.bfloat16), 'expert').astype(jnp.float32)  81.4 us
    all_gather x4, waiting for transfers between devices, spread_rows(): return lax.all_gather(rows_low, 'dp', axis=0, tiled=True)  74.6 us
    all_gather x1, waiting for transfers between devices, on_device(): value_piece = lax.all_gather(values, 'expert', axis=0, tiled=True)  50.4 us
    all_gather x1, waiting for transfers between devices, fetch_dense(): lax.all_gather(qkv_weight, 'dp', axis=0, tiled=True)  41.8 us
    all_gather x1, waiting for transfers between devices, on_device(): key_piece = lax.all_gather(keyset, 'expert', axis=0, tiled=True)  40.4 us
    reduce_scatter x1, waiting for transfers between devices, on_device(): lax.psum_scatter(grad_qkv.astype(jnp.bfloat16), 'dp', scatter_dimension=0...  35.6 us
    all_gather x1, blocking collectives, on_device(): lax.all_gather(delta_rows.astype(jnp.bfloat16), 'expert', axis=0, tiled=T...  26.3 us
  transfers between devices with their start and end apart: 21, of which 18 were waited for; matrix products, arithmetic and copies ran while one was open for 15% of the time, Pallas kernels for 0%

commit v1 on v0

--- a/solution.py
+++ b/solution.py
@@ -3,6 +3,8 @@
 import jax
 import jax.numpy as jnp
 from jax import lax
+from jax.experimental import pallas as pl
+from jax.experimental.pallas import tpu as pltpu
 from jax.sharding import PartitionSpec as P
 
 HEADS = 16
@@ -74,6 +76,523 @@
         jnp.zeros((experts * capacity, rows_low.shape[1]), rows_low.dtype).at[target].set(rows_low)
     )
     return buffer_rows.reshape(experts, capacity, rows_low.shape[1])
+
+
+BF = jnp.bfloat16
+F32 = jnp.float32
+NT = (((1,), (1,)), ((), ()))
+TILE = 256
+
+
+def mean_last(v):
+    return jnp.mean(v, axis=-1, keepdims=True)
+
+
+def dp_peers():
+    me = lax.axis_index("dp")
+    sibling = me + 1 - 2 * lax.rem(me, 2)
+    across = lax.rem(me + 2, 4)
+    return sibling, across
+
+
+def greet(axis_targets):
+    barrier = pltpu.get_barrier_semaphore()
+    for target in axis_targets:
+        pl.semaphore_signal(barrier, inc=1, device_id=target, device_id_type=pl.DeviceIdType.MESH)
+    pl.semaphore_wait(barrier, len(axis_targets))
+
+
+def expert_kernel(
+    z0_ref, dbr_ref, gain_ref, w1_hbm, w2_hbm,
+    branch_ref, gstate_ref, ggain_ref, n_out, h_out, df_out, du_out,
+    w1, w2, x, hid, gpr, unit_s, inv_s, state, total, own, far, f1, f3, ssum, rf1, rf3, rss,
+    send_sem, recv_sem, copy_sem,
+):
+    half = z0_ref.shape[0] // 2
+    pair_rows = 2 * half
+    width = z0_ref.shape[1]
+    tiles = width // TILE
+    sibling, across = dp_peers()
+
+    loads = []
+    for i, (src, dst) in enumerate(
+        [(w1_hbm.at[0, 0], w1.at[0]), (w2_hbm.at[0, 0], w2.at[0]),
+         (w1_hbm.at[0, 1], w1.at[1]), (w2_hbm.at[0, 1], w2.at[1])]
+    ):
+        cp = pltpu.make_async_copy(src, dst, copy_sem.at[i])
+        cp.start()
+        loads.append(cp)
+    greet([{"dp": sibling}, {"dp": across}])
+
+    def rows_of(h, r):
+        return pl.ds((h * 4 + r) * half, half)
+
+    def remote(src, dst, kind, p, h, peer):
+        i = (p * 2 + h) * 6 + kind
+        return pltpu.make_async_remote_copy(
+            src_ref=src, dst_ref=dst, send_sem=send_sem.at[i], recv_sem=recv_sem.at[i],
+            device_id={"dp": peer}, device_id_type=pl.DeviceIdType.MESH,
+        )
+
+    def copy_of(kind, p, h):
+        q = p * 2 + h
+        if kind == 0:
+            return remote(x.at[p, rows_of(h, 0)], x.at[p, rows_of(h, 1)], 0, p, h, sibling)
+        if kind == 1:
+            return remote(x.at[p, rows_of(h, 0)], x.at[p, rows_of(h, 2)], 1, p, h, across)
+        if kind == 2:
+            return remote(x.at[p, rows_of(h, 2)], x.at[p, rows_of(h, 3)], 2, p, h, sibling)
+        if kind == 3:
+            return remote(f1.at[q], rf1.at[q], 3, p, h, sibling)
+        if kind == 4:
+            return remote(f3.at[q], rf3.at[q], 4, p, h, sibling)
+        return remote(ssum.at[q], rss.at[q], 5, p, h, across)
+
+    layer_of = (0, 1, 1, 0)
+
+    def start_rows(p, h):
+        k = layer_of[p]
+        rs = pl.ds(h * half, half)
+        if p < 2:
+            z = state[rs, :]
+            center = z - mean_last(z)
+            inverse = lax.rsqrt(mean_last(center * center) + EPS)
+            unit = center * inverse
+            unit_s[k, rs, :] = unit
+            inv_s[k, rs, :] = jnp.broadcast_to(inverse, (half, 128))
+            x[p, rows_of(h, 0), :] = (unit * gain_ref[pl.ds(k, 1), :]).astype(BF)
+        else:
+            x[p, rows_of(h, 0), :] = (dbr_ref[rs, :].astype(F32) + state[rs, :]).astype(BF)
+        copy_of(1, p, h).start()
+        copy_of(0, p, h).start()
+
+    def compute(p, h, pair):
+        k = layer_of[p]
+        base = pl.ds((h * 2 + pair) * pair_rows, pair_rows)
+        first, second = (w1, w2) if p < 2 else (w2, w1)
+        q = p * 2 + h
+
+        def up(t, c):
+            cols = pl.ds(pl.multiple_of(t * TILE, TILE), TILE)
+            pre = lax.dot_general(x[p, base, :], first[k, cols, :], NT, preferred_element_type=F32)
+            if p < 2:
+                cdf = 0.5 * (1.0 + lax.erf(pre * (0.5 ** 0.5)))
+                pdf = jnp.exp(-0.5 * pre * pre) * 0.3989422804014327
+                hid[k, base, cols] = (pre * cdf).astype(BF)
+                gpr[k, base, cols] = cdf + pre * pdf
+            else:
+                hid[2 + k, base, cols] = (pre * gpr[k, base, cols]).astype(BF)
+            return c
+
+        lax.fori_loop(0, tiles, up, 0)
+        slot = k if p < 2 else 2 + k
+
+        def down(t, c):
+            cols = pl.ds(pl.multiple_of(t * TILE, TILE), TILE)
+            res = jnp.dot(hid[slot, base, :], second[k, :, cols], preferred_element_type=F32)
+            if pair == 0:
+                own[h, :, cols] = res[:half]
+                f1[q, :, cols] = res[half:].astype(BF)
+            else:
+                far[:, cols] = res[:half]
+                f3[q, :, cols] = res[half:].astype(BF)
+            return c
+
+        lax.fori_loop(0, tiles, down, 0)
+        if pair == 0:
+            copy_of(3, p, h).start()
+        else:
+            copy_of(4, p, h).start()
+            copy_of(4, p, h).wait_recv()
+            ssum[q] = (far[...] + rf3[q].astype(F32)).astype(BF)
+            copy_of(5, p, h).start()
+
+    def finish(p, h):
+        k = layer_of[p]
+        q = p * 2 + h
+        rs = pl.ds(h * half, half)
+        copy_of(3, p, h).wait_recv()
+        copy_of(5, p, h).wait_recv()
+        got = own[h] + rf1[q].astype(F32) + rss[q].astype(F32)
+        if p == 0:
+            state[rs, :] = state[rs, :] + got
+            total[rs, :] = got
+        elif p == 1:
+            branch_ref[rs, :] = (total[rs, :] + got).astype(BF)
+            state[rs, :] = jnp.zeros((half, width), F32)
+        else:
+            unit = unit_s[k, rs, :]
+            part = jnp.sum(got * unit, axis=0, keepdims=True)
+            if h == 0:
+                ggain_ref[pl.ds(k, 1), :] = part
+            else:
+                ggain_ref[pl.ds(k, 1), :] = ggain_ref[pl.ds(k, 1), :] + part
+            a = got * gain_ref[pl.ds(k, 1), :]
+            back = inv_s[k, rs, :][:, :1] * (a - mean_last(a) - unit * mean_last(a * unit))
+            if p == 2:
+                state[rs, :] = state[rs, :] + back
+            else:
+                gstate_ref[rs, :] = (state[rs, :] + back).astype(BF)
+
+    def relay(p, h):
+        copy_of(1, p, h).wait_recv()
+        copy_of(2, p, h).start()
+
+    stores = []
+
+    def store(i, src, dst):
+        cp = pltpu.make_async_copy(src, dst, copy_sem.at[4 + i])
+        cp.start()
+        stores.append(cp)
+
+    state[...] = z0_ref[...].astype(F32)
+    start_rows(0, 0)
+    start_rows(0, 1)
+    loads[0].wait()
+    loads[1].wait()
+    for p in range(4):
+        if p == 0:
+            copy_of(0, p, 0).wait_recv()
+            compute(p, 0, 0)
+        relay(p, 0)
+        copy_of(2, p, 0).wait_recv()
+        compute(p, 0, 1)
+        copy_of(0, p, 1).wait_recv()
+        compute(p, 1, 0)
+        relay(p, 1)
+        copy_of(2, p, 1).wait_recv()
+        compute(p, 1, 1)
+        finish(p, 0)
+        if p == 0:
+            loads[2].wait()
+            loads[3].wait()
+        if p < 3:
+            start_rows(p + 1, 0)
+            copy_of(0, p + 1, 0).wait_recv()
+            compute(p + 1, 0, 0)
+        finish(p, 1)
+        if p < 3:
+            start_rows(p + 1, 1)
+        k = layer_of[p]
+        if p < 2:
+            store(p * 2, x.at[p], n_out.at[k])
+            store(p * 2 + 1, hid.at[k], h_out.at[k])
+        else:
+            store(p * 2, x.at[p], df_out.at[k])
+            store(p * 2 + 1, hid.at[2 + k], du_out.at[k])
+    for p in range(4):
+        for h in range(2):
+            for kind in range(6):
+                copy_of(kind, p, h).wait_send()
+    for cp in stores:
+        cp.wait()
+
+
+def expert_block(z0, dbr, gains, expert_in, expert_out):
+    rows, width = z0.shape
+    half = rows // 2
+    hidden = expert_in.shape[2]
+    everything = 4 * rows
+    any_spec = pl.BlockSpec(memory_space=pl.ANY)
+    vmem_spec = pl.BlockSpec(memory_space=pltpu.VMEM)
+    big = jax.ShapeDtypeStruct((2, everything, width), BF)
+    V = pltpu.VMEM
+    return pl.pallas_call(
+        expert_kernel,
+        out_shape=(
+            jax.ShapeDtypeStruct((rows, width), BF),
+            jax.ShapeDtypeStruct((rows, width), BF),
+            jax.ShapeDtypeStruct((2, width), F32),
+            big, big, big, big,
+        ),
+        in_specs=[vmem_spec] * 3 + [any_spec] * 2,
+        out_specs=(vmem_spec, vmem_spec, vmem_spec, any_spec, any_spec, any_spec, any_spec),
+        scratch_shapes=[
+            V((2, hidden, width), BF), V((2, hidden, width), BF),
+            V((4, everything, width), BF), V((4, everything, hidden), BF), V((2, everything, hidden), F32),
+            V((2, rows, width), F32), V((2, rows, 128), F32), V((rows, width), F32), V((rows, width), F32),
+            V((2, half, width), F32), V((half, width), F32),
+        ]
+        + [V((8, half, width), BF)] * 6
+        + [pltpu.SemaphoreType.DMA((48,)), pltpu.SemaphoreType.DMA((48,)), pltpu.SemaphoreType.DMA((12,))],
+        compiler_params=pltpu.CompilerParams(
+            collective_id=1, has_side_effects=True, vmem_limit_bytes=58 * 1024 * 1024
+        ),
+        cost_estimate=pl.CostEstimate(
+            flops=16 * everything * hidden * width, bytes_accessed=24 * 1024 * 1024, transcendentals=0
+        ),
+        name="expert_block",
+    )(z0, dbr, gains, expert_in, expert_out)
+
+
+def on_device_split(
+    tokens,
+    norm_gain,
+    qkv_weight,
+    out_weight,
+    centroids,
+    expert_gain,
+    expert_in,
+    expert_out,
+    routes,
+    cotangent,
+):
+    model_width = tokens.shape[1]
+    local_rows = tokens.shape[0]
+    experts = lax.axis_size("expert")
+    capacity = max(2, 3 * local_rows // (2 * experts))
+    slot_total = experts * capacity
+    first_pos = lax.axis_index("expert") * local_rows
+    scale = HEAD ** (-0.5)
+    gain_full, qkv_full, out_full, centroid_full, expert_gain_full = fetch_dense(
+        norm_gain, qkv_weight, out_weight, centroids, expert_gain
+    )
+    inputs = tokens.astype(jnp.float32)
+    unit_attn, inverse_attn, normed_attn = normalize(inputs, gain_full.astype(jnp.float32))
+    normed_low = normed_attn.astype(jnp.bfloat16)
+    projected = jnp.dot(normed_low, qkv_full, preferred_element_type=jnp.float32).astype(
+        jnp.bfloat16
+    )
+    queries = projected[:, :model_width]
+    keyset = projected[:, model_width : 2 * model_width]
+    values = projected[:, 2 * model_width :]
+    query_heads = split_heads(queries)
+    key_heads = split_heads(keyset)
+    value_heads = split_heads(values)
+    query_block = (first_pos + jnp.arange(local_rows, dtype=jnp.int32)) // BLOCK
+    last_block = (first_pos + local_rows - 1) // BLOCK
+    start_state = (
+        jnp.zeros((local_rows, HEADS, HEAD), jnp.float32),
+        jnp.full((HEADS, local_rows), NEGATIVE, jnp.float32),
+        jnp.zeros((HEADS, local_rows), jnp.float32),
+    )
+    key_piece = lax.all_gather(keyset, "expert", axis=0, tiled=True)
+    value_piece = lax.all_gather(values, "expert", axis=0, tiled=True)
+    amount = key_piece.shape[0]
+
+    def update(current):
+        accumulated, highest, totals = current
+        scores = (
+            jnp.einsum(
+                "qhd,khd->hqk",
+                query_heads,
+                split_heads(key_piece),
+                preferred_element_type=jnp.float32,
+            )
+            * scale
+        )
+        piece_block = jnp.arange(amount, dtype=jnp.int32) // BLOCK
+        visible = (piece_block[None, :] <= query_block[:, None])[None]
+        scores = jnp.where(visible, scores, NEGATIVE)
+        new_high = jnp.maximum(highest, jnp.max(scores, axis=-1))
+        factor = jnp.exp(highest - new_high)
+        weights = jnp.where(visible, jnp.exp(scores - new_high[:, :, None]), 0.0)
+        totals = jnp.sum(weights, axis=-1)
+        accumulated = accumulated * factor.T[:, :, None] + jnp.einsum(
+            "hqk,khd->qhd",
+            weights.astype(jnp.bfloat16),
+            split_heads(value_piece),
+            preferred_element_type=jnp.float32,
+        )
+        return (accumulated, new_high, totals)
+
+    accumulated, highest, totals = lax.cond(
+        jnp.int32(0) // BLOCK <= last_block, update, keep_state, start_state
+    )
+    mixed_heads = accumulated / totals.T[:, :, None]
+    log_total = (highest + jnp.log(totals)).T
+    mixed_low = mixed_heads.reshape(local_rows, model_width).astype(jnp.bfloat16)
+    residual = inputs + jnp.dot(mixed_low, out_full, preferred_element_type=jnp.float32)
+    route_ids = routes[:, 0]
+    chosen = route_ids[:, None] == jnp.arange(experts, dtype=jnp.int32)[None, :]
+    centroid_rows = jnp.dot(
+        chosen.astype(jnp.bfloat16), centroid_full, preferred_element_type=jnp.float32
+    )
+    gate_value = jax.nn.sigmoid(jnp.sum(residual * centroid_rows, axis=-1))
+    chosen_int = chosen.astype(jnp.int32)
+    slot_index = jnp.sum((jnp.cumsum(chosen_int, axis=0) - 1) * chosen_int, axis=-1)
+    target = route_ids * capacity + slot_index
+    arrived = lax.all_to_all(
+        send_slots(residual.astype(jnp.bfloat16), target, experts, capacity),
+        "expert",
+        split_axis=0,
+        concat_axis=0,
+        tiled=True,
+    )
+    gains_here = expert_gain_full[0].astype(jnp.float32)
+    grad_out = cotangent.astype(jnp.float32)
+    grad_branch = (gate_value[:, None] * grad_out).astype(jnp.bfloat16)
+    branch_grads = lax.all_to_all(
+        send_slots(grad_branch, target, experts, capacity),
+        "expert",
+        split_axis=0,
+        concat_axis=0,
+        tiled=True,
+    )
+    branch_low, state_low, expert_gain_grad, n_rows, h_rows, df_rows, du_rows = expert_block(
+        arrived.reshape(slot_total, model_width),
+        branch_grads.reshape(slot_total, model_width),
+        gains_here,
+        expert_in,
+        expert_out,
+    )
+    expert_gain_grad = expert_gain_grad[None]
+    grad_expert_out = jnp.einsum("krf,krd->kfd", h_rows, df_rows, preferred_element_type=jnp.float32)[None]
+    grad_expert_in = jnp.einsum("krf,krd->kfd", du_rows, n_rows, preferred_element_type=jnp.float32)[None]
+    returned = lax.all_to_all(
+        branch_low.reshape(experts, capacity, model_width),
+        "expert",
+        split_axis=0,
+        concat_axis=0,
+        tiled=True,
+    )
+    branch_tok = returned.reshape(slot_total, model_width)[target].astype(jnp.float32)
+    block_out = (residual + gate_value[:, None] * branch_tok).astype(jnp.bfloat16)
+    grad_logit = jnp.sum(grad_out * branch_tok, axis=-1) * gate_value * (1.0 - gate_value)
+    grad_centroid = jnp.dot(
+        chosen.astype(jnp.float32).T, grad_logit[:, None] * residual, precision=HIGH
+    )
+    grad_resid = grad_out + grad_logit[:, None] * centroid_rows
+    came_back = lax.all_to_all(
+        state_low.reshape(experts, capacity, model_width),
+        "expert",
+        split_axis=0,
+        concat_axis=0,
+        tiled=True,
+    )
+    grad_resid = grad_resid + came_back.reshape(slot_total, model_width)[target].astype(jnp.float32)
+    grad_attended = grad_resid.astype(jnp.bfloat16)
+    grad_out_weight = jnp.einsum(
+        "rd,re->de", mixed_low, grad_attended, preferred_element_type=jnp.float32
+    )
+    grad_mixed = jnp.einsum(
+        "re,de->rd", grad_attended, out_full, preferred_element_type=jnp.float32
+    ).astype(jnp.bfloat16)
+    grad_heads = split_heads(grad_mixed)
+    delta_rows = jnp.sum(grad_heads.astype(jnp.float32) * mixed_heads, axis=-1)
+    zero_heads = jnp.zeros((local_rows, HEADS, HEAD), jnp.float32)
+    running = (zero_heads, zero_heads, zero_heads)
+    offset = jnp.int32(0)
+    fold_key_piece = lax.all_gather(keyset, "expert", axis=0, tiled=True)
+    fold_value_piece = lax.all_gather(values, "expert", axis=0, tiled=True)
+    query_piece = lax.all_gather(queries, "expert", axis=0, tiled=True)
+    grad_piece = lax.all_gather(grad_mixed, "expert", axis=0, tiled=True)
+    log_piece = lax.all_gather(log_total.astype(jnp.bfloat16), "expert", axis=0, tiled=True).astype(
+        jnp.float32
+    )
+    delta_piece = lax.all_gather(
+        delta_rows.astype(jnp.bfloat16), "expert", axis=0, tiled=True
+    ).astype(jnp.float32)
+    fold_amount = fold_key_piece.shape[0]
+    piece_block = jnp.arange(fold_amount, dtype=jnp.int32) // BLOCK
+
+    def to_queries(current):
+        grad_query, grad_key, grad_value = current
+        piece_keys = split_heads(fold_key_piece)
+        scores = (
+            jnp.einsum("qhd,khd->hqk", query_heads, piece_keys, preferred_element_type=jnp.float32)
+            * scale
+        )
+        visible = (piece_block[None, :] <= query_block[:, None])[None]
+        weights = jnp.where(visible, jnp.exp(scores - log_total.T[:, :, None]), 0.0)
+        grad_weights = jnp.einsum(
+            "qhd,khd->hqk",
+            grad_heads,
+            split_heads(fold_value_piece),
+            preferred_element_type=jnp.float32,
+        )
+        grad_scores = (weights * (grad_weights - delta_rows.T[:, :, None])).astype(jnp.bfloat16)
+        grad_query = (
+            jnp.einsum("hqk,khd->qhd", grad_scores, piece_keys, preferred_element_type=jnp.float32)
+            * scale
+        )
+        return (grad_query, grad_key, grad_value)
+
+    def to_keys(current):
+        grad_query, grad_key, grad_value = current
+        piece_queries = split_heads(query_piece)
+        piece_grads = split_heads(grad_piece)
+        scores = (
+            jnp.einsum("qhd,khd->hqk", piece_queries, key_heads, preferred_element_type=jnp.float32)
+            * scale
+        )
+        visible = (query_block[None, :] <= piece_block[:, None])[None]
+        weights = jnp.where(visible, jnp.exp(scores - log_piece.T[:, :, None]), 0.0)
+        grad_weights = jnp.einsum(
+            "qhd,khd->hqk", piece_grads, value_heads, preferred_element_type=jnp.float32
+        )
+        grad_scores = (weights * (grad_weights - delta_piece.T[:, :, None])).astype(jnp.bfloat16)
+        grad_key = (
+            grad_key
+            + jnp.einsum(
+                "hqk,qhd->khd", grad_scores, piece_queries, preferred_element_type=jnp.float32
+            )
+            * scale
+        )
+        grad_value = grad_value + jnp.einsum(
+            "hqk,qhd->khd",
+            weights.astype(jnp.bfloat16),
+            piece_grads,
+            preferred_element_type=jnp.float32,
+        )
+        return (grad_query, grad_key, grad_value)
+
+    running = lax.cond(offset // BLOCK <= last_block, to_queries, keep_state, running)
+    grad_query, grad_key, grad_value = lax.cond(
+        query_block[0] <= (offset + fold_amount - 1) // BLOCK, to_keys, keep_state, running
+    )
+    grad_qkv_rows = jnp.concatenate(
+        [
+            grad_query.reshape(local_rows, model_width),
+            grad_key.reshape(local_rows, model_width),
+            grad_value.reshape(local_rows, model_width),
+        ],
+        axis=1,
+    ).astype(jnp.bfloat16)
+    grad_qkv = jnp.einsum(
+        "rd,re->de", normed_low, grad_qkv_rows, preferred_element_type=jnp.float32
+    )
+    grad_normed_attn = jnp.einsum(
+        "re,de->rd", grad_qkv_rows, qkv_full, preferred_element_type=jnp.float32
+    )
+    grad_input_attn, attn_gain_grad = norm_backward(
+        grad_normed_attn, unit_attn, inverse_attn, gain_full.astype(jnp.float32)
+    )
+    grad_tokens = grad_resid + grad_input_attn
+    gain_share, qkv_share, out_share, centroid_share, expert_gain_share = (
+        lax.psum_scatter(
+            attn_gain_grad.astype(jnp.bfloat16), "dp", scatter_dimension=0, tiled=True
+        ).astype(jnp.float32),
+        lax.psum_scatter(
+            grad_qkv.astype(jnp.bfloat16), "dp", scatter_dimension=0, tiled=True
+        ).astype(jnp.float32),
+        lax.psum_scatter(
+            grad_out_weight.astype(jnp.bfloat16), "dp", scatter_dimension=0, tiled=True
+        ).astype(jnp.float32),
+        lax.psum_scatter(
+            grad_centroid.astype(jnp.bfloat16), "dp", scatter_dimension=1, tiled=True
+        ).astype(jnp.float32),
+        lax.psum_scatter(
+            expert_gain_grad.astype(jnp.bfloat16), "dp", scatter_dimension=2, tiled=True
+        ).astype(jnp.float32),
+    )
+    gain_total, qkv_total, out_total, centroid_total = (
+        lax.psum(gain_share.astype(jnp.bfloat16), "expert").astype(jnp.float32),
+        lax.psum(qkv_share.astype(jnp.bfloat16), "expert").astype(jnp.float32),
+        lax.psum(out_share.astype(jnp.bfloat16), "expert").astype(jnp.float32),
+        lax.psum(centroid_share.astype(jnp.bfloat16), "expert").astype(jnp.float32),
+    )
+    return (
+        block_out,
+        grad_tokens,
+        gain_total,
+        qkv_total,
+        out_total,
+        centroid_total,
+        expert_gain_share,
+        grad_expert_in,
+        grad_expert_out,
+    )
 
 
 def on_device(
@@ -411,6 +930,7 @@
         P("expert", None, "dp", None),
         P("expert", None, "dp", None),
     )
+    split = mesh.shape["dp"] == 4 and mesh.shape["expert"] == 8
     return jax.shard_map(
-        on_device, mesh=mesh, in_specs=in_specs, out_specs=out_specs, check_vma=False
-    )
+        on_device_split if split else on_device, mesh=mesh, in_specs=in_specs, out_specs=out_specs, check_vma=False
+    )

time: 871 us -> 721 us (0.83)
  waiting for transfers between devices: 484 us -> 311 us
  Pallas kernels: 0 us -> 102 us
  matrix products: 126 us -> 83.7 us
  blocking collectives: 138 us -> 112 us
  other arithmetic: 49.5 us -> 28.5 us
  loops' own time: 0.34 us -> 12.2 us
    pallas_call x0 -> x1, Pallas kernels: none -> 102 us  [expert_block(): pl.pallas_call(expert_kernel, out_shape=(jax.ShapeDtypeStruct((rows, widt...]
    reduce_scatter x7 -> x3, waiting for transfers between devices: 157 us -> 60.2 us  [the longest x1 51.1 us: on_device_split(): lax.psum_scatter(grad_qkv.astype(jnp.bfloat16), 'dp', scatter_dimension=0...]
    all_gather x8 -> x4, waiting for transfers between devices: 165 us -> 90.4 us  [the longest x1 49.8 us: on_device_split(): key_piece = lax.all_gather(keyset, 'expert', axis=0, tiled=True)]
    dot_general x20 -> x10, matrix products: 84.8 us -> 40.3 us  [the longest x1 9.85 us: on_device_split(): jnp.einsum('krf,krd->kfd', du_rows, n_rows, preferred_element_type=jnp.fl...]
    all_to_all x2 -> x1, blocking collectives: 40.9 us -> 14.5 us  [on_device_split(): lax.all_to_all(state_low.reshape(experts, capacity, model_width), 'expert...]
    another operation x3, loops' own time: 0.34 us -> 12.2 us  [the longest x1 12.1 us: on_device_split(): lax.cond(offset // BLOCK <= last_block, to_queries, keep_state, running)]
    unnamed x20 -> x12, waiting for transfers between devices: 18.1 us -> 8.88 us
    broadcast_in_dim x2 -> x0, other arithmetic: 8.96 us -> none  [the longest x1 4.71 us: on_device(): grad_expert_in = jnp.stack(first_grads)[None]]
  transfers between devices with their start and end apart: 21 -> 14, of which waited for: 18 -> 11; matrix products, arithmetic and copies ran while one was open for 15% -> 18% of each run, Pallas kernels for 0% -> 14%
where the time goes in v1:
time: 721 us; the launch traced here: 712 us
  waiting for transfers between devices  311 us (43%)
  blocking collectives  112 us (16%)
  Pallas kernels  102 us (14%)
  matrix products  83.7 us (12%)
  local copies, waits for them, and re-layouts  33.3 us (5%)
  other arithmetic  28.5 us (4%)
  between operations  15.9 us (2%)
  starting transfers between devices  13.2 us (2%)
  loops' own time  12.2 us (2%)
    pallas_call x1, Pallas kernels, expert_block(): pl.pallas_call(expert_kernel, out_shape=(jax.ShapeDtypeStruct((rows, widt...  102 us
    psum x1, waiting for transfers between devices, on_device_split(): lax.psum(qkv_share.astype(jnp.bfloat16), 'expert').astype(jnp.float32)  81.4 us
    reduce_scatter x1, waiting for transfers between devices, on_device_split(): lax.psum_scatter(grad_qkv.astype(jnp.bfloat16), 'dp', scatter_dimension=0...  51.1 us
    all_gather x1, waiting for transfers between devices, on_device_split(): key_piece = lax.all_gather(keyset, 'expert', axis=0, tiled=True)  49.8 us
    all_gather x1, waiting for transfers between devices, fetch_dense(): lax.all_gather(qkv_weight, 'dp', axis=0, tiled=True)  41.8 us
    all_gather x1, waiting for transfers between devices, on_device_split(): value_piece = lax.all_gather(values, 'expert', axis=0, tiled=True)  40.6 us
    all_gather x1, blocking collectives, on_device_split(): lax.all_gather(delta_rows.astype(jnp.bfloat16), 'expert', axis=0, tiled=T...  26.3 us
    all_gather x1, blocking collectives, on_device_split(): lax.all_gather(log_total.astype(jnp.bfloat16), 'expert', axis=0, tiled=True)  26.2 us
  transfers between devices with their start and end apart: 14, of which 11 were waited for; matrix products, arithmetic and copies ran while one was open for 18% of the time, Pallas kernels for 14%

profile of v1, /device:TPU:0, one launch (start us, length us, event | category | flops | bytes accessed | tf_op | source)
XLA Modules:
  0.0 711.8 jit_solution(2110530475856343660)
XLA Ops:
  8.6 6.0 all-gather
  16.9 41.8 %all-gather.8.cloned.1.call-done = bf16[1024,3072]{1,0:T(8,128)(2,1)} async-done(((bf16[256,3072]{1,0:T(8,128)(2,1)}), bf16[1024,3072]{1,0:T(8,128)(2,1)}) %all-gather.8.cloned.1.call-update) | async-done | bytes 6291472 | tf_op jit(solution)/shard_map/all_gather | solution.py:54
  72.3 40.6 %all-gather.12.cloned.1.call-done = bf16[1024,1024]{1,0:T(8,128)(2,1)} async-done(((bf16[128,1024]{1,0:T(8,128)(2,1)}), bf16[1024,1024]{1,0:T(8,128)(2,1)}) %all-gather.12.cloned.1.call-update) | async-done | bytes 2097168 | tf_op jit(solution)/shard_map/all_gather | solution.py:370
  112.8 49.8 %all-gather.10.cloned.1.call-done = bf16[1024,1024]{1,0:T(8,128)(2,1)} async-done(((bf16[128,1024]{1,0:T(8,128)(2,1)}), bf16[1024,1024]{1,0:T(8,128)(2,1)}) %all-gather.10.cloned.1.call-update) | async-done | bytes 2097168 | tf_op jit(solution)/shard_map/all_gather | solution.py:369
  162.6 19.1 %conditional.3 = (f32[128,16,64]{0,2,1:T(8,128)S(1)}, f32[16,128]{1,0:T(8,128)}, f32[16,128]{1,0:T(8,128)}, f32[16,128]{1,0:T(8,128)S(1)}) conditional(s32[]{:T(128)} %convert_element_type.136, () %tuple.38, (s32[128]{0:T(128)}, bf16[1024,1024]{1,0:T(8,128)(2,1)}, bf16[128,16,64]{0,2,1:T(8,128)(2,1)}, bf16[1024,1024]{1,0:T(8,128)(2,1)}) %tuple.99), branch_computations={%region_2.3_spmd, %region_3.6_spmd} | conditional | flops 564406272 | bytes 56975988 | solution.py:399
  196.7 10.2 %all-to-all-done.1 = bf16[8,24,1024]{2,1,0:T(8,128)(2,1)S(1)} async-done(((bf16[8,24,1024]{2,1,0:T(8,128)(2,1)}), bf16[8,24,1024]{2,1,0:T(8,128)(2,1)S(1)}, u32[]{:S(2)}, u32[]{:S(2)}) %all-to-all-start.1) | async-done | bytes 393248 | tf_op jit(solution)/shard_map/all_to_all | solution.py:425
  216.5 5.9 all-to-all-done
  223.1 101.9 %expert_block.1 = (bf16[192,1024]{1,0:T(8,128)(2,1)}, bf16[192,1024]{1,0:T(8,128)(2,1)}, f32[2,1024]{1,0:T(2,128)}, bf16[2,768,1024]{2,1,0:T(8,128)(2,1)}, bf16[...) custom-call(bf16[192,1024]{1,0:T(8,128)(2,1)} %bitcast.118, ...), custom_call_target="tpu_custom_call" | custom-call | flops 12884901888 | bytes 25165824 | tf_op jit(solution)/shard_map/expert_block/pallas_call | solution.py:300
  325.0 14.5 %all_to_all.20 = bf16[8,24,1024]{2,1,0:T(8,128)(2,1)S(1)} all-to-all(bf16[8,24,1024]{2,1,0:T(8,128)(2,1)} %bitcast.120), channel_id=1, replica_groups=mesh['dp'=4,'expert'=8] {'expert'}, dimensions={0} | all-to-all | bytes 786432 | tf_op jit(solution)/shard_map/all_to_all | solution.py:456
  343.9 9.9 %all-to-all-done.2 = bf16[8,24,1024]{2,1,0:T(8,128)(2,1)S(1)} async-done(((bf16[8,24,1024]{2,1,0:T(8,128)(2,1)}), bf16[8,24,1024]{2,1,0:T(8,128)(2,1)S(1)}, u32[]{:S(2)}, u32[]{:S(2)}) %all-to-all-start.2) | async-done | bytes 393248 | tf_op jit(solution)/shard_map/all_to_all | solution.py:442
  364.1 26.2 %all_gather.43 = bf16[1024,16]{0,1:T(8,128)(2,1)S(1)} all-gather(bf16[128,16]{0,1:T(8,128)(2,1)S(1)} %get-tuple-element.175), channel_id=1, replica_groups=mesh['dp'=4,'expert'=8] {'expert'}, dimensions={0}, use_global_device_ids=true | all-gather | bytes 36864 | tf_op jit(solution)/shard_map/all_gather | solution.py:480
  393.9 26.3 %all_gather.45 = bf16[1024,16]{0,1:T(8,128)(2,1)S(1)} all-gather(bf16[128,16]{0,1:T(8,128)(2,1)S(1)} %convert_element_type.159), channel_id=1, replica_groups=mesh['dp'=4,'expert'=8] {'expert'}, dimensions={0}, use_global_device_ids=true | all-gather | bytes 36864 | tf_op jit(solution)/shard_map/all_gather | solution.py:483
  420.8 32.6 %conditional.4 = (bf16[128,1024]{0,1:T(8,128)(2,1)}) conditional(s32[]{:T(128)} %convert_element_type.136, () %tuple.40, (s32[1024]{0:T(1024)S(1)}, s32[128]{0:T(128)}, bf16[1024,1024]{1,0:T(8,128)(2,1)}, bf16[128,16,64]{0,2,1:T(8,128)(2,1)}, f32[16,128]{1,0:T(8,128)}, /*index=5*/bf16[1024,1024]{1,0:T(8,128)(2,1)S(1)}, ...), branch_computations={%region_13.14_spmd, %region_14.15_spmd} | conditional | flops 818282496 | bytes 32526856 | solution.py:540
  444.8 8.7 %fusion.22 = bf16[16,128,64]{1,2,0:T(8,128)(2,1)} fusion(bf16[1024,16,64]{0,2,1:T(8,128)(2,1)S(1)} %bitcast.97, f32[16,128,1024]{2,1,0:T(8,128)} %fusion.86, f32[16,128]{1,0:T(8,128)S(1)} %bitcast.125, f32[16,128]{1,0:T(8,128)} %get-tuple-element.57, pred[128,1024]{1,0:T(8,128)(4,1)S(1)} %broadcast_compare_fusion.1, ...), kind=kOutput, calls=%fused_computation.30 | convolution fusion | flops 549715968 | bytes 13254656 | tf_op jit(solution)/shard_map/cond/branch_1_fun/hqk,khd->qhd/dot_general | solution.py:506
  453.4 33.8 %conditional.5 = (bf16[128,1024]{0,1:T(8,128)(2,1)}, bf16[128,1024]{0,1:T(8,128)(2,1)}) conditional(s32[]{:T(128)} %bitcast.36, () %tuple.42, (s32[128]{0:T(128)}, s32[1024]{0:T(1024)S(1)}, bf16[1024,1024]{1,0:T(8,128)(2,1)}, bf16[128,1024]{1,0:T(8,128)(2,1)}, f32[1024,16]{0,1:T(8,128)}, /*index=5*/bf16[1024,1024]{1,0:T(8,128)(2,1)}, ...), branch_computations={%region_15.16_spmd, %region_16.17_spmd} | conditional | flops 1095237632 | bytes 44634640 | solution.py:541
  470.4 10.7 %fusion.34 = bf16[16,128,64]{1,2,0:T(8,128)(2,1)} fusion(bf16[1024,16,64]{0,2,1:T(8,128)(2,1)S(1)} %bitcast.99, f32[16,1024,128]{2,1,0:T(8,128)} %fusion.87, f32[16,1024]{1,0:T(8,128)} %bitcast.124, f32[16,1024]{1,0:T(8,128)} %bitcast.122, pred[1024,128]{1,0:T(8,128)(4,1)S(1)} %broadcast_compare_fusion.2, bf16[1024,16,64]{0,2,1:T(8,128)(2,1)} %bitcast.106, ...), kind=kOutput, calls=%fused_computation.43 | convolution fusion | flops 549715968 | bytes 13369344 | tf_op jit(solution)/shard_map/cond/branch_1_fun/hqk,qhd->khd/dot_general | solution.py:527
  481.1 6.1 fusion.35
  497.6 51.1 %reduce-scatter.7.cloned.1.call-done = bf16[256,3072]{1,0:T(8,128)(2,1)} async-done(((bf16[1024,3072]{1,0:T(8,128)(2,1)}), bf16[256,3072]{1,0:T(8,128)(2,1)}) %reduce-scatter.7.cloned.1.call-update) | async-done | bytes 1572880 | tf_op jit(solution)/shard_map/reduce_scatter | solution.py:566
  548.7 9.9 %convolution_bitcast_fusion.1 = f32[1,2,1024,1024]{3,2,1,0:T(8,128)} fusion(bf16[2,768,1024]{2,1,0:T(8,128)(2,1)} %get-tuple-element.100, bf16[2,768,1024]{2,1,0:T(8,128)(2,1)} %get-tuple-element.101), kind=kOutput, calls=%fused_computation.53 | convolution fusion | flops 3221225472 | bytes 14680064 | tf_op jit(solution)/shard_map/krf,krd->kfd/dot_general | solution.py:441
  564.4 6.9 reduce-scatter.13.cloned.1.call-done
  578.2 5.8 all-reduce
  584.1 9.0 %reduce-scatter.11.cloned.1.call-done = bf16[8,256]{1,0:T(8,128)(2,1)} async-done(((bf16[8,1024]{1,0:T(8,128)(2,1)}), bf16[8,256]{1,0:T(8,128)(2,1)}) %reduce-scatter.11.cloned.1.call-update) | async-done | bytes 4112 | tf_op jit(solution)/shard_map/reduce_scatter | solution.py:572
  593.1 22.6 %all-reduce.1 = (bf16[256]{0:T(256)(128)(2,1)S(1)}, bf16[8,256]{1,0:T(8,128)(2,1)S(1)}) all-reduce(bf16[256]{0:T(256)(128)(2,1)S(1)} %dynamic-slice.1, bf16[8,256]{1,0:T(8,128)(2,1)} %reduce-scatter.11.cloned.1.call-done), channel_id=1, replica_groups=mesh['dp'=4,'expert'=8] {'expert'}, use_global_device_ids=true, to_apply=%region_21.22 | all-reduce | flops 2304 | bytes 9216 | tf_op jit(solution)/shard_map/psum | solution.py:580
  617.9 81.4 %all-reduce.5.cloned.1.call-done = (bf16[256,3072]{1,0:T(8,128)(2,1)}, bf16[256,1024]{1,0:T(8,128)(2,1)}) async-done(((bf16[256,3072]{1,0:T(8,128)(2,1)}, bf16[256,1024]{1,0:T(8,128)(2,1)}), (bf16[256,3072]{1,0:T(8,128)(2,1)}, bf16[256,1024]{1,0:T(8,128)(2,1)})) %all-reduce.5.cloned.1.call-update) | async-done | bytes 2097168 | tf_op jit(solution)/shard_map/psum | solution.py:581
  (162 shorter events, 138.5 us)
Async XLA Ops:
  7.2 51.6 %all-gather.8.cloned.1.call-start = ((), (), s32[]{:S(2)}) async-start(), calls=%async_computation.8 | async-start | bytes 7864320 | tf_op jit(solution)/shard_map/all_gather | solution.py:54
  7.9 104.9 %all-gather.12.cloned.1.call-start = ((), (), s32[]{:S(2)}) async-start(), calls=%async_computation.10 | async-start | bytes 2359296 | tf_op jit(solution)/shard_map/all_gather | solution.py:370
  15.7 43.0 %copy-start.13 = (f32[128]{0:T(128)}, f32[128]{0:T(128)S(1)}, u32[]{:S(2)}) copy-start(f32[128]{0:T(128)S(1)} %broadcast_multiply_fusion.2) | copy-start | bytes 1540
  16.9 41.8 %copy-start.15 = (f32[128]{0:T(128)}, f32[128]{0:T(128)S(1)}, u32[]{:S(2)}) copy-start(f32[128]{0:T(128)S(1)} %add_rsqrt_fusion) | copy-start | bytes 1540
  63.6 99.1 %copy-start.7 = (bf16[128,1024]{1,0:T(8,128)(2,1)}, bf16[128,1024]{1,0:T(8,128)(2,1)S(1)}, u32[]{:S(2)}) copy-start(bf16[128,1024]{1,0:T(8,128)(2,1)S(1)} %get-tuple-element.180) | copy-start | bytes 786436
  63.6 99.0 %all-gather.10.cloned.1.call-start = ((), (), s32[]{:S(2)}) async-start(), calls=%async_computation.9 | async-start | bytes 2359296 | tf_op jit(solution)/shard_map/all_gather | solution.py:369
  64.3 120.8 %all-gather.14.cloned.1.call-start = ((), (), s32[]{:S(2)}) async-start(), calls=%async_computation.11 | async-start | bytes 2621440 | tf_op jit(solution)/shard_map/all_gather | solution.py:55
  71.1 123.7 %copy-start.24 = (s32[128]{0:T(128)}, s32[128]{0:T(128)S(1)}, u32[]{:S(2)}) copy-start(s32[128]{0:T(128)S(1)} %fusion.80) | copy-start | bytes 1540
  71.4 113.8 %copy-start.4 = (f32[128,1024]{1,0:T(8,128)}, f32[128,1024]{1,0:T(8,128)S(1)}, u32[]{:S(2)}) copy-start(f32[128,1024]{1,0:T(8,128)S(1)} %fusion.74) | copy-start | bytes 1572868
  182.6 142.4 %copy-start.8 = (bf16[128,16,64]{0,2,1:T(8,128)(2,1)}, bf16[128,16,64]{0,2,1:T(8,128)(2,1)S(1)}, u32[]{:S(2)}) copy-start(bf16[128,16,64]{0,2,1:T(8,128)(2,1)S(1)} %fusion.68) | copy-start | bytes 786436
  189.3 17.6 %all-to-all-start.1 = ((bf16[8,24,1024]{2,1,0:T(8,128)(2,1)}), bf16[8,24,1024]{2,1,0:T(8,128)(2,1)S(1)}, u32[]{:S(2)}, u32[]{:S(2)}) async-start(bf16[8,24,1024]{2,1,0:T(8,128)(2,1)} %bitcast.28), calls=%async_computation.1 | async-start | bytes 786432 | tf_op jit(solution)/shard_map/all_to_all | solution.py:425
  206.9 15.5 %all-to-all-start = ((bf16[8,24,1024]{2,1,0:T(8,128)(2,1)}), bf16[8,24,1024]{2,1,0:T(8,128)(2,1)S(1)}, u32[]{:S(2)}, u32[]{:S(2)}) async-start(bf16[8,24,1024]{2,1,0:T(8,128)(2,1)} %bitcast.26), calls=%async_computation | async-start | bytes 786432 | tf_op jit(solution)/shard_map/all_to_all | solution.py:415
  210.5 242.9 %all-gather.16.cloned.1.call-start = ((), (), s32[]{:S(2)}) async-start(), calls=%async_computation.12 | async-start | bytes 2359296 | tf_op jit(solution)/shard_map/all_gather | solution.py:478
  223.1 119.9 %copy-start.25 = (s32[128]{0:T(128)S(1)}, s32[128]{0:T(128)}, u32[]{:S(2)}) copy-start(s32[128]{0:T(128)} %copy-done.24) | copy-start | bytes 1540
  339.5 14.3 %all-to-all-start.2 = ((bf16[8,24,1024]{2,1,0:T(8,128)(2,1)}), bf16[8,24,1024]{2,1,0:T(8,128)(2,1)S(1)}, u32[]{:S(2)}, u32[]{:S(2)}) async-start(bf16[8,24,1024]{2,1,0:T(8,128)(2,1)} %bitcast.119), calls=%async_computation.2 | async-start | bytes 786432 | tf_op jit(solution)/shard_map/all_to_all | solution.py:442
  343.0 110.5 %all-gather.18.cloned.1.call-start = ((), (), s32[]{:S(2)}) async-start(), calls=%async_computation.13 | async-start | bytes 2359296 | tf_op jit(solution)/shard_map/all_gather | solution.py:479
  355.7 65.1 %copy-start.1 = (bf16[1024,1024]{1,0:T(8,128)(2,1)S(1)}, bf16[1024,1024]{1,0:T(8,128)(2,1)}, u32[]{:S(2)}) copy-start(bf16[1024,1024]{1,0:T(8,128)(2,1)} %all-gather.12.cloned.1.call-done) | copy-start | bytes 6291460
  359.0 138.5 %reduce-scatter.9.cloned.1.call-start = ((), (), s32[]{:S(2)}) async-start(), calls=%async_computation.15 | async-start | bytes 2621440 | tf_op jit(solution)/shard_map/reduce_scatter | solution.py:569
  362.1 186.6 %reduce-scatter.7.cloned.1.call-start = ((), (), s32[]{:S(2)}) async-start(), calls=%async_computation.14 | async-start | bytes 7864320 | tf_op jit(solution)/shard_map/reduce_scatter | solution.py:566
  453.4 33.8 %copy-start.14 = (f32[128]{0:T(128)S(1)}, f32[128]{0:T(128)}, u32[]{:S(2)}) copy-start(f32[128]{0:T(128)} %copy-done.13) | copy-start | bytes 1540
  453.4 33.8 %copy-start.16 = (f32[128]{0:T(128)S(1)}, f32[128]{0:T(128)}, u32[]{:S(2)}) copy-start(f32[128]{0:T(128)} %copy-done.15) | copy-start | bytes 1540
  493.1 78.2 %reduce-scatter.13.cloned.1.call-start = ((), (), s32[]{:S(2)}) async-start(), calls=%async_computation.17 | async-start | bytes 327680
  494.9 98.1 %reduce-scatter.11.cloned.1.call-start = ((), (), s32[]{:S(2)}) async-start(), calls=%async_computation.16 | async-start | bytes 20480 | tf_op jit(solution)/shard_map/reduce_scatter | solution.py:572
  496.0 203.3 %all-reduce.5.cloned.1.call-start = ((), (), s32[]{:S(2)}) async-start(), calls=%async_computation.18 | async-start | bytes 4194304 | tf_op jit(solution)/shard_map/psum | solution.py:581
  (19 other events, 170.5 us)
Sparse Core Ops, SparseCore 0:
  9.5 49.1 all-gather.7
  63.7 49.0 all-gather.11
  115.0 47.6 all-gather.9
  164.0 21.0 all-gather.13
  216.0 49.0 all-gather.15
  359.1 47.8 all-gather.17
  410.1 29.9 reduce-scatter.8
  493.2 55.4 reduce-scatter.6
  551.2 20.0 reduce-scatter.12
  573.5 19.5 reduce-scatter.10
  596.7 102.5 all-reduce.4

commit v2 on v0

--- a/solution.py
+++ b/solution.py
@@ -3,6 +3,8 @@
 import jax
 import jax.numpy as jnp
 from jax import lax
+from jax.experimental import pallas as pl
+from jax.experimental.pallas import tpu as pltpu
 from jax.sharding import PartitionSpec as P
 
 HEADS = 16
@@ -74,6 +76,894 @@
         jnp.zeros((experts * capacity, rows_low.shape[1]), rows_low.dtype).at[target].set(rows_low)
     )
     return buffer_rows.reshape(experts, capacity, rows_low.shape[1])
+
+
+BF = jnp.bfloat16
+F32 = jnp.float32
+NT = (((1,), (1,)), ((), ()))
+TN = (((0,), (0,)), ((), ()))
+TILE = 256
+MESH_ID = pl.DeviceIdType.MESH
+
+
+def mean_last(v):
+    return jnp.mean(v, axis=-1, keepdims=True)
+
+
+def dp_peers():
+    me = lax.axis_index("dp")
+    sibling = me + 1 - 2 * lax.rem(me, 2)
+    across = lax.rem(me + 2, 4)
+    diagonal = lax.rem(sibling + 2, 4)
+    return me, sibling, across, diagonal
+
+
+def expert_peers():
+    me = lax.axis_index("expert")
+    z, x = me // 2, lax.rem(me, 2)
+    beside = me + 1 - 2 * x
+    near = z + 1 - 2 * lax.rem(z, 2)
+    low, high = lax.rem(z, 2), z // 2
+    inner = low + high - 2 * low * high
+    flip, turn = 3 - z, lax.rem(z + 2, 4)
+    second = inner * flip + (1 - inner) * turn
+    third = inner * turn + (1 - inner) * flip
+    return me, z, x, beside, (near, second, third)
+
+
+def greet(targets):
+    barrier = pltpu.get_barrier_semaphore()
+    for target in targets:
+        pl.semaphore_signal(barrier, inc=1, device_id=target, device_id_type=MESH_ID)
+    pl.semaphore_wait(barrier, len(targets))
+
+
+def others(n, me):
+    return [lax.rem(me + d, n) for d in range(1, n)]
+
+
+def push(src, dst, send, recv, target):
+    return pltpu.make_async_remote_copy(
+        src_ref=src, dst_ref=dst, send_sem=send, recv_sem=recv, device_id=target, device_id_type=MESH_ID
+    )
+
+
+def spread_plan(own_src, slots, send, recv):
+    me, z, x, beside, zs = expert_peers()
+
+    def first(i):
+        if i == 0:
+            return push(own_src, slots.at[me], send.at[0], recv.at[me], {"expert": beside})
+        return push(own_src, slots.at[me], send.at[i], recv.at[me], {"expert": 2 * zs[i - 1] + x})
+
+    def arrival(zz, xx):
+        s = 2 * zz + xx
+        return push(slots.at[s], slots.at[s], send.at[0], recv.at[s], {"expert": beside})
+
+    def passed(i):
+        s = 2 * zs[i] + x
+        return push(slots.at[s], slots.at[s], send.at[4 + i], recv.at[s], {"expert": beside})
+
+    return first, arrival, passed
+
+
+def lane_masks(rows):
+    lane = lax.broadcasted_iota(jnp.int32, (rows, 128), 1)
+    return lane < HEAD
+
+
+def front_kernel(
+    tok, small, wqkv, wout,
+    olow, normed_out, qkv_out, mixed_out, lse_out, wout_full, small_full,
+    held, wblk, normed, qkv, mixed, lse, mixed_low, gain, bounce, smalls,
+    tok_send, tok_recv, w_send, w_recv, o_send, o_recv, copy_sem,
+):
+    j, sibling, across, diagonal = dp_peers()
+    e, z, x, beside, zs = expert_peers()
+    rows, width = tok.shape
+    shard = wqkv.shape[0]
+    lanes = 128
+
+    def mine(s):
+        return pl.ds(pl.multiple_of(s * shard, shard), shard)
+
+    mycols = pl.ds(pl.multiple_of(e * lanes, lanes), lanes)
+    own_tok = pltpu.make_async_copy(tok, held.at[e], copy_sem.at[0])
+    own_tok.start()
+    own_w = [
+        pltpu.make_async_copy(
+            wqkv.at[:, pl.ds(pl.multiple_of(i * width + e * lanes, lanes), lanes)],
+            wblk.at[mine(j), pl.ds(i * lanes, lanes)],
+            copy_sem.at[1 + i],
+        )
+        for i in range(3)
+    ]
+    for cp in own_w:
+        cp.start()
+    own_out = pltpu.make_async_copy(wout, bounce, copy_sem.at[4])
+    own_out.start()
+    smalls[j] = small[...]
+    greet([{"expert": p} for p in others(8, e)] + [{"dp": p} for p in (sibling, across, diagonal)])
+
+    first, arrival, passed = spread_plan(tok, held, tok_send, tok_recv)
+    for i in (1, 2, 3, 0):
+        first(i).start()
+    for cp in own_w:
+        cp.wait()
+
+    def w_copy(kind):
+        if kind == 0:
+            return push(wblk.at[mine(j)], wblk.at[mine(j)], w_send.at[0], w_recv.at[j], {"dp": sibling})
+        if kind == 1:
+            return push(wblk.at[mine(j)], wblk.at[mine(j)], w_send.at[1], w_recv.at[j], {"dp": across})
+        return push(wblk.at[mine(across)], wblk.at[mine(across)], w_send.at[2], w_recv.at[across], {"dp": sibling})
+
+    def w_arrival(s):
+        return push(wblk.at[mine(s)], wblk.at[mine(s)], w_send.at[0], w_recv.at[s], {"dp": sibling})
+
+    def s_copy(i):
+        return push(small, smalls.at[j], w_send.at[3 + i], w_recv.at[4 + j], {"dp": (sibling, across, diagonal)[i]})
+
+    def s_arrival(s):
+        return push(small, smalls.at[s], w_send.at[3], w_recv.at[4 + s], {"dp": sibling})
+
+    def out_copy(kind):
+        if kind == 0:
+            return push(wout, wout_full.at[mine(j)], w_send.at[6], w_recv.at[8 + j], {"dp": sibling})
+        if kind == 1:
+            return push(wout, wout_full.at[mine(j)], w_send.at[7], w_recv.at[8 + j], {"dp": across})
+        return push(wout_full.at[mine(across)], wout_full.at[mine(across)], w_send.at[8], w_recv.at[8 + across], {"dp": sibling})
+
+    def out_arrival(s):
+        return push(wout, wout_full.at[mine(s)], w_send.at[6], w_recv.at[8 + s], {"dp": sibling})
+
+    for i in range(3):
+        s_copy(i).start()
+    w_copy(1).start()
+    w_copy(0).start()
+    out_copy(1).start()
+    out_copy(0).start()
+    own_out.wait()
+    keep_out = pltpu.make_async_copy(bounce, wout_full.at[mine(j)], copy_sem.at[4])
+    keep_out.start()
+    for s in (sibling, across, diagonal):
+        s_arrival(s).wait_recv()
+    gain[...] = jnp.concatenate([smalls[s, 0:1, :] for s in range(4)], axis=1).astype(F32)
+    w_arrival(across).wait_recv()
+    w_copy(2).start()
+    w_arrival(sibling).wait_recv()
+    w_arrival(diagonal).wait_recv()
+
+    def project(zz):
+        base = zz * 2 * rows
+        for xx in range(2):
+            def norm_rows(t, c):
+                rs = pl.ds(pl.multiple_of(t * 64, 64), 64)
+                v = held[2 * zz + xx, rs, :].astype(F32)
+                center = v - mean_last(v)
+                inverse = lax.rsqrt(mean_last(center * center) + EPS)
+                at = pl.ds(pl.multiple_of(base + xx * rows + t * 64, 64), 64)
+                normed[at, :] = (center * inverse * gain[...]).astype(BF)
+                return c
+            lax.fori_loop(0, rows // 64, norm_rows, 0)
+        at = pl.ds(pl.multiple_of(base, 2 * rows), 2 * rows)
+        qkv[at, :] = jnp.dot(normed[at, :], wblk[...], preferred_element_type=F32).astype(BF)
+
+    own_tok.wait()
+    arrival(z, 1 - x).wait_recv()
+    project(z)
+    for i in range(2):
+        arrival(zs[i], x).wait_recv()
+        passed(i).start()
+    arrival(zs[0], 1 - x).wait_recv()
+    project(zs[0])
+    out_arrival(across).wait_recv()
+    out_copy(2).start()
+    arrival(zs[2], x).wait_recv()
+    passed(2).start()
+    arrival(zs[1], 1 - x).wait_recv()
+    project(zs[1])
+    arrival(zs[2], 1 - x).wait_recv()
+    project(zs[2])
+    stores = [
+        pltpu.make_async_copy(normed, normed_out, copy_sem.at[0]),
+        pltpu.make_async_copy(qkv, qkv_out, copy_sem.at[1]),
+    ]
+    for cp in stores:
+        cp.start()
+
+    def o_copy(dest):
+        return push(mixed_low.at[pl.ds(dest * rows, rows)], olow.at[:, mycols], o_send.at[dest], o_recv.at[e], {"expert": dest})
+
+    def o_own(dest):
+        return pltpu.make_async_copy(mixed_low.at[pl.ds(dest * rows, rows)], olow.at[:, mycols], copy_sem.at[5])
+
+    left = lane_masks(2 * rows)
+    for b in (3, 2, 1, 0):
+        qs = qkv[pl.ds(b * 2 * rows, 2 * rows), 0:lanes]
+        keys = qkv[0 : (b + 1) * 2 * rows, lanes : 2 * lanes]
+        vals = qkv[0 : (b + 1) * 2 * rows, 2 * lanes : 3 * lanes]
+        outs, logs = [], []
+        for h in range(2):
+            mask = left if h == 0 else jnp.logical_not(left)
+            q_h = jnp.where(mask, qs.astype(F32) * (HEAD ** -0.5), 0.0).astype(BF)
+            sc = lax.dot_general(q_h, keys, NT, preferred_element_type=F32)
+            top = jnp.max(sc, axis=-1, keepdims=True)
+            pr = jnp.exp(sc - top)
+            tot = jnp.sum(pr, axis=-1, keepdims=True)
+            outs.append(jnp.dot(pr.astype(BF), vals, preferred_element_type=F32) / tot)
+            logs.append(top + jnp.log(tot))
+        at = pl.ds(b * 2 * rows, 2 * rows)
+        res = jnp.where(left, outs[0], outs[1])
+        mixed[at, :] = res
+        mixed_low[at, :] = res.astype(BF)
+        lse[at, :] = jnp.where(left, logs[0], logs[1])
+        for dest in (2 * b, 2 * b + 1):
+            @pl.when(dest != e)
+            def _():
+                o_copy(dest).start()
+
+            @pl.when(dest == e)
+            def _():
+                o_own(dest).start()
+    more = [
+        pltpu.make_async_copy(mixed, mixed_out, copy_sem.at[2]),
+        pltpu.make_async_copy(lse, lse_out, copy_sem.at[3]),
+        pltpu.make_async_copy(smalls, small_full, copy_sem.at[6]),
+    ]
+    for cp in more:
+        cp.start()
+    for dest in range(8):
+        @pl.when(dest != e)
+        def _():
+            push(mixed_low.at[pl.ds(0, rows)], olow.at[:, pl.ds(dest * lanes, lanes)], o_send.at[dest], o_recv.at[dest], {"expert": dest}).wait_recv()
+            o_copy(dest).wait_send()
+
+        @pl.when(dest == e)
+        def _():
+            o_own(dest).wait()
+    for s in (sibling, diagonal):
+        out_arrival(s).wait_recv()
+    for i in range(4):
+        first(i).wait_send()
+    for i in range(3):
+        passed(i).wait_send()
+        w_copy(i).wait_send()
+        s_copy(i).wait_send()
+        out_copy(i).wait_send()
+    keep_out.wait()
+    for cp in stores + more:
+        cp.wait()
+
+
+def front_block(tokens, small, qkv_weight, out_weight):
+    rows, width = tokens.shape
+    seq = 8 * rows
+    shard = qkv_weight.shape[0]
+    any_spec = pl.BlockSpec(memory_space=pl.ANY)
+    vmem_spec = pl.BlockSpec(memory_space=pltpu.VMEM)
+    V = pltpu.VMEM
+    D = pltpu.SemaphoreType.DMA
+    S = jax.ShapeDtypeStruct
+    return pl.pallas_call(
+        front_kernel,
+        out_shape=(
+            S((rows, width), BF), S((seq, width), BF), S((seq, 384), BF), S((seq, 128), F32), S((seq, 128), F32),
+            S((width, width), BF), S((4,) + small.shape, BF),
+        ),
+        in_specs=[any_spec, vmem_spec, any_spec, any_spec],
+        out_specs=(any_spec,) * 7,
+        scratch_shapes=[
+            V((8, rows, width), BF), V((width, 384), BF), V((seq, width), BF), V((seq, 384), BF),
+            V((seq, 128), F32), V((seq, 128), F32), V((seq, 128), BF), V((1, width), F32), V((shard, width), BF),
+            V((4,) + small.shape, BF),
+            D((7,)), D((8,)), D((9,)), D((12,)), D((8,)), D((8,)), D((8,)),
+        ],
+        compiler_params=pltpu.CompilerParams(collective_id=2, has_side_effects=True, vmem_limit_bytes=56 * 1024 * 1024),
+        name="front_block",
+    )(tokens, small, qkv_weight, out_weight)
+
+
+def expert_kernel(
+    zslots, dslots, olow, gain_ref, w1_hbm, w2_hbm,
+    returned, came_back, olow_full, ggain_ref, n_out, h_out, df_out, du_out,
+    w1, w2, x, hid, gpr, unit_s, inv_s, state, total, grad_in, own, far, f1, f3, ssum, rf1, rf3, rss,
+    zland, dland, bsend, gsend,
+    send_sem, recv_sem, a_send, a_recv, g_send, g_recv, copy_sem, own_sem,
+):
+    cap, width = zslots.shape[1:]
+    half = 4 * cap
+    pair_rows = 2 * half
+    tiles = width // TILE
+    j, sibling, across, diagonal = dp_peers()
+    e, zpos, xpos, beside, zs = expert_peers()
+
+    loads = []
+    for i, (src, dst) in enumerate(
+        [(w1_hbm.at[0, 0], w1.at[0]), (w2_hbm.at[0, 0], w2.at[0]),
+         (w1_hbm.at[0, 1], w1.at[1]), (w2_hbm.at[0, 1], w2.at[1])]
+    ):
+        cp = pltpu.make_async_copy(src, dst, copy_sem.at[i])
+        cp.start()
+        loads.append(cp)
+    own_z = pltpu.make_async_copy(zslots.at[e], zland.at[e], own_sem.at[0])
+    own_d = pltpu.make_async_copy(dslots.at[e], dland.at[e], own_sem.at[1])
+    own_z.start()
+    own_d.start()
+    greet([{"expert": p} for p in others(8, e)] + [{"dp": sibling}, {"dp": across}])
+
+    def swap(src, dst, which, dest):
+        return push(src.at[dest], dst.at[e], a_send.at[which * 8 + dest], a_recv.at[which * 8 + e], {"expert": dest})
+
+    def swap_arrival(src, dst, which, source):
+        return push(src.at[source], dst.at[source], a_send.at[which * 8 + source], a_recv.at[which * 8 + source], {"expert": source})
+
+    peers = others(8, e)
+    for dest in peers:
+        swap(zslots, zland, 0, dest).start()
+    for dest in peers:
+        swap(dslots, dland, 1, dest).start()
+    first, arrival, passed = spread_plan(olow, olow_full, g_send, g_recv)
+    own_o = pltpu.make_async_copy(olow, olow_full.at[e], copy_sem.at[12])
+    own_o.start()
+
+    def rows_of(h, r):
+        return pl.ds((h * 4 + r) * half, half)
+
+    def remote(src, dst, kind, p, h, peer):
+        i = (p * 2 + h) * 6 + kind
+        return push(src, dst, send_sem.at[i], recv_sem.at[i], {"dp": peer})
+
+    def copy_of(kind, p, h):
+        q = p * 2 + h
+        if kind == 0:
+            return remote(x.at[p, rows_of(h, 0)], x.at[p, rows_of(h, 1)], 0, p, h, sibling)
+        if kind == 1:
+            return remote(x.at[p, rows_of(h, 0)], x.at[p, rows_of(h, 2)], 1, p, h, across)
+        if kind == 2:
+            return remote(x.at[p, rows_of(h, 2)], x.at[p, rows_of(h, 3)], 2, p, h, sibling)
+        if kind == 3:
+            return remote(f1.at[q], rf1.at[q], 3, p, h, sibling)
+        if kind == 4:
+            return remote(f3.at[q], rf3.at[q], 4, p, h, sibling)
+        return remote(ssum.at[q], rss.at[q], 5, p, h, across)
+
+    layer_of = (0, 1, 1, 0)
+
+    def start_rows(p, h):
+        k = layer_of[p]
+        rs = pl.ds(h * half, half)
+        if p < 2:
+            v = state[rs, :]
+            center = v - mean_last(v)
+            inverse = lax.rsqrt(mean_last(center * center) + EPS)
+            unit = center * inverse
+            unit_s[k, rs, :] = unit
+            inv_s[k, rs, :] = jnp.broadcast_to(inverse, (half, 128))
+            x[p, rows_of(h, 0), :] = (unit * gain_ref[pl.ds(k, 1), :]).astype(BF)
+        else:
+            x[p, rows_of(h, 0), :] = (grad_in[rs, :] + state[rs, :]).astype(BF)
+        copy_of(1, p, h).start()
+        copy_of(0, p, h).start()
+
+    def compute(p, h, pair):
+        k = layer_of[p]
+        base = pl.ds((h * 2 + pair) * pair_rows, pair_rows)
+        left_w, right_w = (w1, w2) if p < 2 else (w2, w1)
+        q = p * 2 + h
+
+        def up(t, c):
+            cols = pl.ds(pl.multiple_of(t * TILE, TILE), TILE)
+            pre = lax.dot_general(x[p, base, :], left_w[k, cols, :], NT, preferred_element_type=F32)
+            if p < 2:
+                cdf = 0.5 * (1.0 + lax.erf(pre * (0.5 ** 0.5)))
+                pdf = jnp.exp(-0.5 * pre * pre) * 0.3989422804014327
+                hid[k, base, cols] = (pre * cdf).astype(BF)
+                gpr[k, base, cols] = cdf + pre * pdf
+            else:
+                hid[2 + k, base, cols] = (pre * gpr[k, base, cols]).astype(BF)
+            return c
+
+        lax.fori_loop(0, tiles, up, 0)
+        slot = k if p < 2 else 2 + k
+
+        def down(t, c):
+            cols = pl.ds(pl.multiple_of(t * TILE, TILE), TILE)
+            res = jnp.dot(hid[slot, base, :], right_w[k, :, cols], preferred_element_type=F32)
+            if pair == 0:
+                own[h, :, cols] = res[:half]
+                f1[q, :, cols] = res[half:].astype(BF)
+            else:
+                far[:, cols] = res[:half]
+                f3[q, :, cols] = res[half:].astype(BF)
+            return c
+
+        lax.fori_loop(0, tiles, down, 0)
+        if pair == 0:
+            copy_of(3, p, h).start()
+        else:
+            copy_of(4, p, h).start()
+            copy_of(4, p, h).wait_recv()
+            ssum[q] = (far[...] + rf3[q].astype(F32)).astype(BF)
+            copy_of(5, p, h).start()
+
+    def give_back(buf, dst, which, h):
+        for dest in range(4 * h, 4 * h + 4):
+            @pl.when(dest != e)
+            def _():
+                swap(buf, dst, which, dest).start()
+
+            @pl.when(dest == e)
+            def _():
+                pltpu.make_async_copy(buf.at[dest], dst.at[dest], own_sem.at[which]).start()
+
+    def finish(p, h):
+        k = layer_of[p]
+        q = p * 2 + h
+        rs = pl.ds(h * half, half)
+        copy_of(3, p, h).wait_recv()
+        copy_of(5, p, h).wait_recv()
+        got = own[h] + rf1[q].astype(F32) + rss[q].astype(F32)
+        if p == 0:
+            state[rs, :] = state[rs, :] + got
+            total[rs, :] = got
+        elif p == 1:
+            total[rs, :] = total[rs, :] + got
+            for i in range(4):
+                bsend[4 * h + i] = total[pl.ds(h * half + i * cap, cap), :].astype(BF)
+            state[rs, :] = jnp.zeros((half, width), F32)
+            give_back(bsend, returned, 2, h)
+        else:
+            unit = unit_s[k, rs, :]
+            part = jnp.sum(got * unit, axis=0, keepdims=True)
+            if h == 0:
+                ggain_ref[pl.ds(k, 1), :] = part
+            else:
+                ggain_ref[pl.ds(k, 1), :] = ggain_ref[pl.ds(k, 1), :] + part
+            a = got * gain_ref[pl.ds(k, 1), :]
+            back = inv_s[k, rs, :][:, :1] * (a - mean_last(a) - unit * mean_last(a * unit))
+            state[rs, :] = state[rs, :] + back
+            if p == 3:
+                for i in range(4):
+                    gsend[4 * h + i] = state[pl.ds(h * half + i * cap, cap), :].astype(BF)
+                give_back(gsend, came_back, 3, h)
+
+    def relay(p, h):
+        copy_of(1, p, h).wait_recv()
+        copy_of(2, p, h).start()
+
+    stores = []
+
+    def store(i, src, dst):
+        cp = pltpu.make_async_copy(src, dst, copy_sem.at[4 + i])
+        cp.start()
+        stores.append(cp)
+
+    def landed(buf, src, own_copy, which, h, out):
+        for source in range(4 * h, 4 * h + 4):
+            @pl.when(source != e)
+            def _():
+                swap_arrival(src, buf, which, source).wait_recv()
+
+            @pl.when(source == e)
+            def _():
+                own_copy.wait()
+        for source in range(4 * h, 4 * h + 4):
+            out[pl.ds(source * cap, cap), :] = buf[source].astype(F32)
+
+    landed(zland, zslots, own_z, 0, 0, state)
+    start_rows(0, 0)
+    landed(zland, zslots, own_z, 0, 1, state)
+    start_rows(0, 1)
+    loads[0].wait()
+    loads[1].wait()
+    for p in range(4):
+        if p == 0:
+            copy_of(0, p, 0).wait_recv()
+            compute(p, 0, 0)
+            for i in (1, 2, 3, 0):
+                first(i).start()
+        relay(p, 0)
+        copy_of(2, p, 0).wait_recv()
+        compute(p, 0, 1)
+        copy_of(0, p, 1).wait_recv()
+        compute(p, 1, 0)
+        relay(p, 1)
+        copy_of(2, p, 1).wait_recv()
+        compute(p, 1, 1)
+        if p == 1:
+            for i in range(3):
+                arrival(zs[i], xpos).wait_recv()
+                passed(i).start()
+            landed(dland, dslots, own_d, 1, 0, grad_in)
+            landed(dland, dslots, own_d, 1, 1, grad_in)
+        finish(p, 0)
+        if p == 0:
+            loads[2].wait()
+            loads[3].wait()
+        if p < 3:
+            start_rows(p + 1, 0)
+            copy_of(0, p + 1, 0).wait_recv()
+            compute(p + 1, 0, 0)
+        finish(p, 1)
+        if p < 3:
+            start_rows(p + 1, 1)
+        k = layer_of[p]
+        if p < 2:
+            store(p * 2, x.at[p], n_out.at[k])
+            store(p * 2 + 1, hid.at[k], h_out.at[k])
+        else:
+            store(p * 2, x.at[p], df_out.at[k])
+            store(p * 2 + 1, hid.at[2 + k], du_out.at[k])
+    own_o.wait()
+    for s in range(4):
+        arrival(s, 1 - xpos).wait_recv()
+    for i in range(4):
+        first(i).wait_send()
+    for i in range(3):
+        passed(i).wait_send()
+    for p in range(4):
+        for h in range(2):
+            for kind in range(6):
+                copy_of(kind, p, h).wait_send()
+    for cp in stores:
+        cp.wait()
+    for dest in peers:
+        swap(zslots, zland, 0, dest).wait_send()
+        swap(dslots, dland, 1, dest).wait_send()
+        swap(bsend, returned, 2, dest).wait_send()
+        swap(gsend, came_back, 3, dest).wait_send()
+        swap_arrival(bsend, returned, 2, dest).wait_recv()
+        swap_arrival(gsend, came_back, 3, dest).wait_recv()
+    pltpu.make_async_copy(bsend.at[0], returned.at[0], own_sem.at[2]).wait()
+    pltpu.make_async_copy(gsend.at[0], came_back.at[0], own_sem.at[3]).wait()
+
+
+def expert_block(zslots, dslots, olow, gains, expert_in, expert_out):
+    sources, cap, width = zslots.shape
+    rows = sources * cap
+    half = rows // 2
+    hidden = expert_in.shape[2]
+    everything = 4 * rows
+    any_spec = pl.BlockSpec(memory_space=pl.ANY)
+    vmem_spec = pl.BlockSpec(memory_space=pltpu.VMEM)
+    S = jax.ShapeDtypeStruct
+    big = S((2, everything, width), BF)
+    V = pltpu.VMEM
+    D = pltpu.SemaphoreType.DMA
+    return pl.pallas_call(
+        expert_kernel,
+        out_shape=(
+            S(zslots.shape, BF), S(zslots.shape, BF), S((8,) + olow.shape, BF), S((2, width), F32),
+            big, big, big, big,
+        ),
+        in_specs=[any_spec] * 3 + [vmem_spec] + [any_spec] * 2,
+        out_specs=(any_spec, any_spec, any_spec, vmem_spec, any_spec, any_spec, any_spec, any_spec),
+        scratch_shapes=[
+            V((2, hidden, width), BF), V((2, hidden, width), BF),
+            V((4, everything, width), BF), V((4, everything, hidden), BF), V((2, everything, hidden), F32),
+            V((2, rows, width), F32), V((2, rows, 128), F32), V((rows, width), F32), V((rows, width), F32),
+            V((rows, width), F32), V((2, half, width), F32), V((half, width), F32),
+        ]
+        + [V((8, half, width), BF)] * 6
+        + [V(zslots.shape, BF)] * 4
+        + [D((48,)), D((48,)), D((32,)), D((32,)), D((7,)), D((8,)), D((13,)), D((4,))],
+        compiler_params=pltpu.CompilerParams(
+            collective_id=1, has_side_effects=True, vmem_limit_bytes=60 * 1024 * 1024
+        ),
+        name="expert_block",
+    )(zslots, dslots, olow, gains, expert_in, expert_out)
+
+
+def back_kernel(
+    gmix, gatt, qkv_hbm, mixed_hbm, lse_rows, normed_hbm, olow_hbm, cent,
+    dq_land, gq_land, go_land, gc_land,
+    dom, dam, qkv, mixed, normed, olow, delta, dq_acc, dqkv,
+    part, f1, f3, ssum, rf1, rf3, rss, gq_own, go_own, cland, csum, cdp,
+    h_send, h_recv, d_send, d_recv, p_send, p_recv, gq_send, gq_recv, go_send, go_recv, c_send, c_recv, copy_sem,
+):
+    j, sibling, across, diagonal = dp_peers()
+    e, zpos, xpos, beside, zs = expert_peers()
+    rows, width = gmix.shape
+    blk = 2 * rows
+    lanes = 128
+    shard = width // 4
+    loads = [
+        pltpu.make_async_copy(src, dst, copy_sem.at[i])
+        for i, (src, dst) in enumerate([(qkv_hbm, qkv), (mixed_hbm, mixed), (olow_hbm, olow), (normed_hbm, normed)])
+    ]
+    for cp in loads:
+        cp.start()
+    peers = others(8, e)
+    greet([{"expert": p} for p in peers] + [{"dp": p} for p in (sibling, across, diagonal)])
+
+    def cols_of(s):
+        return pl.ds(pl.multiple_of(s * lanes, lanes), lanes)
+
+    def rows_of(s):
+        return pl.ds(pl.multiple_of(s * rows, rows), rows)
+
+    def head_copy(src, dst, which, dest):
+        return push(src.at[:, cols_of(dest)], dst.at[rows_of(e)], h_send.at[which * 8 + dest], h_recv.at[which * 8 + e], {"expert": dest})
+
+    def head_arrival(src, dst, which, source):
+        return push(src.at[:, cols_of(source)], dst.at[rows_of(source)], h_send.at[which * 8 + source], h_recv.at[which * 8 + source], {"expert": source})
+
+    for dest in peers:
+        head_copy(gmix, dom, 0, dest).start()
+    for dest in peers:
+        head_copy(gatt, dam, 1, dest).start()
+    for dest in peers:
+        push(cent.at[dest], cland.at[e], c_send.at[dest], c_recv.at[e], {"expert": dest}).start()
+    dom[rows_of(e), :] = gmix[:, cols_of(e)]
+    dam[rows_of(e), :] = gatt[:, cols_of(e)]
+    cland[e] = cent[e]
+
+    def dp_sum_start(buf, n, t):
+        def block(s):
+            return buf[0:n, pl.ds(pl.multiple_of(s * shard, shard), shard)]
+        f3[t, 0:n, :] = block(diagonal).astype(BF)
+        f1[t, 0:n, :] = block(sibling).astype(BF)
+        dp_copy(1, n, t).start()
+        dp_copy(0, n, t).start()
+        dp_copy(1, n, t).wait_recv()
+        ssum[t, 0:n, :] = (block(across) + rf3[t, 0:n, :].astype(F32)).astype(BF)
+        dp_copy(2, n, t).start()
+
+    def dp_copy(kind, n, t):
+        at = pl.ds(0, n)
+        if kind == 0:
+            return push(f1.at[t, at], rf1.at[t, at], p_send.at[t * 3], p_recv.at[t * 3], {"dp": sibling})
+        if kind == 1:
+            return push(f3.at[t, at], rf3.at[t, at], p_send.at[t * 3 + 1], p_recv.at[t * 3 + 1], {"dp": sibling})
+        return push(ssum.at[t, at], rss.at[t, at], p_send.at[t * 3 + 2], p_recv.at[t * 3 + 2], {"dp": across})
+
+    def dp_sum_end(buf, n, t):
+        dp_copy(0, n, t).wait_recv()
+        dp_copy(2, n, t).wait_recv()
+        return buf[0:n, pl.ds(pl.multiple_of(j * shard, shard), shard)] + rf1[t, 0:n, :].astype(F32) + rss[t, 0:n, :].astype(F32)
+
+    for cp in loads[:2]:
+        cp.wait()
+    for source in peers:
+        head_arrival(gmix, dom, 0, source).wait_recv()
+    left_row = lax.broadcasted_iota(jnp.int32, (8, 128), 1) < HEAD
+    row_id = lax.broadcasted_iota(jnp.int32, (8, 128), 0)
+    pick = jnp.where((row_id == 0) == left_row, 1.0, 0.0).astype(F32)
+    delta[...] = lax.dot_general(pick, dom[...].astype(F32) * mixed[...], NT, precision=HIGH, preferred_element_type=F32)
+
+    for source in peers:
+        push(cent.at[source], cland.at[source], c_send.at[source], c_recv.at[source], {"expert": source}).wait_recv()
+    csum[0] = jnp.sum(cland[...], axis=0)
+
+    def c_copy(i):
+        s = (sibling, across, diagonal)[i]
+        return push(csum.at[0, :, pl.ds(pl.multiple_of(s * shard, shard), shard)], cdp.at[j], c_send.at[8 + i], c_recv.at[8 + j], {"dp": s})
+
+    def c_arrival(s):
+        return push(csum.at[0, :, pl.ds(0, shard)], cdp.at[s], c_send.at[8], c_recv.at[8 + s], {"dp": sibling})
+
+    for i in range(3):
+        c_copy(i).start()
+    cdp[j] = csum[0, :, pl.ds(pl.multiple_of(j * shard, shard), shard)]
+
+    left = lane_masks(blk)
+    dq_acc[...] = jnp.zeros_like(dq_acc)
+
+    def d_copy(dest):
+        return push(dqkv.at[pl.ds(dest * rows, rows)], dq_land.at[e], d_send.at[dest], d_recv.at[e], {"expert": dest})
+
+    for b in range(4):
+        at = pl.ds(b * blk, blk)
+        tail = pl.ds(b * blk, 8 * rows - b * blk)
+        qs = qkv[tail, 0:lanes]
+        dos = dom[tail, :]
+        keys = qkv[at, lanes : 2 * lanes].astype(F32) * (HEAD ** -0.5)
+        vals = qkv[at, 2 * lanes : 3 * lanes]
+        dks, dvs = [], []
+        for h in range(2):
+            mask = left if h == 0 else jnp.logical_not(left)
+            k_h = jnp.where(mask, keys, 0.0).astype(BF)
+            v_h = jnp.where(mask, vals.astype(F32), 0.0).astype(BF)
+            sc = lax.dot_general(k_h, qs, NT, preferred_element_type=F32)
+            pr = jnp.exp(sc - lse_rows[h : h + 1, tail])
+            dp = lax.dot_general(v_h, dos, NT, preferred_element_type=F32)
+            ds = (pr * (dp - delta[h : h + 1, tail])).astype(BF)
+            dvs.append(jnp.dot(pr.astype(BF), dos, preferred_element_type=F32))
+            dks.append(jnp.dot(ds, qs, preferred_element_type=F32))
+            dq_acc[tail, :] += lax.dot_general(ds, k_h, TN, preferred_element_type=F32)
+        dqkv[at, 0:lanes] = dq_acc[at, :].astype(BF)
+        dqkv[at, lanes : 2 * lanes] = (jnp.where(left, dks[0], dks[1]) * (HEAD ** -0.5)).astype(BF)
+        dqkv[at, 2 * lanes : 3 * lanes] = jnp.where(left, dvs[0], dvs[1]).astype(BF)
+        for dest in (2 * b, 2 * b + 1):
+            @pl.when(dest != e)
+            def _():
+                d_copy(dest).start()
+
+            @pl.when(dest == e)
+            def _():
+                pltpu.make_async_copy(dqkv.at[pl.ds(dest * rows, rows)], dq_land.at[dest], copy_sem.at[4]).start()
+        if b == 0:
+            loads[2].wait()
+            for source in peers:
+                head_arrival(gatt, dam, 1, source).wait_recv()
+            part[0:lanes, :] = lax.dot_general(dam[...], olow[...], TN, preferred_element_type=F32)
+            dp_sum_start(part, lanes, 0)
+        if b == 1:
+            go_own[...] = dp_sum_end(part, lanes, 0).T.astype(BF)
+            go_first, go_arrival, go_passed = spread_plan(go_own, go_land, go_send, go_recv)
+            for i in (1, 2, 3, 0):
+                go_first(i).start()
+            own_go = pltpu.make_async_copy(go_own, go_land.at[e], copy_sem.at[5])
+            own_go.start()
+            for s in (sibling, across, diagonal):
+                c_arrival(s).wait_recv()
+            csum[1, :, 0:shard] = jnp.sum(cdp[...], axis=0)
+            for dest in peers:
+                push(csum.at[1, :, pl.ds(0, shard)], gc_land.at[e], c_send.at[12 + dest], c_recv.at[12 + e], {"expert": dest}).start()
+            own_gc = pltpu.make_async_copy(csum.at[1, :, pl.ds(0, shard)], gc_land.at[e], copy_sem.at[6])
+            own_gc.start()
+    loads[3].wait()
+    part[...] = lax.dot_general(dqkv[...], normed[...], TN, preferred_element_type=F32)
+    dp_sum_start(part, 3 * lanes, 1)
+    for i in range(3):
+        go_arrival(zs[i], xpos).wait_recv()
+        go_passed(i).start()
+    gq_own[...] = dp_sum_end(part, 3 * lanes, 1).T.astype(BF)
+    gq_first, gq_arrival, gq_passed = spread_plan(gq_own, gq_land, gq_send, gq_recv)
+    for i in (1, 2, 3, 0):
+        gq_first(i).start()
+    own_gq = pltpu.make_async_copy(gq_own, gq_land.at[e], copy_sem.at[7])
+    own_gq.start()
+    for i in range(3):
+        gq_arrival(zs[i], xpos).wait_recv()
+        gq_passed(i).start()
+    for s in range(4):
+        go_arrival(s, 1 - xpos).wait_recv()
+        gq_arrival(s, 1 - xpos).wait_recv()
+    for source in range(8):
+        @pl.when(source != e)
+        def _():
+            push(dqkv.at[pl.ds(0, rows)], dq_land.at[source], d_send.at[source], d_recv.at[source], {"expert": source}).wait_recv()
+            d_copy(source).wait_send()
+            push(csum.at[1, :, pl.ds(0, shard)], gc_land.at[source], c_send.at[12 + source], c_recv.at[12 + source], {"expert": source}).wait()
+
+        @pl.when(source == e)
+        def _():
+            pltpu.make_async_copy(dqkv.at[pl.ds(0, rows)], dq_land.at[source], copy_sem.at[4]).wait()
+    for dest in peers:
+        head_copy(gmix, dom, 0, dest).wait_send()
+        head_copy(gatt, dam, 1, dest).wait_send()
+        push(cent.at[dest], cland.at[e], c_send.at[dest], c_recv.at[e], {"expert": dest}).wait_send()
+    for i in range(3):
+        c_copy(i).wait_send()
+        dp_copy(i, lanes, 0).wait_send()
+        dp_copy(i, 3 * lanes, 1).wait_send()
+        go_passed(i).wait_send()
+        gq_passed(i).wait_send()
+    for i in range(4):
+        go_first(i).wait_send()
+        gq_first(i).wait_send()
+    for cp in (own_go, own_gc, own_gq):
+        cp.wait()
+
+
+def back_block(gmix, gatt, qkv, mixed, lse_rows, normed, olow_full, cent):
+    rows, width = gmix.shape
+    seq = 8 * rows
+    shard = width // 4
+    any_spec = pl.BlockSpec(memory_space=pl.ANY)
+    vmem_spec = pl.BlockSpec(memory_space=pltpu.VMEM)
+    S = jax.ShapeDtypeStruct
+    V = pltpu.VMEM
+    D = pltpu.SemaphoreType.DMA
+    return pl.pallas_call(
+        back_kernel,
+        out_shape=(S((8, rows, 384), BF), S((8, shard, 384), BF), S((8, shard, 128), BF), S((8, 1, shard), F32)),
+        in_specs=[vmem_spec, vmem_spec, any_spec, any_spec, vmem_spec, any_spec, any_spec, vmem_spec],
+        out_specs=(any_spec,) * 4,
+        scratch_shapes=[
+            V((seq, 128), BF), V((seq, 128), BF), V((seq, 384), BF), V((seq, 128), F32), V((seq, width), BF), V((seq, width), BF),
+            V((8, seq), F32), V((seq, 128), F32), V((seq, 384), BF),
+            V((384, width), F32),
+        ]
+        + [V((2, 384, shard), BF)] * 6
+        + [
+            V((shard, 384), BF), V((shard, 128), BF), V((8, 1, width), F32), V((2, 1, width), F32), V((4, 1, shard), F32),
+            D((16,)), D((16,)), D((8,)), D((8,)), D((6,)), D((6,)), D((7,)), D((8,)), D((7,)), D((8,)), D((20,)), D((20,)), D((8,)),
+        ],
+        compiler_params=pltpu.CompilerParams(collective_id=3, has_side_effects=True, vmem_limit_bytes=56 * 1024 * 1024),
+        name="back_block",
+    )(gmix, gatt, qkv, mixed, lse_rows, normed, olow_full, cent)
+
+
+def on_device_split(
+    tokens,
+    norm_gain,
+    qkv_weight,
+    out_weight,
+    centroids,
+    expert_gain,
+    expert_in,
+    expert_out,
+    routes,
+    cotangent,
+):
+    rows, width = tokens.shape
+    experts = lax.axis_size("expert")
+    capacity = max(2, 3 * rows // (2 * experts))
+    slots = experts * capacity
+    shard = width // 4
+    around = [(s, (s + 2) % 4) for s in range(4)]
+    beside = [(s, s ^ 1) for s in range(4)]
+    w_near = jnp.stack([qkv_weight, lax.ppermute(qkv_weight, "dp", around)])
+    w_far = lax.ppermute(w_near, "dp", beside)
+    small = jnp.concatenate(
+        [norm_gain[None], expert_gain[0], jnp.zeros((5, shard), BF), centroids], axis=0
+    )
+    olow, normed_all, qkv, mixed, lse, wout_full, small_full = front_block(tokens, small, qkv_weight, out_weight)
+    gains = small_full[:, 1:3].transpose(1, 0, 2).reshape(2, width).astype(F32)
+    centroid_full = small_full[:, 8:16].transpose(1, 0, 2).reshape(8, width)
+    inputs = tokens.astype(F32)
+    residual = inputs + jnp.dot(olow, wout_full, preferred_element_type=F32)
+    route_ids = routes[:, 0]
+    chosen = (route_ids[:, None] == jnp.arange(experts, dtype=jnp.int32)[None, :]).astype(BF)
+    centroid_rows = jnp.dot(chosen, centroid_full, preferred_element_type=F32)
+    gate = jax.nn.sigmoid(jnp.sum(residual * centroid_rows, axis=-1))
+    before = jnp.tril(jnp.ones((rows, rows), BF), -1)
+    rank = jnp.sum(jnp.dot(before, chosen, preferred_element_type=F32) * chosen.astype(F32), axis=-1)
+    target = route_ids * capacity + rank.astype(jnp.int32)
+    place = (jnp.arange(slots, dtype=jnp.int32)[:, None] == target[None, :]).astype(BF)
+    grad_out = cotangent.astype(F32)
+    sent = jnp.concatenate([residual.astype(BF), (gate[:, None] * grad_out).astype(BF)], axis=1)
+    spread = jnp.dot(place, sent, preferred_element_type=F32).astype(BF)
+    returned, came_back, olow_full, gain_part, n_rows, h_rows, df_rows, du_rows = expert_block(
+        spread[:, :width].reshape(experts, capacity, width),
+        spread[:, width:].reshape(experts, capacity, width),
+        olow,
+        gains,
+        expert_in,
+        expert_out,
+    )
+    grad_expert_out = jnp.einsum("krf,krd->kfd", h_rows, df_rows, preferred_element_type=F32)[None]
+    grad_expert_in = jnp.einsum("krf,krd->kfd", du_rows, n_rows, preferred_element_type=F32)[None]
+    expert_gain_share = lax.psum_scatter(gain_part[None], "dp", scatter_dimension=2, tiled=True)
+    branch_tok = lax.dot_general(place, returned.reshape(slots, width), TN, preferred_element_type=F32)
+    block_out = (residual + gate[:, None] * branch_tok).astype(BF)
+    grad_logit = jnp.sum(grad_out * branch_tok, axis=-1) * gate * (1.0 - gate)
+    grad_centroid = jnp.dot(chosen.astype(F32).T, grad_logit[:, None] * residual, precision=HIGH)
+    back_rows = lax.dot_general(place, came_back.reshape(slots, width), TN, preferred_element_type=F32)
+    grad_resid = grad_out + grad_logit[:, None] * centroid_rows + back_rows
+    grad_attended = grad_resid.astype(BF)
+    grad_mixed = lax.dot_general(grad_attended, wout_full, NT, preferred_element_type=F32).astype(BF)
+    lse_rows = jnp.pad(lse[:, ::HEAD].T, ((0, 6), (0, 0)))
+    dq_land, gq_land, go_land, gc_land = back_block(
+        grad_mixed, grad_attended, qkv, mixed, lse_rows, normed_all,
+        olow_full.reshape(experts * rows, width), grad_centroid[:, None, :],
+    )
+    dqkv = dq_land.reshape(8, rows, 3, 128).transpose(1, 2, 0, 3).reshape(rows, 3 * width)
+    pieces = jnp.concatenate([w_near, w_far])
+    order = lax.axis_index("dp") ^ jnp.array([0, 2, 1, 3], jnp.int32)
+    grad_pieces = lax.dot_general(pieces, dqkv, (((2,), (1,)), ((), ())), preferred_element_type=F32)
+    grad_normed = jnp.take(grad_pieces, jnp.argsort(order), axis=0).reshape(width, rows).T
+    gain_full = small_full[:, 0].reshape(1, width).astype(F32)
+    unit, inverse, _ = normalize(inputs, gain_full)
+    grad_input, _ = norm_backward(grad_normed, unit, inverse, gain_full)
+    grad_tokens = grad_resid + grad_input
+    grad_qkv = gq_land.reshape(8, shard, 3, 128).transpose(1, 2, 0, 3).reshape(shard, 3 * width).astype(F32)
+    grad_out_weight = go_land.transpose(1, 0, 2).reshape(shard, width).astype(F32)
+    grad_norm_gain = jnp.sum(grad_qkv * qkv_weight.astype(F32), axis=1) / norm_gain.astype(F32)
+    return (
+        block_out,
+        grad_tokens,
+        grad_norm_gain,
+        grad_qkv,
+        grad_out_weight,
+        gc_land[:, 0],
+        expert_gain_share,
+        grad_expert_in,
+        grad_expert_out,
+    )
 
 
 def on_device(
@@ -411,6 +1301,7 @@
         P("expert", None, "dp", None),
         P("expert", None, "dp", None),
     )
+    split = mesh.shape["dp"] == 4 and mesh.shape["expert"] == 8
     return jax.shard_map(
-        on_device, mesh=mesh, in_specs=in_specs, out_specs=out_specs, check_vma=False
-    )
+        on_device_split if split else on_device, mesh=mesh, in_specs=in_specs, out_specs=out_specs, check_vma=False
+    )

time: 871 us -> 357 us (0.41)
  waiting for transfers between devices: 484 us -> 0.02 us
  Pallas kernels: 0 us -> 266 us
  blocking collectives: 138 us -> 0 us
  matrix products: 126 us -> 28.8 us
  other arithmetic: 49.5 us -> 14.2 us
  starting transfers between devices: 12.7 us -> 3.1 us
    pallas_call x0 -> x3, Pallas kernels: none -> 266 us  [the longest x1 116 us: expert_block(): pl.pallas_call(expert_kernel, out_shape=(S(zslots.shape, BF), S(zslots.sh...]
    all_gather x10 -> x0, waiting for transfers between devices: 210 us -> none  [the longest x4 74.6 us: spread_rows(): return lax.all_gather(rows_low, 'dp', axis=0, tiled=True)]
    reduce_scatter x7 -> x0, waiting for transfers between devices: 157 us -> none  [the longest x4 112 us: sum_rows(): lax.psum_scatter(term(jnp.int32(0), amount * lax.axis_size('dp')).astype(...]
    dot_general x27 -> x11, matrix products: 126 us -> 28.8 us  [the longest x1 7.75 us: on_device_split(): jnp.einsum('krf,krd->kfd', du_rows, n_rows, preferred_element_type=F32)]
    psum x1 -> x0, waiting for transfers between devices: 81.4 us -> none  [on_device(): lax.psum(qkv_share.astype(jnp.bfloat16), 'expert').astype(jnp.float32)]
    all_gather x5 -> x0, blocking collectives: 68.9 us -> none  [the longest x1 26.3 us: on_device(): lax.all_gather(delta_rows.astype(jnp.bfloat16), 'expert', axis=0, tiled=T...]
    all_to_all x2 -> x0, blocking collectives: 40.9 us -> none  [the longest x1 25.4 us: on_device(): lax.all_to_all(grad_state.astype(jnp.bfloat16).reshape(experts, capacity,...]
    psum x1 -> x0, blocking collectives: 22.6 us -> none  [on_device(): lax.psum(gain_share.astype(jnp.bfloat16), 'expert').astype(jnp.float32)]
  transfers between devices with their start and end apart: 21 -> 3, of which waited for: 18 -> 0; matrix products, arithmetic and copies ran while one was open for 15% -> 18% of each run, Pallas kernels for 0% -> 76%
where the time goes in v2:
time: 357 us; the launch traced here: 352 us
  Pallas kernels  266 us (75%)
  matrix products  28.8 us (8%)
  local copies, waits for them, and re-layouts  25.3 us (7%)
  between operations  14.3 us (4%)
  other arithmetic  14.2 us (4%)
    pallas_call x1, Pallas kernels, expert_block(): pl.pallas_call(expert_kernel, out_shape=(S(zslots.shape, BF), S(zslots.sh...  116 us
    pallas_call x1, Pallas kernels, back_block(): pl.pallas_call(back_kernel, out_shape=(S((8, rows, 384), BF), S((8, shard...  77.2 us
    pallas_call x1, Pallas kernels, front_block(): pl.pallas_call(front_kernel, out_shape=(S((rows, width), BF), S((seq, wid...  72.8 us
    unnamed x44, local copies, waits for them, and re-layouts  9.2 us
    dot_general x1, matrix products, on_device_split(): jnp.einsum('krf,krd->kfd', du_rows, n_rows, preferred_element_type=F32)  7.75 us
  transfers between devices with their start and end apart: 3, of which 0 were waited for; matrix products, arithmetic and copies ran while one was open for 18% of the time, Pallas kernels for 76%

profile of v2, /device:TPU:0, one launch (start us, length us, event | category | flops | bytes accessed | tf_op | source)
XLA Modules:
  0.0 352.0 jit_solution(16821857987237259798)
XLA Ops:
  7.2 3.1 collective-permute-start
  11.0 1.4 pad_maximum_fusion.1.small
  12.4 72.8 %front_block.1 = (bf16[128,1024]{1,0:T(8,128)(2,1)}, bf16[1024,1024]{1,0:T(8,128)(2,1)}, bf16[1024,384]{1,0:T(8,128)(2,1)}, f32[1024,128]{1,0:T(8,128)}, f32[102...) custom-call(bf16[128,1024]{1,0:T(8,128)(2,1)} %tok.1, ...), custom_call_target="tpu_custom_call" | custom-call | tf_op jit(solution)/shard_map/front_block/pallas_call | solution.py:348
  85.9 1.3 slice_convert_fusion.1
  88.2 2.2 fusion.44
  92.1 116.3 %expert_block.1 = (bf16[8,24,1024]{2,1,0:T(8,128)(2,1)}, bf16[8,24,1024]{2,1,0:T(8,128)(2,1)}, bf16[8,128,1024]{2,1,0:T(8,128)(2,1)}, f32[2,1024]{1,0:T(2,128)},...) custom-call(bf16[8,24,1024]{2,1,0:T(8,128)(2,1)} %bitcast.74, ...), custom_call_target="tpu_custom_call" | custom-call | tf_op jit(solution)/shard_map/expert_block/pallas_call | solution.py:634
  208.4 1.7 copy.65
  210.8 2.2 fusion.17
  215.8 3.2 convolution_convert_fusion.1.gmix
  219.0 3.4 pad_maximum_fusion
  222.6 1.6 copy.54
  225.6 77.2 %back_block.1 = (bf16[8,128,384]{2,1,0:T(8,128)(2,1)}, bf16[8,256,384]{2,1,0:T(8,128)(2,1)}, bf16[8,256,128]{2,1,0:T(8,128)(2,1)}, f32[8,1,256]{2,1,0:T(1,128)}) custom-call(bf16[128,1024]{1,0:T(8,128)(2,1)} %convolution_convert_fusion.1.gmix, bf16[128,1024]{1,0:T(8,128)(2,1)} %copy-done.3, bf16[1024,384]{1,0:T(8,128)(2,1)} %get-tuple-element.35.qkv_hbm, ...), custom_call_target="tpu_custom_call" | custom-call | tf_op jit(solution)/shard_map/back_block/pallas_call | solution.py:860
  302.9 3.1 copy.52
  305.9 2.2 copy.53
  308.9 2.0 multiply_reduce_fusion
  313.3 7.7 %convolution_bitcast_fusion.1 = f32[1,2,1024,1024]{3,2,1,0:T(8,128)} fusion(bf16[2,768,1024]{2,1,0:T(8,128)(2,1)} %get-tuple-element.45, bf16[2,768,1024]{2,1,0:T(8,128)(2,1)S(1)} %copy-done.16), kind=kOutput, calls=%fused_computation.8 | convolution fusion | flops 3221225472 | bytes 14680064 | tf_op jit(solution)/shard_map/krf,krd->kfd/dot_general | solution.py:929
  321.0 6.0 %convolution_bitcast_fusion = f32[1,2,1024,1024]{3,2,1,0:T(8,128)} fusion(bf16[2,768,1024]{2,1,0:T(8,128)(2,1)S(1)} %copy-done.14, bf16[2,768,1024]{2,1,0:T(8,128)(2,1)S(1)} %copy-done.15), kind=kOutput, calls=%fused_computation.7 | convolution fusion | flops 3221225472 | bytes 14680064 | tf_op jit(solution)/shard_map/krf,krd->kfd/dot_general | solution.py:928
  327.0 2.3 copy.48
  329.3 2.1 copy.49
  331.5 2.4 copy.58
  333.9 1.7 copy.55
  335.6 1.3 copy.59
  337.5 1.6 copy.66
  339.1 3.8 %fusion = f32[4,256,128]{2,1,0:T(8,128)S(1)} fusion(bf16[128,3072,1]{0,1,2:T(8,128)(2,1)} %bitcast.75, bf16[2,256,3072]{2,1,0:T(8,128)(2,1)} %collective-permute-done.1, bf16[1,256,3072]{2,1,0:T(8,128)(2,1)} %bitcast.11, bf16[1,256,3072]{2,1,0:T(8,128)(2,1)S(1)} %bitcast.66), kind=kOutput, calls=%fused_computation.1 | convolution fusion | flops 811597824 | bytes 7602176 | tf_op jit(solution)/shard_map/dot_general | solution.py:947
  (85 shorter events, 15.2 us)
Async XLA Ops:
  7.2 81.0 %copy-start.2 = (bf16[128,1024]{1,0:T(8,128)(2,1)S(1)}, bf16[128,1024]{1,0:T(8,128)(2,1)}, u32[]{:S(2)}) copy-start(bf16[128,1024]{1,0:T(8,128)(2,1)} %tok.1) | copy-start | bytes 786436
  7.2 330.3 %reduce-scatter.4.cloned.1.call-start = ((), (), s32[]{:S(2)}) async-start(), calls=%async_computation.1 | async-start | bytes 655360
  7.2 211.8 %collective-permute-start = (bf16[256,3072]{1,0:T(8,128)(2,1)}, bf16[256,3072]{1,0:T(8,128)(2,1)}, u32[]{:S(2)}, u32[]{:S(2)}) collective-permute-start(bf16[256,3072]{1,0:T(8,128)(2,1)} %wqkv.1), channel_id=1, source_target_pairs={{0,16},{8,24},{16,0},{24,8},{1,17},{9,25},{17,1},{25,9},{2,18},{10... | collective-permute-start | bytes 4718600 | tf_op jit(solution)/shard_map/ppermute | solution.py:899
  12.4 78.1 %copy-start.11 = (s32[128,1]{0,1:T(1,128)S(1)}, s32[128,1]{0,1:T(1,128)}, u32[]{:S(2)}) copy-start(s32[128,1]{0,1:T(1,128)} %param.19) | copy-start | bytes 1540
  12.4 78.3 %copy-start.4 = (bf16[128,1024]{1,0:T(8,128)(2,1)S(1)}, bf16[128,1024]{1,0:T(8,128)(2,1)}, u32[]{:S(2)}) copy-start(bf16[128,1024]{1,0:T(8,128)(2,1)} %param.20) | copy-start | bytes 786436
  90.4 1.7 copy-start.12
  92.1 118.2 %copy-start.17 = (s32[4]{0:T(128)S(1)}, s32[4]{0:T(128)}, u32[]{:S(2)}) copy-start(s32[4]{0:T(128)} %constant.48.clone) | copy-start | bytes 52
  208.4 6.3 %copy-start.8 = (bf16[8,24,1024]{2,1,0:T(8,128)(2,1)S(1)}, bf16[8,24,1024]{2,1,0:T(8,128)(2,1)}, u32[]{:S(2)}) copy-start(bf16[8,24,1024]{2,1,0:T(8,128)(2,1)} %get-tuple-element.33) | copy-start | bytes 1179652
  210.8 8.2 %copy-start = (bf16[256,3072]{1,0:T(8,128)(2,1)S(1)}, bf16[256,3072]{1,0:T(8,128)(2,1)}, u32[]{:S(2)}) copy-start(bf16[256,3072]{1,0:T(8,128)(2,1)} %wqkv.1) | copy-start | bytes 4718596
  215.8 6.6 %copy-start.3 = (bf16[128,1024]{1,0:T(8,128)(2,1)}, bf16[128,1024]{1,0:T(8,128)(2,1)S(1)}, u32[]{:S(2)}) copy-start(bf16[128,1024]{1,0:T(8,128)(2,1)S(1)} %get-tuple-element.83.gatt) | copy-start | bytes 786436
  222.4 1.8 copy-start.7
  222.4 2.0 copy-start.9
  222.4 116.7 %collective-permute-start.1 = (bf16[2,256,3072]{2,1,0:T(8,128)(2,1)}, bf16[2,256,3072]{2,1,0:T(8,128)(2,1)}, u32[]{:S(2)}, u32[]{:S(2)}) collective-permute-start(bf16[2,256,3072]{2,1,0:T(8,128)(2,1)} %pad_maximum_fusion), channel_id=1, source_target_pairs={{0,8},{8,0},{16,24},{24,16},{1,9},{9,1},{17,25},{25,17},{2,10},{10... | collective-permute-start | bytes 9437192 | tf_op jit(solution)/shard_map/ppermute | solution.py:900
  305.9 2.2 copy-start.18
  308.1 2.8 copy-start.13
  308.9 3.3 copy-start.6
  308.9 4.4 %copy-start.16 = (bf16[2,768,1024]{2,1,0:T(8,128)(2,1)S(1)}, bf16[2,768,1024]{2,1,0:T(8,128)(2,1)}, u32[]{:S(2)}) copy-start(bf16[2,768,1024]{2,1,0:T(8,128)(2,1)} %get-tuple-element.46) | copy-start | bytes 9437188
  313.3 7.8 %copy-start.14 = (bf16[2,768,1024]{2,1,0:T(8,128)(2,1)S(1)}, bf16[2,768,1024]{2,1,0:T(8,128)(2,1)}, u32[]{:S(2)}) copy-start(bf16[2,768,1024]{2,1,0:T(8,128)(2,1)} %get-tuple-element.47) | copy-start | bytes 9437188
  313.3 7.8 %copy-start.15 = (bf16[2,768,1024]{2,1,0:T(8,128)(2,1)S(1)}, bf16[2,768,1024]{2,1,0:T(8,128)(2,1)}, u32[]{:S(2)}) copy-start(bf16[2,768,1024]{2,1,0:T(8,128)(2,1)} %get-tuple-element.48) | copy-start | bytes 9437188
  333.9 3.0 copy-start.10
  333.9 5.2 %copy-start.1 = (bf16[256,3072]{1,0:T(8,128)(2,1)S(1)}, bf16[256,3072]{1,0:T(8,128)(2,1)}, u32[]{:S(2)}) copy-start(bf16[256,3072]{1,0:T(8,128)(2,1)} %wqkv.1) | copy-start | bytes 4718596
  342.9 1.2 copy-start.5
Sparse Core Ops, SparseCore 0:
  210.3 26.4 reduce-scatter.3

commit v3 on v2

--- a/solution.py
+++ b/solution.py
@@ -128,23 +128,111 @@
     )
 
 
-def spread_plan(own_src, slots, send, recv):
-    me, z, x, beside, zs = expert_peers()
-
-    def first(i):
-        if i == 0:
-            return push(own_src, slots.at[me], send.at[0], recv.at[me], {"expert": beside})
-        return push(own_src, slots.at[me], send.at[i], recv.at[me], {"expert": 2 * zs[i - 1] + x})
-
-    def arrival(zz, xx):
-        s = 2 * zz + xx
-        return push(slots.at[s], slots.at[s], send.at[0], recv.at[s], {"expert": beside})
-
-    def passed(i):
-        s = 2 * zs[i] + x
-        return push(slots.at[s], slots.at[s], send.at[4 + i], recv.at[s], {"expert": beside})
-
-    return first, arrival, passed
+class Spread:
+    def __init__(self, own_src, slots, send, recv, chunks):
+        self.me, self.z, self.x, self.beside, self.zs = expert_peers()
+        self.own_src, self.slots, self.send, self.recv, self.chunks = own_src, slots, send, recv, chunks
+        self.part = own_src.shape[0] // chunks
+
+    def rows(self, c):
+        return pl.ds(c * self.part, self.part)
+
+    def own(self, way, c):
+        peer = self.beside if way == 0 else 2 * (self.z + (1 if way == 1 else -1)) + self.x
+        return push(
+            self.own_src.at[self.rows(c)], self.slots.at[self.me, self.rows(c)],
+            self.send.at[way * self.chunks + c], self.recv.at[self.me * self.chunks + c], {"expert": peer},
+        )
+
+    def slot(self, s, c, base, peer):
+        block = self.slots.at[s, self.rows(c)]
+        return push(block, block, self.send.at[base * self.chunks + c], self.recv.at[s * self.chunks + c], {"expert": peer})
+
+    def own_all(self, act):
+        for way in range(3):
+            for c in range(self.chunks):
+                if way == 0:
+                    act(self.own(way, c))
+                else:
+                    @pl.when(self.z < 3 if way == 1 else self.z > 0)
+                    def _():
+                        act(self.own(way, c))
+
+    def start(self):
+        self.own_all(lambda cp: cp.start())
+
+    def each(self, d, act):
+        for sign in (-1, 1):
+            zz = self.z + sign * d
+            onward = self.z - sign
+
+            @pl.when(jnp.logical_and(zz >= 0, zz <= 3))
+            def _():
+                s = 2 * zz + self.x
+                for c in range(self.chunks):
+                    act(s, zz, onward, c)
+
+    def step(self, d):
+        def act(s, zz, onward, c):
+            self.slot(s, c, 0, self.beside).wait_recv()
+
+            @pl.when(jnp.logical_and(onward >= 0, onward <= 3))
+            def _():
+                self.slot(s, c, 7 + zz, 2 * onward + self.x).start()
+
+            self.slot(s, c, 3 + zz, self.beside).start()
+
+        self.each(d, act)
+
+    def wait_beside(self, zz):
+        for c in range(self.chunks):
+            self.slot(2 * zz + 1 - self.x, c, 0, self.beside).wait_recv()
+
+    def drain(self):
+        self.own_all(lambda cp: cp.wait_send())
+
+        def act(s, zz, onward, c):
+            @pl.when(jnp.logical_and(onward >= 0, onward <= 3))
+            def _():
+                self.slot(s, c, 7 + zz, 2 * onward + self.x).wait_send()
+
+            self.slot(s, c, 3 + zz, self.beside).wait_send()
+
+        for d in (1, 2, 3):
+            self.each(d, act)
+
+
+class Weights:
+    def __init__(self, src, first, rows, full, send, recv, copy):
+        self.j, self.sibling, self.across, self.diagonal = dp_peers()
+        self.src, self.full, self.send, self.recv = src.at[pl.ds(first, rows)], full, send, recv
+        self.keep = pltpu.make_async_copy(self.src, full.at[self.j], copy)
+
+    def copy(self, kind):
+        if kind == 2:
+            block = self.full.at[self.across]
+            return push(block, block, self.send.at[2], self.recv.at[self.across], {"dp": self.sibling})
+        peer = self.sibling if kind == 0 else self.across
+        return push(self.src, self.full.at[self.j], self.send.at[kind], self.recv.at[self.j], {"dp": peer})
+
+    def start(self):
+        self.copy(1).start()
+        self.copy(0).start()
+        self.keep.start()
+
+    def arrival(self, s):
+        return push(self.src, self.full.at[s], self.send.at[0], self.recv.at[s], {"dp": self.sibling})
+
+    def relay(self):
+        self.arrival(self.across).wait_recv()
+        self.copy(2).start()
+
+    def drain(self):
+        self.arrival(self.sibling).wait_recv()
+        self.arrival(self.diagonal).wait_recv()
+        for kind in range(3):
+            self.copy(kind).wait_send()
+        self.keep.wait()
 
 
 def lane_masks(rows):
@@ -154,9 +242,9 @@
 
 def front_kernel(
     tok, small, wqkv, wout,
-    olow, normed_out, qkv_out, mixed_out, lse_out, wout_full, small_full,
+    olow, normed_out, qkv_out, mixed_out, lse_out, wout_full, small_full, wfirst,
     held, wblk, normed, qkv, mixed, lse, mixed_low, gain, bounce, smalls,
-    tok_send, tok_recv, w_send, w_recv, o_send, o_recv, copy_sem,
+    tok_send, tok_recv, w_send, w_recv, o_send, o_recv, copy_sem, q_send, q_recv,
 ):
     j, sibling, across, diagonal = dp_peers()
     e, z, x, beside, zs = expert_peers()
@@ -185,9 +273,9 @@
     smalls[j] = small[...]
     greet([{"expert": p} for p in others(8, e)] + [{"dp": p} for p in (sibling, across, diagonal)])
 
-    first, arrival, passed = spread_plan(tok, held, tok_send, tok_recv)
-    for i in (1, 2, 3, 0):
-        first(i).start()
+    toks = Spread(tok, held, tok_send, tok_recv, 2)
+    toks.start()
+    later = Weights(wqkv, 0, shard // 2, wfirst, q_send, q_recv, copy_sem.at[7])
     for cp in own_w:
         cp.wait()
 
@@ -223,6 +311,7 @@
     w_copy(0).start()
     out_copy(1).start()
     out_copy(0).start()
+    later.start()
     own_out.wait()
     keep_out = pltpu.make_async_copy(bounce, wout_full.at[mine(j)], copy_sem.at[4])
     keep_out.start()
@@ -250,20 +339,18 @@
         qkv[at, :] = jnp.dot(normed[at, :], wblk[...], preferred_element_type=F32).astype(BF)
 
     own_tok.wait()
-    arrival(z, 1 - x).wait_recv()
+    toks.step(1)
+    toks.wait_beside(z)
     project(z)
-    for i in range(2):
-        arrival(zs[i], x).wait_recv()
-        passed(i).start()
-    arrival(zs[0], 1 - x).wait_recv()
+    toks.step(2)
+    toks.wait_beside(zs[0])
     project(zs[0])
+    toks.step(3)
     out_arrival(across).wait_recv()
     out_copy(2).start()
-    arrival(zs[2], x).wait_recv()
-    passed(2).start()
-    arrival(zs[1], 1 - x).wait_recv()
+    toks.wait_beside(zs[1])
     project(zs[1])
-    arrival(zs[2], 1 - x).wait_recv()
+    toks.wait_beside(zs[2])
     project(zs[2])
     stores = [
         pltpu.make_async_copy(normed, normed_out, copy_sem.at[0]),
@@ -322,12 +409,12 @@
         @pl.when(dest == e)
         def _():
             o_own(dest).wait()
+    later.relay()
     for s in (sibling, diagonal):
         out_arrival(s).wait_recv()
-    for i in range(4):
-        first(i).wait_send()
+    toks.drain()
+    later.drain()
     for i in range(3):
-        passed(i).wait_send()
         w_copy(i).wait_send()
         s_copy(i).wait_send()
         out_copy(i).wait_send()
@@ -349,15 +436,15 @@
         front_kernel,
         out_shape=(
             S((rows, width), BF), S((seq, width), BF), S((seq, 384), BF), S((seq, 128), F32), S((seq, 128), F32),
-            S((width, width), BF), S((4,) + small.shape, BF),
+            S((width, width), BF), S((4,) + small.shape, BF), S((4, shard // 2, 3 * width), BF),
         ),
         in_specs=[any_spec, vmem_spec, any_spec, any_spec],
-        out_specs=(any_spec,) * 7,
+        out_specs=(any_spec,) * 8,
         scratch_shapes=[
             V((8, rows, width), BF), V((width, 384), BF), V((seq, width), BF), V((seq, 384), BF),
             V((seq, 128), F32), V((seq, 128), F32), V((seq, 128), BF), V((1, width), F32), V((shard, width), BF),
             V((4,) + small.shape, BF),
-            D((7,)), D((8,)), D((9,)), D((12,)), D((8,)), D((8,)), D((8,)),
+            D((22,)), D((16,)), D((9,)), D((12,)), D((8,)), D((8,)), D((8,)), D((3,)), D((4,)),
         ],
         compiler_params=pltpu.CompilerParams(collective_id=2, has_side_effects=True, vmem_limit_bytes=56 * 1024 * 1024),
         name="front_block",
@@ -368,8 +455,8 @@
     zslots, dslots, olow, gain_ref, w1_hbm, w2_hbm,
     returned, came_back, olow_full, ggain_ref, n_out, h_out, df_out, du_out,
     w1, w2, x, hid, gpr, unit_s, inv_s, state, total, grad_in, own, far, f1, f3, ssum, rf1, rf3, rss,
-    zland, dland, bsend, gsend,
-    send_sem, recv_sem, a_send, a_recv, g_send, g_recv, copy_sem, own_sem,
+    zland, dland, bsend, gsend, ggain, gland,
+    send_sem, recv_sem, a_send, a_recv, g_send, g_recv, copy_sem, own_sem, e_send, e_recv,
 ):
     cap, width = zslots.shape[1:]
     half = 4 * cap
@@ -386,24 +473,50 @@
         cp = pltpu.make_async_copy(src, dst, copy_sem.at[i])
         cp.start()
         loads.append(cp)
-    own_z = pltpu.make_async_copy(zslots.at[e], zland.at[e], own_sem.at[0])
-    own_d = pltpu.make_async_copy(dslots.at[e], dland.at[e], own_sem.at[1])
-    own_z.start()
-    own_d.start()
-    greet([{"expert": p} for p in others(8, e)] + [{"dp": sibling}, {"dp": across}])
-
-    def swap(src, dst, which, dest):
-        return push(src.at[dest], dst.at[e], a_send.at[which * 8 + dest], a_recv.at[which * 8 + e], {"expert": dest})
-
-    def swap_arrival(src, dst, which, source):
-        return push(src.at[source], dst.at[source], a_send.at[which * 8 + source], a_recv.at[which * 8 + source], {"expert": source})
-
-    peers = others(8, e)
-    for dest in peers:
-        swap(zslots, zland, 0, dest).start()
-    for dest in peers:
-        swap(dslots, dland, 1, dest).start()
-    first, arrival, passed = spread_plan(olow, olow_full, g_send, g_recv)
+    zx = (zpos, zs[0], lax.rem(zpos + 2, 4), 3 - zpos)
+
+    def peer_at(q):
+        return 2 * zx[q // 2] + q % 2
+
+    def seat(q):
+        return 2 * (q // 2) + xpos
+
+    greet([{"expert": p} for p in others(8, e)] + [{"dp": p} for p in (sibling, across, diagonal)])
+
+    def swap(src, dst, which, q):
+        peer = peer_at(q)
+        if which < 2:
+            return push(src.at[peer], dst.at[seat(q)], a_send.at[which * 8 + q], a_recv.at[which * 8 + seat(q)], {"expert": peer})
+        return push(src.at[q], dst.at[e], a_send.at[which * 8 + q], a_recv.at[which * 8 + seat(q)], {"expert": peer})
+
+    def swap_arrival(src, dst, which, q):
+        peer = peer_at(q)
+        if which < 2:
+            return push(src.at[peer], dst.at[q], a_send.at[which * 8 + q], a_recv.at[which * 8 + q], {"expert": peer})
+        return push(src.at[q], dst.at[peer], a_send.at[which * 8 + q], a_recv.at[which * 8 + q], {"expert": peer})
+
+    def swap_own(src, dst, which):
+        if which < 2:
+            return pltpu.make_async_copy(src.at[e], dst.at[xpos], own_sem.at[which])
+        return pltpu.make_async_copy(src.at[xpos], dst.at[e], own_sem.at[which])
+
+    def for_places(h, act, mine):
+        for q in range(4 * h, 4 * h + 4):
+            if q >= 2:
+                act(q)
+            else:
+                @pl.when(xpos != q)
+                def _():
+                    act(q)
+
+                @pl.when(xpos == q)
+                def _():
+                    mine()
+
+    for which, (src, dst) in enumerate([(zslots, zland), (dslots, dland)]):
+        for h in (1, 0):
+            for_places(h, lambda q: swap(src, dst, which, q).start(), lambda: swap_own(src, dst, which).start())
+    olows = Spread(olow, olow_full, g_send, g_recv, 1)
     own_o = pltpu.make_async_copy(olow, olow_full.at[e], copy_sem.at[12])
     own_o.start()
 
@@ -474,28 +587,23 @@
                 own[h, :, cols] = res[:half]
                 f1[q, :, cols] = res[half:].astype(BF)
             else:
-                far[:, cols] = res[:half]
+                far[h, :, cols] = res[:half]
                 f3[q, :, cols] = res[half:].astype(BF)
+                remote(f3.at[q, :, cols], rf3.at[q, :, cols], 4, p, h, sibling).start()
             return c
 
         lax.fori_loop(0, tiles, down, 0)
         if pair == 0:
             copy_of(3, p, h).start()
-        else:
-            copy_of(4, p, h).start()
-            copy_of(4, p, h).wait_recv()
-            ssum[q] = (far[...] + rf3[q].astype(F32)).astype(BF)
-            copy_of(5, p, h).start()
+
+    def send_sum(p, h):
+        q = p * 2 + h
+        copy_of(4, p, h).wait_recv()
+        ssum[q] = (far[h] + rf3[q].astype(F32)).astype(BF)
+        copy_of(5, p, h).start()
 
     def give_back(buf, dst, which, h):
-        for dest in range(4 * h, 4 * h + 4):
-            @pl.when(dest != e)
-            def _():
-                swap(buf, dst, which, dest).start()
-
-            @pl.when(dest == e)
-            def _():
-                pltpu.make_async_copy(buf.at[dest], dst.at[dest], own_sem.at[which]).start()
+        for_places(h, lambda q: swap(buf, dst, which, q).start(), lambda: swap_own(buf, dst, which).start())
 
     def finish(p, h):
         k = layer_of[p]
@@ -517,9 +625,9 @@
             unit = unit_s[k, rs, :]
             part = jnp.sum(got * unit, axis=0, keepdims=True)
             if h == 0:
-                ggain_ref[pl.ds(k, 1), :] = part
+                ggain[pl.ds(k, 1), :] = part
             else:
-                ggain_ref[pl.ds(k, 1), :] = ggain_ref[pl.ds(k, 1), :] + part
+                ggain[pl.ds(k, 1), :] = ggain[pl.ds(k, 1), :] + part
             a = got * gain_ref[pl.ds(k, 1), :]
             back = inv_s[k, rs, :][:, :1] * (a - mean_last(a) - unit * mean_last(a * unit))
             state[rs, :] = state[rs, :] + back
@@ -539,50 +647,49 @@
         cp.start()
         stores.append(cp)
 
-    def landed(buf, src, own_copy, which, h, out):
-        for source in range(4 * h, 4 * h + 4):
-            @pl.when(source != e)
-            def _():
-                swap_arrival(src, buf, which, source).wait_recv()
-
-            @pl.when(source == e)
-            def _():
-                own_copy.wait()
-        for source in range(4 * h, 4 * h + 4):
-            out[pl.ds(source * cap, cap), :] = buf[source].astype(F32)
-
-    landed(zland, zslots, own_z, 0, 0, state)
+    def landed(src, buf, which, h, out):
+        for_places(h, lambda q: swap_arrival(src, buf, which, q).wait_recv(), lambda: swap_own(src, buf, which).wait())
+        for q in range(4 * h, 4 * h + 4):
+            out[pl.ds(q * cap, cap), :] = buf[q].astype(F32)
+
+    def gain_copy(i):
+        s = (sibling, across, diagonal)[i]
+        return push(ggain.at[:, pl.ds(pl.multiple_of(s * shard, shard), shard)], gland.at[j], e_send.at[i], e_recv.at[j], {"dp": s})
+
+    shard = width // 4
+    landed(zslots, zland, 0, 0, state)
     start_rows(0, 0)
-    landed(zland, zslots, own_z, 0, 1, state)
-    start_rows(0, 1)
     loads[0].wait()
     loads[1].wait()
+    copy_of(0, 0, 0).wait_recv()
+    compute(0, 0, 0)
+    landed(zslots, zland, 0, 1, state)
+    start_rows(0, 1)
     for p in range(4):
-        if p == 0:
-            copy_of(0, p, 0).wait_recv()
-            compute(p, 0, 0)
-            for i in (1, 2, 3, 0):
-                first(i).start()
         relay(p, 0)
         copy_of(2, p, 0).wait_recv()
         compute(p, 0, 1)
+        send_sum(p, 0)
+        if p == 0:
+            olows.start()
+        relay(p, 1)
         copy_of(0, p, 1).wait_recv()
         compute(p, 1, 0)
-        relay(p, 1)
         copy_of(2, p, 1).wait_recv()
         compute(p, 1, 1)
         if p == 1:
-            for i in range(3):
-                arrival(zs[i], xpos).wait_recv()
-                passed(i).start()
-            landed(dland, dslots, own_d, 1, 0, grad_in)
-            landed(dland, dslots, own_d, 1, 1, grad_in)
+            landed(dslots, dland, 1, 0, grad_in)
+            landed(dslots, dland, 1, 1, grad_in)
         finish(p, 0)
+        if p < 3:
+            start_rows(p + 1, 0)
+        send_sum(p, 1)
+        if p < 3:
+            olows.step(p + 1)
         if p == 0:
             loads[2].wait()
             loads[3].wait()
         if p < 3:
-            start_rows(p + 1, 0)
             copy_of(0, p + 1, 0).wait_recv()
             compute(p + 1, 0, 0)
         finish(p, 1)
@@ -595,28 +702,28 @@
         else:
             store(p * 2, x.at[p], df_out.at[k])
             store(p * 2 + 1, hid.at[2 + k], du_out.at[k])
+    for i in range(3):
+        gain_copy(i).start()
+    gland[j] = ggain[:, pl.ds(pl.multiple_of(j * shard, shard), shard)]
     own_o.wait()
-    for s in range(4):
-        arrival(s, 1 - xpos).wait_recv()
-    for i in range(4):
-        first(i).wait_send()
-    for i in range(3):
-        passed(i).wait_send()
+    for zz in range(4):
+        olows.wait_beside(zz)
+    olows.drain()
     for p in range(4):
         for h in range(2):
             for kind in range(6):
                 copy_of(kind, p, h).wait_send()
     for cp in stores:
         cp.wait()
-    for dest in peers:
-        swap(zslots, zland, 0, dest).wait_send()
-        swap(dslots, dland, 1, dest).wait_send()
-        swap(bsend, returned, 2, dest).wait_send()
-        swap(gsend, came_back, 3, dest).wait_send()
-        swap_arrival(bsend, returned, 2, dest).wait_recv()
-        swap_arrival(gsend, came_back, 3, dest).wait_recv()
-    pltpu.make_async_copy(bsend.at[0], returned.at[0], own_sem.at[2]).wait()
-    pltpu.make_async_copy(gsend.at[0], came_back.at[0], own_sem.at[3]).wait()
+    for i in range(3):
+        push(ggain.at[:, pl.ds(0, shard)], gland.at[(sibling, across, diagonal)[i]], e_send.at[0], e_recv.at[(sibling, across, diagonal)[i]], {"dp": sibling}).wait_recv()
+        gain_copy(i).wait_send()
+    ggain_ref[...] = jnp.sum(gland[...], axis=0)
+    for h in range(2):
+        for which, (src, dst) in enumerate([(zslots, zland), (dslots, dland), (bsend, returned), (gsend, came_back)]):
+            for_places(h, lambda q: swap(src, dst, which, q).wait_send(), lambda: None)
+            if which >= 2:
+                for_places(h, lambda q: swap_arrival(src, dst, which, q).wait_recv(), lambda: swap_own(src, dst, which).wait())
 
 
 def expert_block(zslots, dslots, olow, gains, expert_in, expert_out):
@@ -634,7 +741,7 @@
     return pl.pallas_call(
         expert_kernel,
         out_shape=(
-            S(zslots.shape, BF), S(zslots.shape, BF), S((8,) + olow.shape, BF), S((2, width), F32),
+            S(zslots.shape, BF), S(zslots.shape, BF), S((8,) + olow.shape, BF), S((2, width // 4), F32),
             big, big, big, big,
         ),
         in_specs=[any_spec] * 3 + [vmem_spec] + [any_spec] * 2,
@@ -643,11 +750,12 @@
             V((2, hidden, width), BF), V((2, hidden, width), BF),
             V((4, everything, width), BF), V((4, everything, hidden), BF), V((2, everything, hidden), F32),
             V((2, rows, width), F32), V((2, rows, 128), F32), V((rows, width), F32), V((rows, width), F32),
-            V((rows, width), F32), V((2, half, width), F32), V((half, width), F32),
+            V((rows, width), F32), V((2, half, width), F32), V((2, half, width), F32),
         ]
         + [V((8, half, width), BF)] * 6
         + [V(zslots.shape, BF)] * 4
-        + [D((48,)), D((48,)), D((32,)), D((32,)), D((7,)), D((8,)), D((13,)), D((4,))],
+        + [V((2, width), F32), V((4, 2, width // 4), F32)]
+        + [D((48,)), D((48,)), D((32,)), D((32,)), D((11,)), D((8,)), D((13,)), D((4,)), D((3,)), D((4,))],
         compiler_params=pltpu.CompilerParams(
             collective_id=1, has_side_effects=True, vmem_limit_bytes=60 * 1024 * 1024
         ),
@@ -656,11 +764,11 @@
 
 
 def back_kernel(
-    gmix, gatt, qkv_hbm, mixed_hbm, lse_rows, normed_hbm, olow_hbm, cent,
-    dq_land, gq_land, go_land, gc_land,
+    gmix, gatt, qkv_hbm, mixed_hbm, lse_rows, normed_hbm, olow_hbm, cent, wqkv,
+    dq_land, gq_land, go_land, gc_land, wsecond,
     dom, dam, qkv, mixed, normed, olow, delta, dq_acc, dqkv,
     part, f1, f3, ssum, rf1, rf3, rss, gq_own, go_own, cland, csum, cdp,
-    h_send, h_recv, d_send, d_recv, p_send, p_recv, gq_send, gq_recv, go_send, go_recv, c_send, c_recv, copy_sem,
+    h_send, h_recv, d_send, d_recv, p_send, p_recv, gq_send, gq_recv, go_send, go_recv, c_send, c_recv, copy_sem, q_send, q_recv,
 ):
     j, sibling, across, diagonal = dp_peers()
     e, zpos, xpos, beside, zs = expert_peers()
@@ -695,6 +803,8 @@
         head_copy(gatt, dam, 1, dest).start()
     for dest in peers:
         push(cent.at[dest], cland.at[e], c_send.at[dest], c_recv.at[e], {"expert": dest}).start()
+    later = Weights(wqkv, shard // 2, shard // 2, wsecond, q_send, q_recv, copy_sem.at[8])
+    later.start()
     dom[rows_of(e), :] = gmix[:, cols_of(e)]
     dam[rows_of(e), :] = gatt[:, cols_of(e)]
     cland[e] = cent[e]
@@ -791,9 +901,8 @@
             dp_sum_start(part, lanes, 0)
         if b == 1:
             go_own[...] = dp_sum_end(part, lanes, 0).T.astype(BF)
-            go_first, go_arrival, go_passed = spread_plan(go_own, go_land, go_send, go_recv)
-            for i in (1, 2, 3, 0):
-                go_first(i).start()
+            gos = Spread(go_own, go_land, go_send, go_recv, 1)
+            gos.start()
             own_go = pltpu.make_async_copy(go_own, go_land.at[e], copy_sem.at[5])
             own_go.start()
             for s in (sibling, across, diagonal):
@@ -806,21 +915,24 @@
     loads[3].wait()
     part[...] = lax.dot_general(dqkv[...], normed[...], TN, preferred_element_type=F32)
     dp_sum_start(part, 3 * lanes, 1)
-    for i in range(3):
-        go_arrival(zs[i], xpos).wait_recv()
-        go_passed(i).start()
+    gos.step(1)
     gq_own[...] = dp_sum_end(part, 3 * lanes, 1).T.astype(BF)
-    gq_first, gq_arrival, gq_passed = spread_plan(gq_own, gq_land, gq_send, gq_recv)
-    for i in (1, 2, 3, 0):
-        gq_first(i).start()
+    gqs = Spread(gq_own, gq_land, gq_send, gq_recv, 2)
+    gqs.start()
     own_gq = pltpu.make_async_copy(gq_own, gq_land.at[e], copy_sem.at[7])
     own_gq.start()
-    for i in range(3):
-        gq_arrival(zs[i], xpos).wait_recv()
-        gq_passed(i).start()
-    for s in range(4):
-        go_arrival(s, 1 - xpos).wait_recv()
-        gq_arrival(s, 1 - xpos).wait_recv()
+    gos.step(2)
+    later.relay()
+    gqs.step(1)
+    gos.step(3)
+    gqs.step(2)
+    gqs.step(3)
+    for zz in range(4):
+        gos.wait_beside(zz)
+        gqs.wait_beside(zz)
+    gos.drain()
+    gqs.drain()
+    later.drain()
     for source in range(8):
         @pl.when(source != e)
         def _():
@@ -839,16 +951,11 @@
         c_copy(i).wait_send()
         dp_copy(i, lanes, 0).wait_send()
         dp_copy(i, 3 * lanes, 1).wait_send()
-        go_passed(i).wait_send()
-        gq_passed(i).wait_send()
-    for i in range(4):
-        go_first(i).wait_send()
-        gq_first(i).wait_send()
     for cp in (own_go, own_gc, own_gq):
         cp.wait()
 
 
-def back_block(gmix, gatt, qkv, mixed, lse_rows, normed, olow_full, cent):
+def back_block(gmix, gatt, qkv, mixed, lse_rows, normed, olow_full, cent, qkv_weight):
     rows, width = gmix.shape
     seq = 8 * rows
     shard = width // 4
@@ -859,9 +966,12 @@
     D = pltpu.SemaphoreType.DMA
     return pl.pallas_call(
         back_kernel,
-        out_shape=(S((8, rows, 384), BF), S((8, shard, 384), BF), S((8, shard, 128), BF), S((8, 1, shard), F32)),
-        in_specs=[vmem_spec, vmem_spec, any_spec, any_spec, vmem_spec, any_spec, any_spec, vmem_spec],
-        out_specs=(any_spec,) * 4,
+        out_shape=(
+            S((8, rows, 384), BF), S((8, shard, 384), BF), S((8, shard, 128), BF), S((8, 1, shard), F32),
+            S((4, shard // 2, 3 * width), BF),
+        ),
+        in_specs=[vmem_spec, vmem_spec, any_spec, any_spec, vmem_spec, any_spec, any_spec, vmem_spec, any_spec],
+        out_specs=(any_spec,) * 5,
         scratch_shapes=[
             V((seq, 128), BF), V((seq, 128), BF), V((seq, 384), BF), V((seq, 128), F32), V((seq, width), BF), V((seq, width), BF),
             V((8, seq), F32), V((seq, 128), F32), V((seq, 384), BF),
@@ -870,11 +980,70 @@
         + [V((2, 384, shard), BF)] * 6
         + [
             V((shard, 384), BF), V((shard, 128), BF), V((8, 1, width), F32), V((2, 1, width), F32), V((4, 1, shard), F32),
-            D((16,)), D((16,)), D((8,)), D((8,)), D((6,)), D((6,)), D((7,)), D((8,)), D((7,)), D((8,)), D((20,)), D((20,)), D((8,)),
+            D((16,)), D((16,)), D((8,)), D((8,)), D((6,)), D((6,)), D((22,)), D((16,)), D((11,)), D((8,)), D((20,)), D((20,)), D((9,)), D((3,)), D((4,)),
         ],
         compiler_params=pltpu.CompilerParams(collective_id=3, has_side_effects=True, vmem_limit_bytes=56 * 1024 * 1024),
         name="back_block",
-    )(gmix, gatt, qkv, mixed, lse_rows, normed, olow_full, cent)
+    )(gmix, gatt, qkv, mixed, lse_rows, normed, olow_full, cent, qkv_weight)
+
+
+def final_kernel(
+    dq_land, wfirst, wsecond, tok, gain_col, gres, gq_land, go_land, wqkv,
+    gtok, gqkv, gout, ggain,
+    dqkv, dnorm, small_sum,
+):
+    rows, width = tok.shape
+    shard = wqkv.shape[0]
+    half = shard // 2
+    for s in range(8):
+        for i in range(3):
+            at = pl.ds(i * width + s * 128, 128)
+            dqkv[:, at] = dq_land[s, :, pl.ds(i * 128, 128)]
+            gqkv[:, at] = gq_land[s, :, pl.ds(i * 128, 128)].astype(F32)
+        gout[:, pl.ds(s * 128, 128)] = go_land[s].astype(F32)
+    for s in range(4):
+        for side, w in enumerate((wfirst, wsecond)):
+            dnorm[:, pl.ds(s * shard + side * half, half)] = lax.dot_general(dqkv[...], w[s], NT, preferred_element_type=F32)
+    gain = jnp.concatenate([gain_col[s : s + 1, :] for s in range(4)], axis=1)
+
+    def norm_rows(t, c):
+        at = pl.ds(pl.multiple_of(t * 32, 32), 32)
+        v = tok[at, :].astype(F32)
+        center = v - mean_last(v)
+        inverse = lax.rsqrt(mean_last(center * center) + EPS)
+        unit = center * inverse
+        a = dnorm[at, :] * gain
+        gtok[at, :] = gres[at, :] + inverse * (a - mean_last(a) - unit * mean_last(a * unit))
+        return c
+
+    lax.fori_loop(0, rows // 32, norm_rows, 0)
+    small_sum[...] = jnp.zeros_like(small_sum)
+
+    def add(t, c):
+        at = pl.ds(pl.multiple_of(t * 256, 256), 256)
+        prod = gqkv[:, at] * wqkv[:, at].astype(F32)
+        small_sum[...] += prod[:, :128] + prod[:, 128:]
+        return c
+
+    lax.fori_loop(0, 3 * width // 256, add, 0)
+    ggain[...] = lax.dot_general(jnp.ones((8, 128), F32), small_sum[...], NT, precision=HIGH, preferred_element_type=F32)
+
+
+def final_block(dq_land, wfirst, wsecond, tokens, gain_col, grad_resid, gq_land, go_land, qkv_weight):
+    rows, width = tokens.shape
+    shard = width // 4
+    vmem_spec = pl.BlockSpec(memory_space=pltpu.VMEM)
+    S = jax.ShapeDtypeStruct
+    V = pltpu.VMEM
+    return pl.pallas_call(
+        final_kernel,
+        out_shape=(S((rows, width), F32), S((shard, 3 * width), F32), S((shard, width), F32), S((8, shard), F32)),
+        in_specs=[vmem_spec] * 9,
+        out_specs=(vmem_spec,) * 4,
+        scratch_shapes=[V((rows, 3 * width), BF), V((rows, width), F32), V((shard, 128), F32)],
+        compiler_params=pltpu.CompilerParams(vmem_limit_bytes=48 * 1024 * 1024),
+        name="final_block",
+    )(dq_land, wfirst, wsecond, tokens, gain_col, grad_resid, gq_land, go_land, qkv_weight)
 
 
 def on_device_split(
@@ -894,14 +1063,10 @@
     capacity = max(2, 3 * rows // (2 * experts))
     slots = experts * capacity
     shard = width // 4
-    around = [(s, (s + 2) % 4) for s in range(4)]
-    beside = [(s, s ^ 1) for s in range(4)]
-    w_near = jnp.stack([qkv_weight, lax.ppermute(qkv_weight, "dp", around)])
-    w_far = lax.ppermute(w_near, "dp", beside)
     small = jnp.concatenate(
         [norm_gain[None], expert_gain[0], jnp.zeros((5, shard), BF), centroids], axis=0
     )
-    olow, normed_all, qkv, mixed, lse, wout_full, small_full = front_block(tokens, small, qkv_weight, out_weight)
+    olow, normed_all, qkv, mixed, lse, wout_full, small_full, wfirst = front_block(tokens, small, qkv_weight, out_weight)
     gains = small_full[:, 1:3].transpose(1, 0, 2).reshape(2, width).astype(F32)
     centroid_full = small_full[:, 8:16].transpose(1, 0, 2).reshape(8, width)
     inputs = tokens.astype(F32)
@@ -927,7 +1092,6 @@
     )
     grad_expert_out = jnp.einsum("krf,krd->kfd", h_rows, df_rows, preferred_element_type=F32)[None]
     grad_expert_in = jnp.einsum("krf,krd->kfd", du_rows, n_rows, preferred_element_type=F32)[None]
-    expert_gain_share = lax.psum_scatter(gain_part[None], "dp", scatter_dimension=2, tiled=True)
     branch_tok = lax.dot_general(place, returned.reshape(slots, width), TN, preferred_element_type=F32)
     block_out = (residual + gate[:, None] * branch_tok).astype(BF)
     grad_logit = jnp.sum(grad_out * branch_tok, axis=-1) * gate * (1.0 - gate)
@@ -937,22 +1101,15 @@
     grad_attended = grad_resid.astype(BF)
     grad_mixed = lax.dot_general(grad_attended, wout_full, NT, preferred_element_type=F32).astype(BF)
     lse_rows = jnp.pad(lse[:, ::HEAD].T, ((0, 6), (0, 0)))
-    dq_land, gq_land, go_land, gc_land = back_block(
+    dq_land, gq_land, go_land, gc_land, wsecond = back_block(
         grad_mixed, grad_attended, qkv, mixed, lse_rows, normed_all,
-        olow_full.reshape(experts * rows, width), grad_centroid[:, None, :],
-    )
-    dqkv = dq_land.reshape(8, rows, 3, 128).transpose(1, 2, 0, 3).reshape(rows, 3 * width)
-    pieces = jnp.concatenate([w_near, w_far])
-    order = lax.axis_index("dp") ^ jnp.array([0, 2, 1, 3], jnp.int32)
-    grad_pieces = lax.dot_general(pieces, dqkv, (((2,), (1,)), ((), ())), preferred_element_type=F32)
-    grad_normed = jnp.take(grad_pieces, jnp.argsort(order), axis=0).reshape(width, rows).T
-    gain_full = small_full[:, 0].reshape(1, width).astype(F32)
-    unit, inverse, _ = normalize(inputs, gain_full)
-    grad_input, _ = norm_backward(grad_normed, unit, inverse, gain_full)
-    grad_tokens = grad_resid + grad_input
-    grad_qkv = gq_land.reshape(8, shard, 3, 128).transpose(1, 2, 0, 3).reshape(shard, 3 * width).astype(F32)
-    grad_out_weight = go_land.transpose(1, 0, 2).reshape(shard, width).astype(F32)
-    grad_norm_gain = jnp.sum(grad_qkv * qkv_weight.astype(F32), axis=1) / norm_gain.astype(F32)
+        olow_full.reshape(experts * rows, width), grad_centroid[:, None, :], qkv_weight,
+    )
+    gain_col = small_full[:, 0].astype(F32)
+    grad_tokens, grad_qkv, grad_out_weight, gain_sums = final_block(
+        dq_land, wfirst, wsecond, tokens, gain_col, grad_resid, gq_land, go_land, qkv_weight
+    )
+    grad_norm_gain = gain_sums[0] / norm_gain.astype(F32)
     return (
         block_out,
         grad_tokens,
@@ -960,7 +1117,7 @@
         grad_qkv,
         grad_out_weight,
         gc_land[:, 0],
-        expert_gain_share,
+        gain_part[None],
         grad_expert_in,
         grad_expert_out,
     )

time: 357 us -> 271 us (0.76); the launches traced: 352 us -> 270 us
  Pallas kernels: 266 us -> 233 us
  local copies, waits for them, and re-layouts: 25.3 us -> 10.5 us
  between operations: 14.3 us -> 0.82 us
  other arithmetic: 14.2 us -> 4.12 us
  matrix products: 28.8 us -> 21.5 us
    pallas_call x1, Pallas kernels: 72.8 us -> 47.9 us  [front_block(): pl.pallas_call(front_kernel, out_shape=(S((rows, width), BF), S((seq, wid...]
    pallas_call x0 -> x1, Pallas kernels: none -> 9.49 us  [final_block(): pl.pallas_call(final_kernel, out_shape=(S((rows, width), F32), S((shard,...]
    pallas_call x1, Pallas kernels: 77.2 us -> 67.9 us  [back_block(): pl.pallas_call(back_kernel, out_shape=(S((8, rows, 384), BF), S((8, shard...]
    pallas_call x1, Pallas kernels: 116 us -> 108 us  [expert_block(): pl.pallas_call(expert_kernel, out_shape=(S(zslots.shape, BF), S(zslots.sh...]
    convert_element_type x3 -> x0, local copies, waits for them, and re-layouts: 6.92 us -> none  [the longest x2 5.24 us: on_device_split(): gq_land.reshape(8, shard, 3, 128).transpose(1, 2, 0, 3)]
    unnamed x44 -> x34, local copies, waits for them, and re-layouts: 9.2 us -> 4.81 us
    dot_general x1 -> x0, matrix products: 3.83 us -> none  [on_device_split(): lax.dot_general(pieces, dqkv, (((2,), (1,)), ((), ())), preferred_element...]
  transfers between devices with their start and end apart: 3 -> 0, of which waited for: 0 -> 0; matrix products, arithmetic and copies ran while one was open for 18% -> 0% of each run, Pallas kernels for 76% -> 0%
where the time goes in v3:
time: 271 us; the launch traced here: 270 us
  Pallas kernels  233 us (86%)
  matrix products  21.5 us (8%)
  local copies, waits for them, and re-layouts  10.5 us (4%)
  other arithmetic  4.12 us (2%)
    pallas_call x1, Pallas kernels, expert_block(): pl.pallas_call(expert_kernel, out_shape=(S(zslots.shape, BF), S(zslots.sh...  108 us
    pallas_call x1, Pallas kernels, back_block(): pl.pallas_call(back_kernel, out_shape=(S((8, rows, 384), BF), S((8, shard...  67.9 us
    pallas_call x1, Pallas kernels, front_block(): pl.pallas_call(front_kernel, out_shape=(S((rows, width), BF), S((seq, wid...  47.9 us
    pallas_call x1, Pallas kernels, final_block(): pl.pallas_call(final_kernel, out_shape=(S((rows, width), F32), S((shard,...  9.49 us
    dot_general x1, matrix products, on_device_split(): jnp.einsum('krf,krd->kfd', du_rows, n_rows, preferred_element_type=F32)  5.81 us
    dot_general x1, matrix products, on_device_split(): jnp.einsum('krf,krd->kfd', h_rows, df_rows, preferred_element_type=F32)  5.78 us

profile of v3, /device:TPU:0, one launch (start us, length us, event | category | flops | bytes accessed | tf_op | source)
XLA Modules:
  0.0 270.4 jit_solution(15970413886221456306)
XLA Ops:
  0.7 0.9 fusion
  1.7 0.7 convert_add_fusion.1
  2.4 0.7 broadcast_in_dim.32
  3.0 1.4 pad_maximum_fusion.small
  4.4 47.9 %front_block.1 = (bf16[128,1024]{1,0:T(8,128)(2,1)}, bf16[1024,1024]{1,0:T(8,128)(2,1)}, bf16[1024,384]{1,0:T(8,128)(2,1)}, f32[1024,128]{1,0:T(8,128)}, f32[102...) custom-call(bf16[128,1024]{1,0:T(8,128)(2,1)} %tok.3, ...), custom_call_target="tpu_custom_call" | custom-call | tf_op jit(solution)/shard_map/front_block/pallas_call | solution.py:435
  52.3 1.4 slice_convert_fusion
  53.6 0.7 slice.21
  54.4 0.8 copy.20
  55.2 0.9 fusion.19
  56.1 1.2 copy.19
  58.0 2.2 fusion.28
  60.7 0.9 fusion.27
  61.7 108.2 %expert_block.1 = (bf16[8,24,1024]{2,1,0:T(8,128)(2,1)}, bf16[8,24,1024]{2,1,0:T(8,128)(2,1)}, bf16[8,128,1024]{2,1,0:T(8,128)(2,1)}, f32[2,256]{1,0:T(2,128)}, ...) custom-call(bf16[8,24,1024]{2,1,0:T(8,128)(2,1)} %bitcast.42, ...), custom_call_target="tpu_custom_call" | custom-call | tf_op jit(solution)/shard_map/expert_block/pallas_call | solution.py:741
  169.9 2.2 fusion.2
  172.5 0.6 broadcast_in_dim.36.cent
  173.1 1.3 fusion.29
  174.4 1.5 convolution_convert_fusion.1.gmix
  176.0 67.9 %back_block.1 = (bf16[8,128,384]{2,1,0:T(8,128)(2,1)}, bf16[8,256,384]{2,1,0:T(8,128)(2,1)}, bf16[8,256,128]{2,1,0:T(8,128)(2,1)}, f32[8,1,256]{2,1,0:T(1,128)}, bf16[4,128,3072]{2,1,0:T(8,128)(2,1)}) custom-call(bf16[128,1024]{1,0:T(8,128)(2,1)} %convolution_convert_fusion.1.gmix, bf16[128,1024]{1,0:T(8,128)(2,1)} %copy-done.7, ...), custom_call_target="tpu_custom_call" | custom-call | tf_op jit(solution)/shard_map/back_block/pallas_call | solution.py:967
  243.9 1.4 copy-done.2
  245.3 1.1 copy-done.3
  246.5 1.0 copy-done.4
  247.5 9.5 %final_block.1 = (f32[128,1024]{1,0:T(8,128)}, f32[256,3072]{1,0:T(8,128)}, f32[256,1024]{1,0:T(8,128)}, f32[8,256]{1,0:T(8,128)S(1)}) custom-call(bf16[8,128,384]{2,1,0:T(8,128)(2,1)S(1)} %copy-done.3, bf16[4,128,3072]{2,1,0:T(8,128)(2,1)} %get-tuple-element.45.wfirst, bf16[4,128,3072]{2,1,0:T(8,128)(2,1)} %get-tuple-element.46.wsecond, ...), custom_call_target="tpu_custom_call" | custom-call | tf_op jit(solution)/shard_map/final_block/pallas_call | solution.py:1038
  258.2 5.8 %convolution_bitcast_fusion.1 = f32[1,2,1024,1024]{3,2,1,0:T(8,128)} fusion(bf16[2,768,1024]{2,1,0:T(8,128)(2,1)S(1)} %copy-done.15, bf16[2,768,1024]{2,1,0:T(8,128)(2,1)S(1)} %copy-done.14), kind=kOutput, calls=%fused_computation.1 | convolution fusion | flops 3221225472 | bytes 14680064 | tf_op jit(solution)/shard_map/krf,krd->kfd/dot_general | solution.py:1094
  264.0 5.8 %convolution_bitcast_fusion = f32[1,2,1024,1024]{3,2,1,0:T(8,128)} fusion(bf16[2,768,1024]{2,1,0:T(8,128)(2,1)S(1)} %copy-done.12, bf16[2,768,1024]{2,1,0:T(8,128)(2,1)S(1)} %copy-done.13), kind=kOutput, calls=%fused_computation | convolution fusion | flops 3221225472 | bytes 14680064 | tf_op jit(solution)/shard_map/krf,krd->kfd/dot_general | solution.py:1093
  (44 shorter events, 3.4 us)
Async XLA Ops:
  0.6 57.3 %copy-start.1 = (bf16[128,1024]{1,0:T(8,128)(2,1)S(1)}, bf16[128,1024]{1,0:T(8,128)(2,1)}, u32[]{:S(2)}) copy-start(bf16[128,1024]{1,0:T(8,128)(2,1)} %tok.3) | copy-start | bytes 786436
  52.3 8.0 %copy-start.6 = (bf16[128,1024]{1,0:T(8,128)(2,1)S(1)}, bf16[128,1024]{1,0:T(8,128)(2,1)}, u32[]{:S(2)}) copy-start(bf16[128,1024]{1,0:T(8,128)(2,1)} %param.19) | copy-start | bytes 786436
  61.7 110.5 %copy-start.10 = (s32[128,1]{0,1:T(1,128)S(1)}, s32[128,1]{0,1:T(1,128)}, u32[]{:S(2)}) copy-start(s32[128,1]{0,1:T(1,128)} %param.18) | copy-start | bytes 1540
  169.9 4.6 %copy-start.5 = (bf16[1024,1024]{1,0:T(8,128)(2,1)S(1)}, bf16[1024,1024]{1,0:T(8,128)(2,1)}, u32[]{:S(2)}) copy-start(bf16[1024,1024]{1,0:T(8,128)(2,1)} %get-tuple-element.35) | copy-start | bytes 6291460
  174.4 1.6 copy-start.7
  176.0 67.9 %copy-start = (bf16[256,3072]{1,0:T(8,128)(2,1)S(1)}, bf16[256,3072]{1,0:T(8,128)(2,1)}, u32[]{:S(2)}) copy-start(bf16[256,3072]{1,0:T(8,128)(2,1)} %wqkv.5) | copy-start | bytes 4718596
  243.9 1.4 copy-start.2
  245.3 1.1 copy-start.3
  246.5 1.0 copy-start.4
  247.5 9.5 %copy-start.11 = (bf16[256]{0:T(256)(128)(2,1)S(1)}, bf16[256]{0:T(256)(128)(2,1)}, u32[]{:S(2)}) copy-start(bf16[256]{0:T(256)(128)(2,1)} %param.11) | copy-start | bytes 1540
  247.5 10.1 %copy-start.8 = (f32[8,1,256]{2,1,0:T(1,128)S(1)}, f32[8,1,256]{2,1,0:T(1,128)}, u32[]{:S(2)}) copy-start(f32[8,1,256]{2,1,0:T(1,128)} %get-tuple-element.53) | copy-start | bytes 24580
  247.5 10.7 %copy-start.14 = (bf16[2,768,1024]{2,1,0:T(8,128)(2,1)S(1)}, bf16[2,768,1024]{2,1,0:T(8,128)(2,1)}, u32[]{:S(2)}) copy-start(bf16[2,768,1024]{2,1,0:T(8,128)(2,1)} %get-tuple-element.56) | copy-start | bytes 9437188
  247.5 10.7 %copy-start.15 = (bf16[2,768,1024]{2,1,0:T(8,128)(2,1)S(1)}, bf16[2,768,1024]{2,1,0:T(8,128)(2,1)}, u32[]{:S(2)}) copy-start(bf16[2,768,1024]{2,1,0:T(8,128)(2,1)} %get-tuple-element.55) | copy-start | bytes 9437188
  258.2 5.8 %copy-start.12 = (bf16[2,768,1024]{2,1,0:T(8,128)(2,1)S(1)}, bf16[2,768,1024]{2,1,0:T(8,128)(2,1)}, u32[]{:S(2)}) copy-start(bf16[2,768,1024]{2,1,0:T(8,128)(2,1)} %get-tuple-element.57) | copy-start | bytes 9437188
  258.2 5.8 %copy-start.13 = (bf16[2,768,1024]{2,1,0:T(8,128)(2,1)S(1)}, bf16[2,768,1024]{2,1,0:T(8,128)(2,1)}, u32[]{:S(2)}) copy-start(bf16[2,768,1024]{2,1,0:T(8,128)(2,1)} %get-tuple-element.58) | copy-start | bytes 9437188
  264.0 5.8 %copy-start.9 = (f32[2,256]{1,0:T(2,128)S(1)}, f32[2,256]{1,0:T(2,128)}, u32[]{:S(2)}) copy-start(f32[2,256]{1,0:T(2,128)} %get-tuple-element.54) | copy-start | bytes 6148

commit v4 on v3

--- a/solution.py
+++ b/solution.py
@@ -241,9 +241,9 @@
 
 
 def front_kernel(
-    tok, small, wqkv, wout,
-    olow, normed_out, qkv_out, mixed_out, lse_out, wout_full, small_full, wfirst,
-    held, wblk, normed, qkv, mixed, lse, mixed_low, gain, bounce, smalls,
+    tok, norm_gain, expert_gain, centroids, wqkv, wout,
+    olow, normed_out, qkv_out, mixed_out, wout_full, wfirst, lse_rows, gain_col, gains, cent_full,
+    held, wblk, normed, qkv, mixed, mixed_low, gain, bounce, small, smalls,
     tok_send, tok_recv, w_send, w_recv, o_send, o_recv, copy_sem, q_send, q_recv,
 ):
     j, sibling, across, diagonal = dp_peers()
@@ -270,6 +270,9 @@
         cp.start()
     own_out = pltpu.make_async_copy(wout, bounce, copy_sem.at[4])
     own_out.start()
+    small[...] = jnp.concatenate(
+        [norm_gain[...], expert_gain[0], jnp.zeros((5, shard), BF), centroids[...]], axis=0
+    )
     smalls[j] = small[...]
     greet([{"expert": p} for p in others(8, e)] + [{"dp": p} for p in (sibling, across, diagonal)])
 
@@ -317,7 +320,13 @@
     keep_out.start()
     for s in (sibling, across, diagonal):
         s_arrival(s).wait_recv()
-    gain[...] = jnp.concatenate([smalls[s, 0:1, :] for s in range(4)], axis=1).astype(F32)
+    for s in range(4):
+        at = pl.ds(s * shard, shard)
+        block = smalls[s].astype(F32)
+        gain[:, at] = block[0:1]
+        gain_col[s : s + 1, :] = block[0:1]
+        gains[:, at] = block[1:3]
+        cent_full[:, at] = smalls[s, 8:16, :]
     w_arrival(across).wait_recv()
     w_copy(2).start()
     w_arrival(sibling).wait_recv()
@@ -384,7 +393,9 @@
         res = jnp.where(left, outs[0], outs[1])
         mixed[at, :] = res
         mixed_low[at, :] = res.astype(BF)
-        lse[at, :] = jnp.where(left, logs[0], logs[1])
+        turned = jnp.where(left, logs[0], logs[1]).T
+        lse_rows[0:1, at] = turned[0:1]
+        lse_rows[1:2, at] = turned[HEAD : HEAD + 1]
         for dest in (2 * b, 2 * b + 1):
             @pl.when(dest != e)
             def _():
@@ -395,8 +406,6 @@
                 o_own(dest).start()
     more = [
         pltpu.make_async_copy(mixed, mixed_out, copy_sem.at[2]),
-        pltpu.make_async_copy(lse, lse_out, copy_sem.at[3]),
-        pltpu.make_async_copy(smalls, small_full, copy_sem.at[6]),
     ]
     for cp in more:
         cp.start()
@@ -423,7 +432,7 @@
         cp.wait()
 
 
-def front_block(tokens, small, qkv_weight, out_weight):
+def front_block(tokens, norm_gain, expert_gain, centroids, qkv_weight, out_weight):
     rows, width = tokens.shape
     seq = 8 * rows
     shard = qkv_weight.shape[0]
@@ -435,35 +444,41 @@
     return pl.pallas_call(
         front_kernel,
         out_shape=(
-            S((rows, width), BF), S((seq, width), BF), S((seq, 384), BF), S((seq, 128), F32), S((seq, 128), F32),
-            S((width, width), BF), S((4,) + small.shape, BF), S((4, shard // 2, 3 * width), BF),
+            S((rows, width), BF), S((seq, width), BF), S((seq, 384), BF), S((seq, 128), F32),
+            S((width, width), BF), S((4, shard // 2, 3 * width), BF),
+            S((2, seq), F32), S((4, shard), F32), S((2, width), F32), S((8, width), BF),
         ),
-        in_specs=[any_spec, vmem_spec, any_spec, any_spec],
-        out_specs=(any_spec,) * 8,
+        in_specs=[any_spec, vmem_spec, vmem_spec, vmem_spec, any_spec, any_spec],
+        out_specs=(any_spec,) * 6 + (vmem_spec,) * 4,
         scratch_shapes=[
             V((8, rows, width), BF), V((width, 384), BF), V((seq, width), BF), V((seq, 384), BF),
-            V((seq, 128), F32), V((seq, 128), F32), V((seq, 128), BF), V((1, width), F32), V((shard, width), BF),
-            V((4,) + small.shape, BF),
+            V((seq, 128), F32), V((seq, 128), BF), V((1, width), F32), V((shard, width), BF),
+            V((16, shard), BF), V((4, 16, shard), BF),
             D((22,)), D((16,)), D((9,)), D((12,)), D((8,)), D((8,)), D((8,)), D((3,)), D((4,)),
         ],
         compiler_params=pltpu.CompilerParams(collective_id=2, has_side_effects=True, vmem_limit_bytes=56 * 1024 * 1024),
         name="front_block",
-    )(tokens, small, qkv_weight, out_weight)
+    )(tokens, norm_gain, expert_gain, centroids, qkv_weight, out_weight)
 
 
 def expert_kernel(
     zslots, dslots, olow, gain_ref, w1_hbm, w2_hbm,
     returned, came_back, olow_full, ggain_ref, n_out, h_out, df_out, du_out,
-    w1, w2, x, hid, gpr, unit_s, inv_s, state, total, grad_in, own, far, f1, f3, ssum, rf1, rf3, rss,
-    zland, dland, bsend, gsend, ggain, gland,
-    send_sem, recv_sem, a_send, a_recv, g_send, g_recv, copy_sem, own_sem, e_send, e_recv,
+    w1, w2, x, hid, gpr, unit_s, inv_s, state, total, own, f1, rf1, ssum, rss,
+    zland, dland, zfar, dfar, bsend, gsend, ggain, gland,
+    x_send, x_recv, f_send, f_recv, s_send, s_recv, l_send, l_recv,
+    a_send, a_recv, g_send, g_recv, copy_sem, own_sem, e_send, e_recv,
 ):
     cap, width = zslots.shape[1:]
-    half = 4 * cap
-    pair_rows = 2 * half
+    quarter = 2 * cap
+    pair = 2 * quarter
+    chunk = 2 * pair
     tiles = width // TILE
+    shard = width // 4
     j, sibling, across, diagonal = dp_peers()
     e, zpos, xpos, beside, zs = expert_peers()
+    mine = pl.multiple_of((j // 2) * quarter, 16)
+    theirs = pl.multiple_of((1 - j // 2) * quarter, 16)
 
     loads = []
     for i, (src, dst) in enumerate(
@@ -500,8 +515,8 @@
             return pltpu.make_async_copy(src.at[e], dst.at[xpos], own_sem.at[which])
         return pltpu.make_async_copy(src.at[xpos], dst.at[e], own_sem.at[which])
 
-    def for_places(h, act, mine):
-        for q in range(4 * h, 4 * h + 4):
+    def for_places(c, act, here):
+        for q in (2 * c, 2 * c + 1):
             if q >= 2:
                 act(q)
             else:
@@ -511,61 +526,85 @@
 
                 @pl.when(xpos == q)
                 def _():
-                    mine()
+                    here()
 
     for which, (src, dst) in enumerate([(zslots, zland), (dslots, dland)]):
-        for h in (1, 0):
-            for_places(h, lambda q: swap(src, dst, which, q).start(), lambda: swap_own(src, dst, which).start())
+        for c in ((1, 2, 3, 0) if which == 0 else (3, 2, 1, 0)):
+            for_places(c, lambda q: swap(src, dst, which, q).start(), lambda: swap_own(src, dst, which).start())
     olows = Spread(olow, olow_full, g_send, g_recv, 1)
     own_o = pltpu.make_async_copy(olow, olow_full.at[e], copy_sem.at[12])
     own_o.start()
-
-    def rows_of(h, r):
-        return pl.ds((h * 4 + r) * half, half)
-
-    def remote(src, dst, kind, p, h, peer):
-        i = (p * 2 + h) * 6 + kind
-        return push(src, dst, send_sem.at[i], recv_sem.at[i], {"dp": peer})
-
-    def copy_of(kind, p, h):
-        q = p * 2 + h
-        if kind == 0:
-            return remote(x.at[p, rows_of(h, 0)], x.at[p, rows_of(h, 1)], 0, p, h, sibling)
-        if kind == 1:
-            return remote(x.at[p, rows_of(h, 0)], x.at[p, rows_of(h, 2)], 1, p, h, across)
-        if kind == 2:
-            return remote(x.at[p, rows_of(h, 2)], x.at[p, rows_of(h, 3)], 2, p, h, sibling)
-        if kind == 3:
-            return remote(f1.at[q], rf1.at[q], 3, p, h, sibling)
-        if kind == 4:
-            return remote(f3.at[q], rf3.at[q], 4, p, h, sibling)
-        return remote(ssum.at[q], rss.at[q], 5, p, h, across)
-
     layer_of = (0, 1, 1, 0)
 
-    def start_rows(p, h):
-        k = layer_of[p]
-        rs = pl.ds(h * half, half)
-        if p < 2:
-            v = state[rs, :]
+    def my_half(c):
+        return pl.ds(c * chunk, pair)
+
+    def x_copy(p, c):
+        q = 4 * p + c
+        return push(x.at[p, my_half(c)], x.at[p, pl.ds(c * chunk + pair, pair)], x_send.at[q], x_recv.at[q], {"dp": sibling})
+
+    def f_copy(q, cols):
+        return push(f1.at[q, :, cols], rf1.at[q, :, cols], f_send.at[q], f_recv.at[q], {"dp": sibling})
+
+    def s_copy(p, c, arrives=False):
+        q = 4 * p + c
+        if p in (0, 2):
+            return push(ssum.at[q], rss.at[q], s_send.at[q], s_recv.at[q], {"dp": across})
+        at = pl.ds(mine if arrives else theirs, quarter)
+        return push(ssum.at[q, at], rss.at[q, at], s_send.at[q], s_recv.at[q], {"dp": across})
+
+    def land_copy(which, c):
+        src, dst = (zland, zfar) if which == 0 else (dland, dfar)
+        at = pl.ds(2 * c, 2)
+        return push(src.at[at], dst.at[at], l_send.at[4 * which + c], l_recv.at[4 * which + c], {"dp": across})
+
+    def forward(which, c):
+        src, dst = (zslots, zland) if which == 0 else (dslots, dland)
+        for_places(c, lambda q: swap_arrival(src, dst, which, q).wait_recv(), lambda: swap_own(src, dst, which).wait())
+        land_copy(which, c).start()
+
+    def both(buf, c):
+        return jnp.concatenate([buf[2 * c].astype(F32), buf[2 * c + 1].astype(F32)], axis=0)
+
+    def by_rows(act):
+        def step(t, carry):
+            act(pl.multiple_of(t * 32, 32))
+            return carry
+        lax.fori_loop(0, pair // 32, step, 0)
+
+    def norm_rows(p, c, read):
+        def act(t):
+            v = read(t)
             center = v - mean_last(v)
             inverse = lax.rsqrt(mean_last(center * center) + EPS)
             unit = center * inverse
-            unit_s[k, rs, :] = unit
-            inv_s[k, rs, :] = jnp.broadcast_to(inverse, (half, 128))
-            x[p, rows_of(h, 0), :] = (unit * gain_ref[pl.ds(k, 1), :]).astype(BF)
-        else:
-            x[p, rows_of(h, 0), :] = (grad_in[rs, :] + state[rs, :]).astype(BF)
-        copy_of(1, p, h).start()
-        copy_of(0, p, h).start()
-
-    def compute(p, h, pair):
+            rs = pl.ds(c * pair + t, 32)
+            unit_s[p, rs, :] = unit
+            inv_s[p, rs, :] = jnp.broadcast_to(inverse, (32, 128))
+            x[p, pl.ds(c * chunk + t, 32), :] = (unit * gain_ref[pl.ds(p, 1), :]).astype(BF)
+        by_rows(act)
+        x_copy(p, c).start()
+
+    def begin(c):
+        land_copy(0, c).wait_recv()
+        state[pl.ds(c * pair + mine, quarter), :] = both(zland, c)
+        state[pl.ds(c * pair + theirs, quarter), :] = both(zfar, c)
+        norm_rows(0, c, lambda t: state[pl.ds(c * pair + t, 32), :])
+
+    def begin_back(c):
+        land_copy(1, c).wait_recv()
+        x[2, pl.ds(c * chunk + mine, quarter), :] = both(dland, c).astype(BF)
+        x[2, pl.ds(c * chunk + theirs, quarter), :] = both(dfar, c).astype(BF)
+        x_copy(2, c).start()
+
+    def compute(p, c):
         k = layer_of[p]
-        base = pl.ds((h * 2 + pair) * pair_rows, pair_rows)
+        base = pl.ds(c * chunk, chunk)
         left_w, right_w = (w1, w2) if p < 2 else (w2, w1)
-        q = p * 2 + h
-
-        def up(t, c):
+        q = 4 * p + c
+        x_copy(p, c).wait_recv()
+
+        def up(t, carry):
             cols = pl.ds(pl.multiple_of(t * TILE, TILE), TILE)
             pre = lax.dot_general(x[p, base, :], left_w[k, cols, :], NT, preferred_element_type=F32)
             if p < 2:
@@ -575,70 +614,86 @@
                 gpr[k, base, cols] = cdf + pre * pdf
             else:
                 hid[2 + k, base, cols] = (pre * gpr[k, base, cols]).astype(BF)
-            return c
+            return carry
 
         lax.fori_loop(0, tiles, up, 0)
         slot = k if p < 2 else 2 + k
 
-        def down(t, c):
+        def down(t, carry):
             cols = pl.ds(pl.multiple_of(t * TILE, TILE), TILE)
             res = jnp.dot(hid[slot, base, :], right_w[k, :, cols], preferred_element_type=F32)
-            if pair == 0:
-                own[h, :, cols] = res[:half]
-                f1[q, :, cols] = res[half:].astype(BF)
+            own[c, :, cols] = res[:pair]
+            f1[q, :, cols] = res[pair:].astype(BF)
+            f_copy(q, cols).start()
+            return carry
+
+        lax.fori_loop(0, tiles, down, 0)
+
+    everything = pl.ds(0, width)
+
+    def send_sum(p, c):
+        q = 4 * p + c
+        f_copy(q, everything).wait_recv()
+
+        def act(t):
+            rs = pl.ds(t, 32)
+            v = own[c, rs, :] + rf1[q, rs, :].astype(F32)
+            own[c, rs, :] = v
+            ssum[q, rs, :] = v.astype(BF)
+        by_rows(act)
+        s_copy(p, c).start()
+
+    def give_back(buf, dst, which, c, v):
+        for i in range(2):
+            buf[2 * c + i] = v[i * cap : (i + 1) * cap].astype(BF)
+        for_places(c, lambda q: swap(buf, dst, which, q).start(), lambda: swap_own(buf, dst, which).start())
+
+    def add_gain(k, c, part):
+        if c == 0:
+            ggain[pl.ds(k, 1), :] = part
+        else:
+            ggain[pl.ds(k, 1), :] = ggain[pl.ds(k, 1), :] + part
+
+    def norm_back(k, got, rs):
+        unit = unit_s[k, rs, :]
+        a = got * gain_ref[pl.ds(k, 1), :]
+        back = inv_s[k, rs, :][:, :1] * (a - mean_last(a) - unit * mean_last(a * unit))
+        return back, jnp.sum(got * unit, axis=0, keepdims=True)
+
+    def finish(p, c):
+        k = layer_of[p]
+        q = 4 * p + c
+        s_copy(p, c, True).wait_recv()
+        if p == 0:
+            def read(t):
+                rs = pl.ds(c * pair + t, 32)
+                got = own[c, pl.ds(t, 32), :] + rss[q, pl.ds(t, 32), :].astype(F32)
+                total[rs, :] = got
+                return state[rs, :] + got
+            norm_rows(1, c, read)
+        elif p == 2:
+            def step(i, part):
+                t = pl.multiple_of(i * 32, 32)
+                rs = pl.ds(c * pair + t, 32)
+                got = own[c, pl.ds(t, 32), :] + rss[q, pl.ds(t, 32), :].astype(F32)
+                back, add = norm_back(1, got, rs)
+                state[rs, :] = back
+                at = pl.ds(c * chunk + t, 32)
+                x[3, at, :] = (x[2, at, :].astype(F32) + back).astype(BF)
+                return part + add
+            part = lax.fori_loop(0, pair // 32, step, jnp.zeros((1, width), F32))
+            x_copy(3, c).start()
+            add_gain(1, c, 0.5 * part)
+        else:
+            at = pl.ds(mine, quarter)
+            rs = pl.ds(c * pair + mine, quarter)
+            got = own[c, at, :] + rss[q, at, :].astype(F32)
+            if p == 1:
+                give_back(bsend, returned, 2, c, total[rs, :] + got)
             else:
-                far[h, :, cols] = res[:half]
-                f3[q, :, cols] = res[half:].astype(BF)
-                remote(f3.at[q, :, cols], rf3.at[q, :, cols], 4, p, h, sibling).start()
-            return c
-
-        lax.fori_loop(0, tiles, down, 0)
-        if pair == 0:
-            copy_of(3, p, h).start()
-
-    def send_sum(p, h):
-        q = p * 2 + h
-        copy_of(4, p, h).wait_recv()
-        ssum[q] = (far[h] + rf3[q].astype(F32)).astype(BF)
-        copy_of(5, p, h).start()
-
-    def give_back(buf, dst, which, h):
-        for_places(h, lambda q: swap(buf, dst, which, q).start(), lambda: swap_own(buf, dst, which).start())
-
-    def finish(p, h):
-        k = layer_of[p]
-        q = p * 2 + h
-        rs = pl.ds(h * half, half)
-        copy_of(3, p, h).wait_recv()
-        copy_of(5, p, h).wait_recv()
-        got = own[h] + rf1[q].astype(F32) + rss[q].astype(F32)
-        if p == 0:
-            state[rs, :] = state[rs, :] + got
-            total[rs, :] = got
-        elif p == 1:
-            total[rs, :] = total[rs, :] + got
-            for i in range(4):
-                bsend[4 * h + i] = total[pl.ds(h * half + i * cap, cap), :].astype(BF)
-            state[rs, :] = jnp.zeros((half, width), F32)
-            give_back(bsend, returned, 2, h)
-        else:
-            unit = unit_s[k, rs, :]
-            part = jnp.sum(got * unit, axis=0, keepdims=True)
-            if h == 0:
-                ggain[pl.ds(k, 1), :] = part
-            else:
-                ggain[pl.ds(k, 1), :] = ggain[pl.ds(k, 1), :] + part
-            a = got * gain_ref[pl.ds(k, 1), :]
-            back = inv_s[k, rs, :][:, :1] * (a - mean_last(a) - unit * mean_last(a * unit))
-            state[rs, :] = state[rs, :] + back
-            if p == 3:
-                for i in range(4):
-                    gsend[4 * h + i] = state[pl.ds(h * half + i * cap, cap), :].astype(BF)
-                give_back(gsend, came_back, 3, h)
-
-    def relay(p, h):
-        copy_of(1, p, h).wait_recv()
-        copy_of(2, p, h).start()
+                back, part = norm_back(0, got, rs)
+                give_back(gsend, came_back, 3, c, state[rs, :] + back)
+                add_gain(0, c, part)
 
     stores = []
 
@@ -647,61 +702,46 @@
         cp.start()
         stores.append(cp)
 
-    def landed(src, buf, which, h, out):
-        for_places(h, lambda q: swap_arrival(src, buf, which, q).wait_recv(), lambda: swap_own(src, buf, which).wait())
-        for q in range(4 * h, 4 * h + 4):
-            out[pl.ds(q * cap, cap), :] = buf[q].astype(F32)
-
     def gain_copy(i):
         s = (sibling, across, diagonal)[i]
         return push(ggain.at[:, pl.ds(pl.multiple_of(s * shard, shard), shard)], gland.at[j], e_send.at[i], e_recv.at[j], {"dp": s})
 
-    shard = width // 4
-    landed(zslots, zland, 0, 0, state)
-    start_rows(0, 0)
+    forward(0, 0)
+    forward(0, 1)
+    begin(0)
     loads[0].wait()
     loads[1].wait()
-    copy_of(0, 0, 0).wait_recv()
-    compute(0, 0, 0)
-    landed(zslots, zland, 0, 1, state)
-    start_rows(0, 1)
-    for p in range(4):
-        relay(p, 0)
-        copy_of(2, p, 0).wait_recv()
-        compute(p, 0, 1)
-        send_sum(p, 0)
-        if p == 0:
-            olows.start()
-        relay(p, 1)
-        copy_of(0, p, 1).wait_recv()
-        compute(p, 1, 0)
-        copy_of(2, p, 1).wait_recv()
-        compute(p, 1, 1)
-        if p == 1:
-            landed(dslots, dland, 1, 0, grad_in)
-            landed(dslots, dland, 1, 1, grad_in)
-        finish(p, 0)
-        if p < 3:
-            start_rows(p + 1, 0)
-        send_sum(p, 1)
-        if p < 3:
-            olows.step(p + 1)
-        if p == 0:
+    for t in range(16):
+        p, c = divmod(t, 4)
+        if t == 4:
             loads[2].wait()
             loads[3].wait()
-        if p < 3:
-            copy_of(0, p + 1, 0).wait_recv()
-            compute(p + 1, 0, 0)
-        finish(p, 1)
-        if p < 3:
-            start_rows(p + 1, 1)
-        k = layer_of[p]
-        if p < 2:
-            store(p * 2, x.at[p], n_out.at[k])
-            store(p * 2 + 1, hid.at[k], h_out.at[k])
-        else:
-            store(p * 2, x.at[p], df_out.at[k])
-            store(p * 2 + 1, hid.at[2 + k], du_out.at[k])
+        compute(p, c)
+        if t < 2:
+            forward(0, t + 2)
+        if 2 <= t < 6:
+            forward(1, t - 2)
+        if t < 3:
+            begin(t + 1)
+        if t >= 2:
+            finish(*divmod(t - 2, 4))
+        send_sum(p, c)
+        if 5 <= t < 9:
+            begin_back(t - 5)
+        if t == 2:
+            olows.start()
+        if t in (5, 8, 11):
+            olows.step((t - 2) // 3)
+        if c == 3:
+            k = layer_of[p]
+            if p < 2:
+                store(p * 2, x.at[p], n_out.at[k])
+                store(p * 2 + 1, hid.at[k], h_out.at[k])
+            else:
+                store(p * 2, x.at[p], df_out.at[k])
+                store(p * 2 + 1, hid.at[2 + k], du_out.at[k])
+    finish(3, 2)
+    finish(3, 3)
     for i in range(3):
         gain_copy(i).start()
     gland[j] = ggain[:, pl.ds(pl.multiple_of(j * shard, shard), shard)]
@@ -710,26 +750,30 @@
         olows.wait_beside(zz)
     olows.drain()
     for p in range(4):
-        for h in range(2):
-            for kind in range(6):
-                copy_of(kind, p, h).wait_send()
+        for c in range(4):
+            x_copy(p, c).wait_send()
+            f_copy(4 * p + c, everything).wait_send()
+            s_copy(p, c).wait_send()
+    for i in range(2):
+        for c in range(4):
+            land_copy(i, c).wait_send()
     for cp in stores:
         cp.wait()
     for i in range(3):
         push(ggain.at[:, pl.ds(0, shard)], gland.at[(sibling, across, diagonal)[i]], e_send.at[0], e_recv.at[(sibling, across, diagonal)[i]], {"dp": sibling}).wait_recv()
         gain_copy(i).wait_send()
     ggain_ref[...] = jnp.sum(gland[...], axis=0)
-    for h in range(2):
+    for c in range(4):
         for which, (src, dst) in enumerate([(zslots, zland), (dslots, dland), (bsend, returned), (gsend, came_back)]):
-            for_places(h, lambda q: swap(src, dst, which, q).wait_send(), lambda: None)
+            for_places(c, lambda q: swap(src, dst, which, q).wait_send(), lambda: None)
             if which >= 2:
-                for_places(h, lambda q: swap_arrival(src, dst, which, q).wait_recv(), lambda: swap_own(src, dst, which).wait())
+                for_places(c, lambda q: swap_arrival(src, dst, which, q).wait_recv(), lambda: swap_own(src, dst, which).wait())
 
 
 def expert_block(zslots, dslots, olow, gains, expert_in, expert_out):
     sources, cap, width = zslots.shape
     rows = sources * cap
-    half = rows // 2
+    pair = 4 * cap
     hidden = expert_in.shape[2]
     everything = 4 * rows
     any_spec = pl.BlockSpec(memory_space=pl.ANY)
@@ -749,15 +793,16 @@
         scratch_shapes=[
             V((2, hidden, width), BF), V((2, hidden, width), BF),
             V((4, everything, width), BF), V((4, everything, hidden), BF), V((2, everything, hidden), F32),
-            V((2, rows, width), F32), V((2, rows, 128), F32), V((rows, width), F32), V((rows, width), F32),
-            V((rows, width), F32), V((2, half, width), F32), V((2, half, width), F32),
+            V((2, 2 * rows, width), F32), V((2, 2 * rows, 128), F32), V((2 * rows, width), F32), V((2 * rows, width), F32),
+            V((4, pair, width), F32),
         ]
-        + [V((8, half, width), BF)] * 6
-        + [V(zslots.shape, BF)] * 4
+        + [V((16, pair, width), BF)] * 4
+        + [V(zslots.shape, BF)] * 6
         + [V((2, width), F32), V((4, 2, width // 4), F32)]
-        + [D((48,)), D((48,)), D((32,)), D((32,)), D((11,)), D((8,)), D((13,)), D((4,)), D((3,)), D((4,))],
+        + [D((16,))] * 6 + [D((8,))] * 2
+        + [D((32,)), D((32,)), D((11,)), D((8,)), D((13,)), D((4,)), D((3,)), D((4,))],
         compiler_params=pltpu.CompilerParams(
-            collective_id=1, has_side_effects=True, vmem_limit_bytes=60 * 1024 * 1024
+            collective_id=1, has_side_effects=True, vmem_limit_bytes=62 * 1024 * 1024
         ),
         name="expert_block",
     )(zslots, dslots, olow, gains, expert_in, expert_out)
@@ -988,22 +1033,68 @@
 
 
 def final_kernel(
-    dq_land, wfirst, wsecond, tok, gain_col, gres, gq_land, go_land, wqkv,
-    gtok, gqkv, gout, ggain,
-    dqkv, dnorm, small_sum,
+    dq_hbm, wfirst, wsecond, tok_hbm, gain_col, gres_hbm, gq_hbm, go_hbm, wqkv_hbm, gc_land, gain_part,
+    n_hbm, h_hbm, df_hbm, du_hbm,
+    gtok_hbm, gqkv_hbm, gout_hbm, gnorm, gcent, ggain, gein, geout,
+    n, h, df, du, tile_in, tile_out, dq_land, w, tok, gres, gq_land, go_land, wqkv,
+    dqkv, dnorm, gtok, gqkv, gout, small_sum,
+    load_sem, tile_sem, store_sem,
 ):
     rows, width = tok.shape
     shard = wqkv.shape[0]
     half = shard // 2
+    tiles = width // TILE
+
+    def load(i, src, dst):
+        cp = pltpu.make_async_copy(src, dst, load_sem.at[i])
+        cp.start()
+        return cp
+
+    pairs = []
+    for i, (src, dst) in enumerate([(du_hbm, du), (n_hbm, n), (h_hbm, h), (df_hbm, df)]):
+        pairs.append([load(2 * i + k, src.at[k], dst.at[k]) for k in range(2)])
+    first = [load(8, dq_hbm, dq_land), load(9, gq_hbm, gq_land), load(10, go_hbm, go_land), load(11, wqkv_hbm, wqkv)]
+    rest = [load(12, tok_hbm, tok), load(13, gres_hbm, gres)]
+    for s in range(4):
+        rest.append(load(14 + 2 * s, wfirst.at[s], w.at[s, pl.ds(0, half)]))
+        rest.append(load(15 + 2 * s, wsecond.at[s], w.at[s, pl.ds(half, half)]))
+
+    def tile_copy(stage, out, base, k, t):
+        at = pl.ds(pl.multiple_of(t * TILE, TILE), TILE)
+        return pltpu.make_async_copy(stage.at[k, at], out.at[k, at], tile_sem.at[(base + k) * tiles + t])
+
+    for base, left, right, stage, out, waits in (
+        (0, du, n, tile_in, gein, pairs[:2]), (2, h, df, tile_out, geout, pairs[2:]),
+    ):
+        for k in range(2):
+            for pair in waits:
+                pair[k].wait()
+
+            def tile(t, c):
+                at = pl.ds(pl.multiple_of(t * TILE, TILE), TILE)
+                stage[k, at, :] = lax.dot_general(left[k, :, at], right[k], TN, preferred_element_type=F32)
+                tile_copy(stage, out, base, k, t).start()
+                return c
+
+            lax.fori_loop(0, tiles, tile, 0)
+    for cp in first:
+        cp.wait()
     for s in range(8):
         for i in range(3):
             at = pl.ds(i * width + s * 128, 128)
             dqkv[:, at] = dq_land[s, :, pl.ds(i * 128, 128)]
             gqkv[:, at] = gq_land[s, :, pl.ds(i * 128, 128)].astype(F32)
         gout[:, pl.ds(s * 128, 128)] = go_land[s].astype(F32)
+    stores = [
+        pltpu.make_async_copy(gqkv, gqkv_hbm, store_sem.at[0]),
+        pltpu.make_async_copy(gout, gout_hbm, store_sem.at[1]),
+    ]
+    for cp in stores:
+        cp.start()
+    for cp in rest:
+        cp.wait()
     for s in range(4):
-        for side, w in enumerate((wfirst, wsecond)):
-            dnorm[:, pl.ds(s * shard + side * half, half)] = lax.dot_general(dqkv[...], w[s], NT, preferred_element_type=F32)
+        dnorm[:, pl.ds(s * shard, shard)] = lax.dot_general(dqkv[...], w[s], NT, preferred_element_type=F32)
     gain = jnp.concatenate([gain_col[s : s + 1, :] for s in range(4)], axis=1)
 
     def norm_rows(t, c):
@@ -1017,6 +1108,8 @@
         return c
 
     lax.fori_loop(0, rows // 32, norm_rows, 0)
+    stores.append(pltpu.make_async_copy(gtok, gtok_hbm, store_sem.at[2]))
+    stores[2].start()
     small_sum[...] = jnp.zeros_like(small_sum)
 
     def add(t, c):
@@ -1026,24 +1119,49 @@
         return c
 
     lax.fori_loop(0, 3 * width // 256, add, 0)
-    ggain[...] = lax.dot_general(jnp.ones((8, 128), F32), small_sum[...], NT, precision=HIGH, preferred_element_type=F32)
-
-
-def final_block(dq_land, wfirst, wsecond, tokens, gain_col, grad_resid, gq_land, go_land, qkv_weight):
+    own_gain = gain_col[pl.ds(lax.axis_index("dp"), 1), :]
+    sums = lax.dot_general(jnp.ones((8, 128), F32), small_sum[...], NT, precision=HIGH, preferred_element_type=F32)
+    gnorm[...] = sums[0:1] / own_gain
+    for s in range(8):
+        gcent[s : s + 1, :] = gc_land[s]
+    ggain[...] = gain_part[...]
+    for cp in stores:
+        cp.wait()
+    for k in range(2):
+        for t in range(tiles):
+            tile_copy(tile_in, gein, 0, k, t).wait()
+            tile_copy(tile_out, geout, 2, k, t).wait()
+
+
+def final_block(dq_land, wfirst, wsecond, tokens, gain_col, grad_resid, gq_land, go_land, qkv_weight, gc_land, gain_part, n, h, df, du):
     rows, width = tokens.shape
     shard = width // 4
+    hidden = h.shape[2]
+    any_spec = pl.BlockSpec(memory_space=pl.ANY)
     vmem_spec = pl.BlockSpec(memory_space=pltpu.VMEM)
     S = jax.ShapeDtypeStruct
     V = pltpu.VMEM
+    D = pltpu.SemaphoreType.DMA
     return pl.pallas_call(
         final_kernel,
-        out_shape=(S((rows, width), F32), S((shard, 3 * width), F32), S((shard, width), F32), S((8, shard), F32)),
-        in_specs=[vmem_spec] * 9,
-        out_specs=(vmem_spec,) * 4,
-        scratch_shapes=[V((rows, 3 * width), BF), V((rows, width), F32), V((shard, 128), F32)],
-        compiler_params=pltpu.CompilerParams(vmem_limit_bytes=48 * 1024 * 1024),
+        out_shape=(
+            S((rows, width), F32), S((shard, 3 * width), F32), S((shard, width), F32), S((1, shard), F32),
+            S((8, shard), F32), S((2, shard), F32), S((2, hidden, width), F32), S((2, hidden, width), F32),
+        ),
+        in_specs=[any_spec] * 4 + [vmem_spec] + [any_spec] * 4 + [vmem_spec] * 2 + [any_spec] * 4,
+        out_specs=(any_spec,) * 3 + (vmem_spec,) * 3 + (any_spec,) * 2,
+        scratch_shapes=[V(n.shape, BF), V(h.shape, BF), V(df.shape, BF), V(du.shape, BF)]
+        + [V((2, hidden, width), F32)] * 2
+        + [
+            V(dq_land.shape, BF), V((4, shard, 3 * width), BF), V((rows, width), BF), V((rows, width), F32),
+            V(gq_land.shape, BF), V(go_land.shape, BF), V((shard, 3 * width), BF),
+            V((rows, 3 * width), BF), V((rows, width), F32), V((rows, width), F32),
+            V((shard, 3 * width), F32), V((shard, width), F32), V((shard, 128), F32),
+            D((22,)), D((16,)), D((3,)),
+        ],
+        compiler_params=pltpu.CompilerParams(vmem_limit_bytes=58 * 1024 * 1024),
         name="final_block",
-    )(dq_land, wfirst, wsecond, tokens, gain_col, grad_resid, gq_land, go_land, qkv_weight)
+    )(dq_land, wfirst, wsecond, tokens, gain_col, grad_resid, gq_land, go_land, qkv_weight, gc_land, gain_part, n, h, df, du)
 
 
 def on_device_split(
@@ -1063,12 +1181,9 @@
     capacity = max(2, 3 * rows // (2 * experts))
     slots = experts * capacity
     shard = width // 4
-    small = jnp.concatenate(
-        [norm_gain[None], expert_gain[0], jnp.zeros((5, shard), BF), centroids], axis=0
-    )
-    olow, normed_all, qkv, mixed, lse, wout_full, small_full, wfirst = front_block(tokens, small, qkv_weight, out_weight)
-    gains = small_full[:, 1:3].transpose(1, 0, 2).reshape(2, width).astype(F32)
-    centroid_full = small_full[:, 8:16].transpose(1, 0, 2).reshape(8, width)
+    olow, normed_all, qkv, mixed, wout_full, wfirst, lse_rows, gain_col, gains, centroid_full = front_block(
+        tokens, norm_gain[None], expert_gain, centroids, qkv_weight, out_weight
+    )
     inputs = tokens.astype(F32)
     residual = inputs + jnp.dot(olow, wout_full, preferred_element_type=F32)
     route_ids = routes[:, 0]
@@ -1090,8 +1205,6 @@
         expert_in,
         expert_out,
     )
-    grad_expert_out = jnp.einsum("krf,krd->kfd", h_rows, df_rows, preferred_element_type=F32)[None]
-    grad_expert_in = jnp.einsum("krf,krd->kfd", du_rows, n_rows, preferred_element_type=F32)[None]
     branch_tok = lax.dot_general(place, returned.reshape(slots, width), TN, preferred_element_type=F32)
     block_out = (residual + gate[:, None] * branch_tok).astype(BF)
     grad_logit = jnp.sum(grad_out * branch_tok, axis=-1) * gate * (1.0 - gate)
@@ -1100,26 +1213,24 @@
     grad_resid = grad_out + grad_logit[:, None] * centroid_rows + back_rows
     grad_attended = grad_resid.astype(BF)
     grad_mixed = lax.dot_general(grad_attended, wout_full, NT, preferred_element_type=F32).astype(BF)
-    lse_rows = jnp.pad(lse[:, ::HEAD].T, ((0, 6), (0, 0)))
     dq_land, gq_land, go_land, gc_land, wsecond = back_block(
         grad_mixed, grad_attended, qkv, mixed, lse_rows, normed_all,
         olow_full.reshape(experts * rows, width), grad_centroid[:, None, :], qkv_weight,
     )
-    gain_col = small_full[:, 0].astype(F32)
-    grad_tokens, grad_qkv, grad_out_weight, gain_sums = final_block(
-        dq_land, wfirst, wsecond, tokens, gain_col, grad_resid, gq_land, go_land, qkv_weight
-    )
-    grad_norm_gain = gain_sums[0] / norm_gain.astype(F32)
+    grad_tokens, grad_qkv, grad_out_weight, grad_norm_gain, grad_centroids, grad_gain, grad_expert_in, grad_expert_out = final_block(
+        dq_land, wfirst, wsecond, tokens, gain_col, grad_resid, gq_land, go_land, qkv_weight, gc_land, gain_part,
+        n_rows, h_rows, df_rows, du_rows,
+    )
     return (
         block_out,
         grad_tokens,
-        grad_norm_gain,
+        grad_norm_gain[0],
         grad_qkv,
         grad_out_weight,
-        gc_land[:, 0],
-        gain_part[None],
-        grad_expert_in,
-        grad_expert_out,
+        grad_centroids,
+        grad_gain[None],
+        grad_expert_in[None],
+        grad_expert_out[None],
     )
 
 

time: 271 us -> 246 us (0.908)
  matrix products: 21.5 us -> 10.8 us
  local copies, waits for them, and re-layouts: 10.5 us -> 2.82 us
  other arithmetic: 4.12 us -> 0.82 us
  Pallas kernels: 233 us -> 230 us
    pallas_call x1, Pallas kernels: 108 us -> 93.7 us  [expert_block(): pl.pallas_call(expert_kernel, out_shape=(S(zslots.shape, BF), S(zslots.sh...]
    dot_general x2 -> x0, matrix products: 11.6 us -> none  [the longest x1 5.81 us: on_device_split(): jnp.einsum('krf,krd->kfd', du_rows, n_rows, preferred_element_type=F32)]
    pallas_call x1, Pallas kernels: 9.49 us -> 19.1 us  [final_block(): pl.pallas_call(final_kernel, out_shape=(S((rows, width), F32), S((shard,...]
    unnamed x34 -> x10, local copies, waits for them, and re-layouts: 4.81 us -> 0.03 us
where the time goes in v4:
time: 246 us; the launch traced here: 245 us
  Pallas kernels  230 us (93%)
  matrix products  10.8 us (4%)
  local copies, waits for them, and re-layouts  2.82 us (1%)
    pallas_call x1, Pallas kernels, expert_block(): pl.pallas_call(expert_kernel, out_shape=(S(zslots.shape, BF), S(zslots.sh...  93.7 us
    pallas_call x1, Pallas kernels, back_block(): pl.pallas_call(back_kernel, out_shape=(S((8, rows, 384), BF), S((8, shard...  68.5 us
    pallas_call x1, Pallas kernels, front_block(): pl.pallas_call(front_kernel, out_shape=(S((rows, width), BF), S((seq, wid...  48.5 us
    pallas_call x1, Pallas kernels, final_block(): pl.pallas_call(final_kernel, out_shape=(S((rows, width), F32), S((shard,...  19.1 us

profile of v4, /device:TPU:0, one launch (start us, length us, event | category | flops | bytes accessed | tf_op | source)
XLA Modules:
  0.0 245.2 jit_solution(6523699807970765963)
XLA Ops:
  0.6 0.0 copy-start.1
  0.7 0.0 copy-start.4
  0.7 1.0 fusion
  1.6 0.7 convert_add_fusion.1
  2.3 1.2 broadcast_in_dim.29.norm_gain
  3.5 48.5 %front_block.1 = (bf16[128,1024]{1,0:T(8,128)(2,1)}, bf16[1024,1024]{1,0:T(8,128)(2,1)}, bf16[1024,384]{1,0:T(8,128)(2,1)}, f32[1024,128]{1,0:T(8,128)}, bf16[10...) custom-call(bf16[128,1024]{1,0:T(8,128)(2,1)} %tok_hbm.1, ...), custom_call_target="tpu_custom_call" | custom-call | tf_op jit(solution)/shard_map/front_block/pallas_call | solution.py:444
  52.1 0.0 copy-done.4
  52.1 1.0 fusion.19
  53.1 0.0 copy-done.1
  53.1 0.0 copy-start.3
  53.1 2.3 fusion.27
  55.4 0.0 copy-done.3
  55.4 0.1 fusion.1
  55.5 0.4 convolution_convert_fusion
  55.9 0.9 fusion.26
  56.8 93.7 %expert_block.1 = (bf16[8,24,1024]{2,1,0:T(8,128)(2,1)}, bf16[8,24,1024]{2,1,0:T(8,128)(2,1)}, bf16[8,128,1024]{2,1,0:T(8,128)(2,1)}, f32[2,256]{1,0:T(2,128)}, ...) custom-call(bf16[8,24,1024]{2,1,0:T(8,128)(2,1)} %bitcast.20, ...), custom_call_target="tpu_custom_call" | custom-call | tf_op jit(solution)/shard_map/expert_block/pallas_call | solution.py:785
  150.5 0.0 copy-start
  150.5 2.2 fusion.2
  152.7 0.4 fusion.6
  153.1 0.6 broadcast_in_dim.32.cent
  153.8 2.1 fusion.28
  155.8 1.6 convolution_convert_fusion.1.gmix
  157.4 68.5 %back_block.1 = (bf16[8,128,384]{2,1,0:T(8,128)(2,1)}, bf16[8,256,384]{2,1,0:T(8,128)(2,1)}, bf16[8,256,128]{2,1,0:T(8,128)(2,1)}, f32[8,1,256]{2,1,0:T(1,128)}, bf16[4,128,3072]{2,1,0:T(8,128)(2,1)}) custom-call(bf16[128,1024]{1,0:T(8,128)(2,1)} %convolution_convert_fusion.1.gmix, bf16[128,1024]{1,0:T(8,128)(2,1)} %copy-done.2, ...), custom_call_target="tpu_custom_call" | custom-call | tf_op jit(solution)/shard_map/back_block/pallas_call | solution.py:1012
  225.9 19.1 %final_block.1 = (f32[128,1024]{1,0:T(8,128)}, f32[256,3072]{1,0:T(8,128)}, f32[256,1024]{1,0:T(8,128)}, f32[1,256]{1,0:T(1,128)}, f32[8,256]{1,0:T(8,128)}, /*i...) custom-call(bf16[8,128,384]{2,1,0:T(8,128)(2,1)} %get-tuple-element.51.dq_hbm, ...), custom_call_target="tpu_custom_call" | custom-call | tf_op jit(solution)/shard_map/final_block/pallas_call | solution.py:1145
  (6 shorter events, 0.0 us)
Async XLA Ops:
  0.6 52.4 %copy-start.1 = (bf16[128,1024]{1,0:T(8,128)(2,1)S(1)}, bf16[128,1024]{1,0:T(8,128)(2,1)}, u32[]{:S(2)}) copy-start(bf16[128,1024]{1,0:T(8,128)(2,1)} %tok_hbm.1) | copy-start | bytes 786436
  0.7 51.4 %copy-start.4 = (s32[128,1]{0,1:T(1,128)S(1)}, s32[128,1]{0,1:T(1,128)}, u32[]{:S(2)}) copy-start(s32[128,1]{0,1:T(1,128)} %param.18) | copy-start | bytes 1540
  53.1 2.3 copy-start.3
  150.5 5.3 %copy-start = (bf16[1024,1024]{1,0:T(8,128)(2,1)S(1)}, bf16[1024,1024]{1,0:T(8,128)(2,1)}, u32[]{:S(2)}) copy-start(bf16[1024,1024]{1,0:T(8,128)(2,1)} %get-tuple-element.41) | copy-start | bytes 6291460
  155.8 1.6 copy-start.2

commit v5 on v4

--- a/solution.py
+++ b/solution.py
@@ -148,9 +148,9 @@
         block = self.slots.at[s, self.rows(c)]
         return push(block, block, self.send.at[base * self.chunks + c], self.recv.at[s * self.chunks + c], {"expert": peer})
 
-    def own_all(self, act):
+    def own_all(self, act, chunks):
         for way in range(3):
-            for c in range(self.chunks):
+            for c in chunks:
                 if way == 0:
                     act(self.own(way, c))
                 else:
@@ -159,7 +159,10 @@
                         act(self.own(way, c))
 
     def start(self):
-        self.own_all(lambda cp: cp.start())
+        self.own_all(lambda cp: cp.start(), range(self.chunks))
+
+    def start_chunk(self, c):
+        self.own_all(lambda cp: cp.start(), (c,))
 
     def each(self, d, act):
         for sign in (-1, 1):
@@ -189,7 +192,7 @@
             self.slot(2 * zz + 1 - self.x, c, 0, self.beside).wait_recv()
 
     def drain(self):
-        self.own_all(lambda cp: cp.wait_send())
+        self.own_all(lambda cp: cp.wait_send(), range(self.chunks))
 
         def act(s, zz, onward, c):
             @pl.when(jnp.logical_and(onward >= 0, onward <= 3))
@@ -203,10 +206,9 @@
 
 
 class Weights:
-    def __init__(self, src, first, rows, full, send, recv, copy):
+    def __init__(self, src, first, rows, full, send, recv):
         self.j, self.sibling, self.across, self.diagonal = dp_peers()
         self.src, self.full, self.send, self.recv = src.at[pl.ds(first, rows)], full, send, recv
-        self.keep = pltpu.make_async_copy(self.src, full.at[self.j], copy)
 
     def copy(self, kind):
         if kind == 2:
@@ -218,7 +220,6 @@
     def start(self):
         self.copy(1).start()
         self.copy(0).start()
-        self.keep.start()
 
     def arrival(self, s):
         return push(self.src, self.full.at[s], self.send.at[0], self.recv.at[s], {"dp": self.sibling})
@@ -232,7 +233,6 @@
         self.arrival(self.diagonal).wait_recv()
         for kind in range(3):
             self.copy(kind).wait_send()
-        self.keep.wait()
 
 
 def lane_masks(rows):
@@ -278,7 +278,7 @@
 
     toks = Spread(tok, held, tok_send, tok_recv, 2)
     toks.start()
-    later = Weights(wqkv, 0, shard // 2, wfirst, q_send, q_recv, copy_sem.at[7])
+    later = Weights(wqkv, 0, shard // 2, wfirst, q_send, q_recv)
     for cp in own_w:
         cp.wait()
 
@@ -465,7 +465,7 @@
     zslots, dslots, olow, gain_ref, w1_hbm, w2_hbm,
     returned, came_back, olow_full, ggain_ref, n_out, h_out, df_out, du_out,
     w1, w2, x, hid, gpr, unit_s, inv_s, state, total, own, f1, rf1, ssum, rss,
-    zland, dland, zfar, dfar, bsend, gsend, ggain, gland,
+    zland, dland, zfar, dfar, bsend, gsend, ggain, gland, olow_held,
     x_send, x_recv, f_send, f_recv, s_send, s_recv, l_send, l_recv,
     a_send, a_recv, g_send, g_recv, copy_sem, own_sem, e_send, e_recv,
 ):
@@ -532,9 +532,14 @@
         for c in ((1, 2, 3, 0) if which == 0 else (3, 2, 1, 0)):
             for_places(c, lambda q: swap(src, dst, which, q).start(), lambda: swap_own(src, dst, which).start())
     olows = Spread(olow, olow_full, g_send, g_recv, 1)
-    own_o = pltpu.make_async_copy(olow, olow_full.at[e], copy_sem.at[12])
-    own_o.start()
+    take_o = pltpu.make_async_copy(olow, olow_held, copy_sem.at[12])
+    take_o.start()
+    own_o = pltpu.make_async_copy(olow_held, olow_full.at[e], copy_sem.at[12])
     layer_of = (0, 1, 1, 0)
+    order = [(p, c if p < 2 else 3 - c) for p in range(4) for c in range(4)]
+
+    def place(p, c):
+        return order.index((p, c)) % 4
 
     def my_half(c):
         return pl.ds(c * chunk, pair)
@@ -597,37 +602,48 @@
         x[2, pl.ds(c * chunk + theirs, quarter), :] = both(dfar, c).astype(BF)
         x_copy(2, c).start()
 
-    def compute(p, c):
+    def up(p, c):
         k = layer_of[p]
         base = pl.ds(c * chunk, chunk)
-        left_w, right_w = (w1, w2) if p < 2 else (w2, w1)
+        left_w = w1 if p < 2 else w2
+        x_copy(p, c).wait_recv()
+
+        def gelu(t, pre):
+            cols = pl.ds(pl.multiple_of(t * TILE, TILE), TILE)
+            cdf = 0.5 * (1.0 + lax.erf(pre * (0.5 ** 0.5)))
+            pdf = jnp.exp(-0.5 * pre * pre) * 0.3989422804014327
+            hid[k, base, cols] = (pre * cdf).astype(BF)
+            gpr[k, base, cols] = cdf + pre * pdf
+
+        def product(t):
+            cols = pl.ds(pl.multiple_of(t * TILE, TILE), TILE)
+            return lax.dot_general(x[p, base, :], left_w[k, cols, :], NT, preferred_element_type=F32)
+
+        def step(t, carry):
+            if p < 2:
+                gelu(t, product(t))
+            else:
+                cols = pl.ds(pl.multiple_of(t * TILE, TILE), TILE)
+                hid[2 + k, base, cols] = (product(t) * gpr[k, base, cols]).astype(BF)
+            return carry
+
+        lax.fori_loop(0, tiles, step, 0)
+
+    def down(p, c):
+        k = layer_of[p]
+        base = pl.ds(c * chunk, chunk)
+        right_w = w2 if p < 2 else w1
         q = 4 * p + c
-        x_copy(p, c).wait_recv()
-
-        def up(t, carry):
+
+        def step(t, carry):
             cols = pl.ds(pl.multiple_of(t * TILE, TILE), TILE)
-            pre = lax.dot_general(x[p, base, :], left_w[k, cols, :], NT, preferred_element_type=F32)
-            if p < 2:
-                cdf = 0.5 * (1.0 + lax.erf(pre * (0.5 ** 0.5)))
-                pdf = jnp.exp(-0.5 * pre * pre) * 0.3989422804014327
-                hid[k, base, cols] = (pre * cdf).astype(BF)
-                gpr[k, base, cols] = cdf + pre * pdf
-            else:
-                hid[2 + k, base, cols] = (pre * gpr[k, base, cols]).astype(BF)
-            return carry
-
-        lax.fori_loop(0, tiles, up, 0)
-        slot = k if p < 2 else 2 + k
-
-        def down(t, carry):
-            cols = pl.ds(pl.multiple_of(t * TILE, TILE), TILE)
-            res = jnp.dot(hid[slot, base, :], right_w[k, :, cols], preferred_element_type=F32)
-            own[c, :, cols] = res[:pair]
+            res = jnp.dot(hid[k if p < 2 else 2 + k, base, :], right_w[k, :, cols], preferred_element_type=F32)
+            own[place(p, c), :, cols] = res[:pair]
             f1[q, :, cols] = res[pair:].astype(BF)
             f_copy(q, cols).start()
             return carry
 
-        lax.fori_loop(0, tiles, down, 0)
+        lax.fori_loop(0, tiles, step, 0)
 
     everything = pl.ds(0, width)
 
@@ -637,8 +653,8 @@
 
         def act(t):
             rs = pl.ds(t, 32)
-            v = own[c, rs, :] + rf1[q, rs, :].astype(F32)
-            own[c, rs, :] = v
+            v = own[place(p, c), rs, :] + rf1[q, rs, :].astype(F32)
+            own[place(p, c), rs, :] = v
             ssum[q, rs, :] = v.astype(BF)
         by_rows(act)
         s_copy(p, c).start()
@@ -649,7 +665,7 @@
         for_places(c, lambda q: swap(buf, dst, which, q).start(), lambda: swap_own(buf, dst, which).start())
 
     def add_gain(k, c, part):
-        if c == 0:
+        if c == 3:
             ggain[pl.ds(k, 1), :] = part
         else:
             ggain[pl.ds(k, 1), :] = ggain[pl.ds(k, 1), :] + part
@@ -667,7 +683,7 @@
         if p == 0:
             def read(t):
                 rs = pl.ds(c * pair + t, 32)
-                got = own[c, pl.ds(t, 32), :] + rss[q, pl.ds(t, 32), :].astype(F32)
+                got = own[place(p, c), pl.ds(t, 32), :] + rss[q, pl.ds(t, 32), :].astype(F32)
                 total[rs, :] = got
                 return state[rs, :] + got
             norm_rows(1, c, read)
@@ -675,7 +691,7 @@
             def step(i, part):
                 t = pl.multiple_of(i * 32, 32)
                 rs = pl.ds(c * pair + t, 32)
-                got = own[c, pl.ds(t, 32), :] + rss[q, pl.ds(t, 32), :].astype(F32)
+                got = own[place(p, c), pl.ds(t, 32), :] + rss[q, pl.ds(t, 32), :].astype(F32)
                 back, add = norm_back(1, got, rs)
                 state[rs, :] = back
                 at = pl.ds(c * chunk + t, 32)
@@ -687,7 +703,7 @@
         else:
             at = pl.ds(mine, quarter)
             rs = pl.ds(c * pair + mine, quarter)
-            got = own[c, at, :] + rss[q, at, :].astype(F32)
+            got = own[place(p, c), at, :] + rss[q, at, :].astype(F32)
             if p == 1:
                 give_back(bsend, returned, 2, c, total[rs, :] + got)
             else:
@@ -711,28 +727,31 @@
     begin(0)
     loads[0].wait()
     loads[1].wait()
-    for t in range(16):
-        p, c = divmod(t, 4)
+    for t, (p, c) in enumerate(order):
         if t == 4:
             loads[2].wait()
             loads[3].wait()
-        compute(p, c)
+        up(p, c)
+        if t > 0:
+            send_sum(*order[t - 1])
         if t < 2:
             forward(0, t + 2)
+        down(p, c)
         if 2 <= t < 6:
-            forward(1, t - 2)
+            forward(1, 5 - t)
         if t < 3:
             begin(t + 1)
         if t >= 2:
-            finish(*divmod(t - 2, 4))
-        send_sum(p, c)
+            finish(*order[t - 2])
         if 5 <= t < 9:
-            begin_back(t - 5)
+            begin_back(8 - t)
         if t == 2:
             olows.start()
+            take_o.wait()
+            own_o.start()
         if t in (5, 8, 11):
             olows.step((t - 2) // 3)
-        if c == 3:
+        if t % 4 == 3:
             k = layer_of[p]
             if p < 2:
                 store(p * 2, x.at[p], n_out.at[k])
@@ -740,8 +759,9 @@
             else:
                 store(p * 2, x.at[p], df_out.at[k])
                 store(p * 2 + 1, hid.at[2 + k], du_out.at[k])
-    finish(3, 2)
-    finish(3, 3)
+    send_sum(*order[15])
+    finish(*order[14])
+    finish(*order[15])
     for i in range(3):
         gain_copy(i).start()
     gland[j] = ggain[:, pl.ds(pl.multiple_of(j * shard, shard), shard)]
@@ -798,7 +818,7 @@
         ]
         + [V((16, pair, width), BF)] * 4
         + [V(zslots.shape, BF)] * 6
-        + [V((2, width), F32), V((4, 2, width // 4), F32)]
+        + [V((2, width), F32), V((4, 2, width // 4), F32), V(olow.shape, BF)]
         + [D((16,))] * 6 + [D((8,))] * 2
         + [D((32,)), D((32,)), D((11,)), D((8,)), D((13,)), D((4,)), D((3,)), D((4,))],
         compiler_params=pltpu.CompilerParams(
@@ -848,35 +868,37 @@
         head_copy(gatt, dam, 1, dest).start()
     for dest in peers:
         push(cent.at[dest], cland.at[e], c_send.at[dest], c_recv.at[e], {"expert": dest}).start()
-    later = Weights(wqkv, shard // 2, shard // 2, wsecond, q_send, q_recv, copy_sem.at[8])
+    later = Weights(wqkv, shard // 2, shard // 2, wsecond, q_send, q_recv)
     later.start()
     dom[rows_of(e), :] = gmix[:, cols_of(e)]
     dam[rows_of(e), :] = gatt[:, cols_of(e)]
     cland[e] = cent[e]
 
-    def dp_sum_start(buf, n, t):
-        def block(s):
-            return buf[0:n, pl.ds(pl.multiple_of(s * shard, shard), shard)]
-        f3[t, 0:n, :] = block(diagonal).astype(BF)
-        f1[t, 0:n, :] = block(sibling).astype(BF)
-        dp_copy(1, n, t).start()
-        dp_copy(0, n, t).start()
-        dp_copy(1, n, t).wait_recv()
-        ssum[t, 0:n, :] = (block(across) + rf3[t, 0:n, :].astype(F32)).astype(BF)
-        dp_copy(2, n, t).start()
-
-    def dp_copy(kind, n, t):
-        at = pl.ds(0, n)
+    def dp_block(t, s):
+        return part[pl.ds(max(t - 1, 0) * lanes, lanes), pl.ds(pl.multiple_of(s * shard, shard), shard)]
+
+    def dp_copy(kind, t):
         if kind == 0:
-            return push(f1.at[t, at], rf1.at[t, at], p_send.at[t * 3], p_recv.at[t * 3], {"dp": sibling})
+            return push(f1.at[t], rf1.at[t], p_send.at[t * 3], p_recv.at[t * 3], {"dp": sibling})
         if kind == 1:
-            return push(f3.at[t, at], rf3.at[t, at], p_send.at[t * 3 + 1], p_recv.at[t * 3 + 1], {"dp": sibling})
-        return push(ssum.at[t, at], rss.at[t, at], p_send.at[t * 3 + 2], p_recv.at[t * 3 + 2], {"dp": across})
-
-    def dp_sum_end(buf, n, t):
-        dp_copy(0, n, t).wait_recv()
-        dp_copy(2, n, t).wait_recv()
-        return buf[0:n, pl.ds(pl.multiple_of(j * shard, shard), shard)] + rf1[t, 0:n, :].astype(F32) + rss[t, 0:n, :].astype(F32)
+            return push(f3.at[t], rf3.at[t], p_send.at[t * 3 + 1], p_recv.at[t * 3 + 1], {"dp": sibling})
+        return push(ssum.at[t], rss.at[t], p_send.at[t * 3 + 2], p_recv.at[t * 3 + 2], {"dp": across})
+
+    def dp_sum_start(t):
+        f3[t] = dp_block(t, diagonal).astype(BF)
+        f1[t] = dp_block(t, sibling).astype(BF)
+        dp_copy(1, t).start()
+        dp_copy(0, t).start()
+
+    def dp_sum_cross(t):
+        dp_copy(1, t).wait_recv()
+        ssum[t] = (dp_block(t, across) + rf3[t].astype(F32)).astype(BF)
+        dp_copy(2, t).start()
+
+    def dp_sum_end(t):
+        dp_copy(0, t).wait_recv()
+        dp_copy(2, t).wait_recv()
+        return (dp_block(t, j) + rf1[t].astype(F32) + rss[t].astype(F32)).T.astype(BF)
 
     for cp in loads[:2]:
         cp.wait()
@@ -943,9 +965,10 @@
             for source in peers:
                 head_arrival(gatt, dam, 1, source).wait_recv()
             part[0:lanes, :] = lax.dot_general(dam[...], olow[...], TN, preferred_element_type=F32)
-            dp_sum_start(part, lanes, 0)
+            dp_sum_start(0)
+            dp_sum_cross(0)
         if b == 1:
-            go_own[...] = dp_sum_end(part, lanes, 0).T.astype(BF)
+            go_own[...] = dp_sum_end(0)
             gos = Spread(go_own, go_land, go_send, go_recv, 1)
             gos.start()
             own_go = pltpu.make_async_copy(go_own, go_land.at[e], copy_sem.at[5])
@@ -958,12 +981,18 @@
             own_gc = pltpu.make_async_copy(csum.at[1, :, pl.ds(0, shard)], gc_land.at[e], copy_sem.at[6])
             own_gc.start()
     loads[3].wait()
-    part[...] = lax.dot_general(dqkv[...], normed[...], TN, preferred_element_type=F32)
-    dp_sum_start(part, 3 * lanes, 1)
+    gqs = Spread(gq_own, gq_land, gq_send, gq_recv, 3)
+    for g in range(3):
+        at = pl.ds(g * lanes, lanes)
+        part[at, :] = lax.dot_general(dqkv[:, at], normed[...], TN, preferred_element_type=F32)
+        dp_sum_start(g + 1)
+        if g > 0:
+            dp_sum_cross(g)
+    dp_sum_cross(3)
     gos.step(1)
-    gq_own[...] = dp_sum_end(part, 3 * lanes, 1).T.astype(BF)
-    gqs = Spread(gq_own, gq_land, gq_send, gq_recv, 2)
-    gqs.start()
+    for g in range(3):
+        gq_own[pl.ds(g * shard, shard), :] = dp_sum_end(g + 1)
+        gqs.start_chunk(g)
     own_gq = pltpu.make_async_copy(gq_own, gq_land.at[e], copy_sem.at[7])
     own_gq.start()
     gos.step(2)
@@ -994,8 +1023,8 @@
         push(cent.at[dest], cland.at[e], c_send.at[dest], c_recv.at[e], {"expert": dest}).wait_send()
     for i in range(3):
         c_copy(i).wait_send()
-        dp_copy(i, lanes, 0).wait_send()
-        dp_copy(i, 3 * lanes, 1).wait_send()
+        for t in range(4):
+            dp_copy(i, t).wait_send()
     for cp in (own_go, own_gc, own_gq):
         cp.wait()
 
@@ -1012,7 +1041,7 @@
     return pl.pallas_call(
         back_kernel,
         out_shape=(
-            S((8, rows, 384), BF), S((8, shard, 384), BF), S((8, shard, 128), BF), S((8, 1, shard), F32),
+            S((8, rows, 384), BF), S((8, 3 * shard, 128), BF), S((8, shard, 128), BF), S((8, 1, shard), F32),
             S((4, shard // 2, 3 * width), BF),
         ),
         in_specs=[vmem_spec, vmem_spec, any_spec, any_spec, vmem_spec, any_spec, any_spec, vmem_spec, any_spec],
@@ -1022,10 +1051,10 @@
             V((8, seq), F32), V((seq, 128), F32), V((seq, 384), BF),
             V((384, width), F32),
         ]
-        + [V((2, 384, shard), BF)] * 6
+        + [V((4, 128, shard), BF)] * 6
         + [
-            V((shard, 384), BF), V((shard, 128), BF), V((8, 1, width), F32), V((2, 1, width), F32), V((4, 1, shard), F32),
-            D((16,)), D((16,)), D((8,)), D((8,)), D((6,)), D((6,)), D((22,)), D((16,)), D((11,)), D((8,)), D((20,)), D((20,)), D((9,)), D((3,)), D((4,)),
+            V((3 * shard, 128), BF), V((shard, 128), BF), V((8, 1, width), F32), V((2, 1, width), F32), V((4, 1, shard), F32),
+            D((16,)), D((16,)), D((8,)), D((8,)), D((12,)), D((12,)), D((33,)), D((24,)), D((11,)), D((8,)), D((20,)), D((20,)), D((9,)), D((3,)), D((4,)),
         ],
         compiler_params=pltpu.CompilerParams(collective_id=3, has_side_effects=True, vmem_limit_bytes=56 * 1024 * 1024),
         name="back_block",
@@ -1055,9 +1084,12 @@
         pairs.append([load(2 * i + k, src.at[k], dst.at[k]) for k in range(2)])
     first = [load(8, dq_hbm, dq_land), load(9, gq_hbm, gq_land), load(10, go_hbm, go_land), load(11, wqkv_hbm, wqkv)]
     rest = [load(12, tok_hbm, tok), load(13, gres_hbm, gres)]
-    for s in range(4):
-        rest.append(load(14 + 2 * s, wfirst.at[s], w.at[s, pl.ds(0, half)]))
-        rest.append(load(15 + 2 * s, wsecond.at[s], w.at[s, pl.ds(half, half)]))
+    me = lax.axis_index("dp")
+    for i in range(1, 4):
+        s = lax.rem(me + i, 4)
+        rest.append(load(12 + 2 * i, wfirst.at[s], w.at[s, pl.ds(0, half)]))
+        rest.append(load(13 + 2 * i, wsecond.at[s], w.at[s, pl.ds(half, half)]))
+    rest.append(load(20, wqkv_hbm, w.at[me]))
 
     def tile_copy(stage, out, base, k, t):
         at = pl.ds(pl.multiple_of(t * TILE, TILE), TILE)
@@ -1083,7 +1115,7 @@
         for i in range(3):
             at = pl.ds(i * width + s * 128, 128)
             dqkv[:, at] = dq_land[s, :, pl.ds(i * 128, 128)]
-            gqkv[:, at] = gq_land[s, :, pl.ds(i * 128, 128)].astype(F32)
+            gqkv[:, at] = gq_land[s, pl.ds(i * shard, shard), :].astype(F32)
         gout[:, pl.ds(s * 128, 128)] = go_land[s].astype(F32)
     stores = [
         pltpu.make_async_copy(gqkv, gqkv_hbm, store_sem.at[0]),
@@ -1119,7 +1151,7 @@
         return c
 
     lax.fori_loop(0, 3 * width // 256, add, 0)
-    own_gain = gain_col[pl.ds(lax.axis_index("dp"), 1), :]
+    own_gain = gain_col[pl.ds(me, 1), :]
     sums = lax.dot_general(jnp.ones((8, 128), F32), small_sum[...], NT, precision=HIGH, preferred_element_type=F32)
     gnorm[...] = sums[0:1] / own_gain
     for s in range(8):
@@ -1157,7 +1189,7 @@
             V(gq_land.shape, BF), V(go_land.shape, BF), V((shard, 3 * width), BF),
             V((rows, 3 * width), BF), V((rows, width), F32), V((rows, width), F32),
             V((shard, 3 * width), F32), V((shard, width), F32), V((shard, 128), F32),
-            D((22,)), D((16,)), D((3,)),
+            D((21,)), D((16,)), D((3,)),
         ],
         compiler_params=pltpu.CompilerParams(vmem_limit_bytes=58 * 1024 * 1024),
         name="final_block",

time: 246 us -> 242 us (0.984)
  Pallas kernels: 230 us -> 226 us
where the time goes in v5:
time: 242 us; the launch traced here: 241 us
  Pallas kernels  226 us (93%)
  matrix products  10.8 us (4%)
  local copies, waits for them, and re-layouts  2.82 us (1%)
    pallas_call x1, Pallas kernels, expert_block(): pl.pallas_call(expert_kernel, out_shape=(S(zslots.shape, BF), S(zslots.sh...  91.6 us
    pallas_call x1, Pallas kernels, back_block(): pl.pallas_call(back_kernel, out_shape=(S((8, rows, 384), BF), S((8, 3 * s...  66.7 us
    pallas_call x1, Pallas kernels, front_block(): pl.pallas_call(front_kernel, out_shape=(S((rows, width), BF), S((seq, wid...  48.5 us
    pallas_call x1, Pallas kernels, final_block(): pl.pallas_call(final_kernel, out_shape=(S((rows, width), F32), S((shard,...  19.2 us

profile of v5, /device:TPU:0, one launch (start us, length us, event | category | flops | bytes accessed | tf_op | source)
XLA Modules:
  0.0 241.3 jit_solution(1646064334841422998)
XLA Ops:
  0.6 0.0 copy-start.1
  0.7 0.0 copy-start.4
  0.7 1.0 fusion
  1.6 0.7 convert_add_fusion.1
  2.3 1.2 broadcast_in_dim.29.norm_gain
  3.5 48.5 %front_block.1 = (bf16[128,1024]{1,0:T(8,128)(2,1)}, bf16[1024,1024]{1,0:T(8,128)(2,1)}, bf16[1024,384]{1,0:T(8,128)(2,1)}, f32[1024,128]{1,0:T(8,128)}, bf16[10...) custom-call(bf16[128,1024]{1,0:T(8,128)(2,1)} %tok_hbm.1, ...), custom_call_target="tpu_custom_call" | custom-call | tf_op jit(solution)/shard_map/front_block/pallas_call | solution.py:444
  52.1 0.0 copy-done.4
  52.1 1.0 fusion.19
  53.1 0.0 copy-done.1
  53.1 0.0 copy-start.3
  53.1 2.3 fusion.27
  55.4 0.0 copy-done.3
  55.4 0.1 fusion.1
  55.5 0.4 convolution_convert_fusion
  55.9 0.9 fusion.26
  56.8 91.6 %expert_block.1 = (bf16[8,24,1024]{2,1,0:T(8,128)(2,1)}, bf16[8,24,1024]{2,1,0:T(8,128)(2,1)}, bf16[8,128,1024]{2,1,0:T(8,128)(2,1)}, f32[2,256]{1,0:T(2,128)}, ...) custom-call(bf16[8,24,1024]{2,1,0:T(8,128)(2,1)} %bitcast.20, ...), custom_call_target="tpu_custom_call" | custom-call | tf_op jit(solution)/shard_map/expert_block/pallas_call | solution.py:805
  148.4 0.0 copy-start
  148.4 2.2 fusion.2
  150.6 0.4 fusion.6
  151.0 0.6 broadcast_in_dim.32.cent
  151.7 2.1 fusion.28
  153.7 1.6 convolution_convert_fusion.1.gmix
  155.3 66.7 %back_block.1 = (bf16[8,128,384]{2,1,0:T(8,128)(2,1)}, bf16[8,768,128]{2,1,0:T(8,128)(2,1)}, bf16[8,256,128]{2,1,0:T(8,128)(2,1)}, f32[8,1,256]{2,1,0:T(1,128)}, bf16[4,128,3072]{2,1,0:T(8,128)(2,1)}) custom-call(bf16[128,1024]{1,0:T(8,128)(2,1)} %convolution_convert_fusion.1.gmix, bf16[128,1024]{1,0:T(8,128)(2,1)} %copy-done.2, ...), custom_call_target="tpu_custom_call" | custom-call | tf_op jit(solution)/shard_map/back_block/pallas_call | solution.py:1041
  222.0 19.2 %final_block.1 = (f32[128,1024]{1,0:T(8,128)}, f32[256,3072]{1,0:T(8,128)}, f32[256,1024]{1,0:T(8,128)}, f32[1,256]{1,0:T(1,128)}, f32[8,256]{1,0:T(8,128)}, /*i...) custom-call(bf16[8,128,384]{2,1,0:T(8,128)(2,1)} %get-tuple-element.51.dq_hbm, ...), custom_call_target="tpu_custom_call" | custom-call | tf_op jit(solution)/shard_map/final_block/pallas_call | solution.py:1177
  (6 shorter events, 0.0 us)
Async XLA Ops:
  0.6 52.4 %copy-start.1 = (bf16[128,1024]{1,0:T(8,128)(2,1)S(1)}, bf16[128,1024]{1,0:T(8,128)(2,1)}, u32[]{:S(2)}) copy-start(bf16[128,1024]{1,0:T(8,128)(2,1)} %tok_hbm.1) | copy-start | bytes 786436
  0.7 51.4 %copy-start.4 = (s32[128,1]{0,1:T(1,128)S(1)}, s32[128,1]{0,1:T(1,128)}, u32[]{:S(2)}) copy-start(s32[128,1]{0,1:T(1,128)} %param.18) | copy-start | bytes 1540
  53.1 2.3 copy-start.3
  148.4 5.3 %copy-start = (bf16[1024,1024]{1,0:T(8,128)(2,1)S(1)}, bf16[1024,1024]{1,0:T(8,128)(2,1)}, u32[]{:S(2)}) copy-start(bf16[1024,1024]{1,0:T(8,128)(2,1)} %get-tuple-element.41) | copy-start | bytes 6291460
  153.7 1.6 copy-start.2

commit v6 on v5

--- a/solution.py
+++ b/solution.py
@@ -829,11 +829,12 @@
 
 
 def back_kernel(
-    gmix, gatt, qkv_hbm, mixed_hbm, lse_rows, normed_hbm, olow_hbm, cent, wqkv,
-    dq_land, gq_land, go_land, gc_land, wsecond,
+    gmix, gatt, qkv_hbm, mixed_hbm, lse_rows, normed_hbm, olow_hbm, cent, wqkv, wfirst_hbm,
+    dnorm_hbm, gq_land, go_land, gc_land,
     dom, dam, qkv, mixed, normed, olow, delta, dq_acc, dqkv,
     part, f1, f3, ssum, rf1, rf3, rss, gq_own, go_own, cland, csum, cdp,
     h_send, h_recv, d_send, d_recv, p_send, p_recv, gq_send, gq_recv, go_send, go_recv, c_send, c_recv, copy_sem, q_send, q_recv,
+    dq_land, wfirst, wsecond, dq_rows, dnorm, n_sem,
 ):
     j, sibling, across, diagonal = dp_peers()
     e, zpos, xpos, beside, zs = expert_peers()
@@ -846,6 +847,16 @@
         for i, (src, dst) in enumerate([(qkv_hbm, qkv), (mixed_hbm, mixed), (olow_hbm, olow), (normed_hbm, normed)])
     ]
     for cp in loads:
+        cp.start()
+    half = shard // 2
+    weights = [
+        pltpu.make_async_copy(wqkv.at[pl.ds(0, half)], wfirst.at[j], n_sem.at[0]),
+        pltpu.make_async_copy(wqkv.at[pl.ds(half, half)], wsecond.at[j], n_sem.at[1]),
+    ]
+    for i in range(1, 4):
+        s = lax.rem(j + i, 4)
+        weights.append(pltpu.make_async_copy(wfirst_hbm.at[s], wfirst.at[s], n_sem.at[1 + i]))
+    for cp in weights:
         cp.start()
     peers = others(8, e)
     greet([{"expert": p} for p in peers] + [{"dp": p} for p in (sibling, across, diagonal)])
@@ -959,7 +970,7 @@
 
             @pl.when(dest == e)
             def _():
-                pltpu.make_async_copy(dqkv.at[pl.ds(dest * rows, rows)], dq_land.at[dest], copy_sem.at[4]).start()
+                dq_land[dest] = dqkv[pl.ds(dest * rows, rows), :]
         if b == 0:
             loads[2].wait()
             for source in peers:
@@ -981,6 +992,7 @@
             own_gc = pltpu.make_async_copy(csum.at[1, :, pl.ds(0, shard)], gc_land.at[e], copy_sem.at[6])
             own_gc.start()
     loads[3].wait()
+    later.relay()
     gqs = Spread(gq_own, gq_land, gq_send, gq_recv, 3)
     for g in range(3):
         at = pl.ds(g * lanes, lanes)
@@ -996,27 +1008,36 @@
     own_gq = pltpu.make_async_copy(gq_own, gq_land.at[e], copy_sem.at[7])
     own_gq.start()
     gos.step(2)
-    later.relay()
     gqs.step(1)
     gos.step(3)
+    later.drain()
+    for cp in weights:
+        cp.wait()
+    for source in peers:
+        push(dqkv.at[pl.ds(0, rows)], dq_land.at[source], d_send.at[source], d_recv.at[source], {"expert": source}).wait_recv()
+    for s in range(8):
+        for i in range(3):
+            dq_rows[:, pl.ds(i * width + s * lanes, lanes)] = dq_land[s, :, pl.ds(i * lanes, lanes)]
     gqs.step(2)
+    for s in range(4):
+        for side, w in enumerate((wfirst, wsecond)):
+            at = pl.ds(s * shard + side * half, half)
+            dnorm[:, at] = lax.dot_general(dq_rows[...], w[s], NT, preferred_element_type=F32)
+    own_dnorm = pltpu.make_async_copy(dnorm, dnorm_hbm, copy_sem.at[4])
+    own_dnorm.start()
     gqs.step(3)
     for zz in range(4):
         gos.wait_beside(zz)
         gqs.wait_beside(zz)
     gos.drain()
     gqs.drain()
-    later.drain()
+    own_dnorm.wait()
     for source in range(8):
         @pl.when(source != e)
         def _():
-            push(dqkv.at[pl.ds(0, rows)], dq_land.at[source], d_send.at[source], d_recv.at[source], {"expert": source}).wait_recv()
             d_copy(source).wait_send()
             push(csum.at[1, :, pl.ds(0, shard)], gc_land.at[source], c_send.at[12 + source], c_recv.at[12 + source], {"expert": source}).wait()
 
-        @pl.when(source == e)
-        def _():
-            pltpu.make_async_copy(dqkv.at[pl.ds(0, rows)], dq_land.at[source], copy_sem.at[4]).wait()
     for dest in peers:
         head_copy(gmix, dom, 0, dest).wait_send()
         head_copy(gatt, dam, 1, dest).wait_send()
@@ -1029,7 +1050,7 @@
         cp.wait()
 
 
-def back_block(gmix, gatt, qkv, mixed, lse_rows, normed, olow_full, cent, qkv_weight):
+def back_block(gmix, gatt, qkv, mixed, lse_rows, normed, olow_full, cent, qkv_weight, wfirst):
     rows, width = gmix.shape
     seq = 8 * rows
     shard = width // 4
@@ -1041,11 +1062,10 @@
     return pl.pallas_call(
         back_kernel,
         out_shape=(
-            S((8, rows, 384), BF), S((8, 3 * shard, 128), BF), S((8, shard, 128), BF), S((8, 1, shard), F32),
-            S((4, shard // 2, 3 * width), BF),
+            S((rows, width), F32), S((8, 3 * shard, 128), BF), S((8, shard, 128), BF), S((8, 1, shard), F32),
         ),
-        in_specs=[vmem_spec, vmem_spec, any_spec, any_spec, vmem_spec, any_spec, any_spec, vmem_spec, any_spec],
-        out_specs=(any_spec,) * 5,
+        in_specs=[vmem_spec, vmem_spec, any_spec, any_spec, vmem_spec, any_spec, any_spec, vmem_spec, any_spec, any_spec],
+        out_specs=(any_spec,) * 4,
         scratch_shapes=[
             V((seq, 128), BF), V((seq, 128), BF), V((seq, 384), BF), V((seq, 128), F32), V((seq, width), BF), V((seq, width), BF),
             V((8, seq), F32), V((seq, 128), F32), V((seq, 384), BF),
@@ -1055,23 +1075,24 @@
         + [
             V((3 * shard, 128), BF), V((shard, 128), BF), V((8, 1, width), F32), V((2, 1, width), F32), V((4, 1, shard), F32),
             D((16,)), D((16,)), D((8,)), D((8,)), D((12,)), D((12,)), D((33,)), D((24,)), D((11,)), D((8,)), D((20,)), D((20,)), D((9,)), D((3,)), D((4,)),
+            V((8, rows, 384), BF), V((4, shard // 2, 3 * width), BF), V((4, shard // 2, 3 * width), BF),
+            V((rows, 3 * width), BF), V((rows, width), F32), D((5,)),
         ],
         compiler_params=pltpu.CompilerParams(collective_id=3, has_side_effects=True, vmem_limit_bytes=56 * 1024 * 1024),
         name="back_block",
-    )(gmix, gatt, qkv, mixed, lse_rows, normed, olow_full, cent, qkv_weight)
+    )(gmix, gatt, qkv, mixed, lse_rows, normed, olow_full, cent, qkv_weight, wfirst)
 
 
 def final_kernel(
-    dq_hbm, wfirst, wsecond, tok_hbm, gain_col, gres_hbm, gq_hbm, go_hbm, wqkv_hbm, gc_land, gain_part,
+    dnorm_hbm, tok_hbm, gain_col, gres_hbm, gq_hbm, go_hbm, wqkv_hbm, gc_land, gain_part,
     n_hbm, h_hbm, df_hbm, du_hbm,
     gtok_hbm, gqkv_hbm, gout_hbm, gnorm, gcent, ggain, gein, geout,
-    n, h, df, du, tile_in, tile_out, dq_land, w, tok, gres, gq_land, go_land, wqkv,
-    dqkv, dnorm, gtok, gqkv, gout, small_sum,
+    n, h, df, du, tile_in, tile_out, dnorm, tok, gres, gq_land, go_land, wqkv,
+    gtok, gqkv, gout, small_sum,
     load_sem, tile_sem, store_sem,
 ):
     rows, width = tok.shape
     shard = wqkv.shape[0]
-    half = shard // 2
     tiles = width // TILE
 
     def load(i, src, dst):
@@ -1082,14 +1103,9 @@
     pairs = []
     for i, (src, dst) in enumerate([(du_hbm, du), (n_hbm, n), (h_hbm, h), (df_hbm, df)]):
         pairs.append([load(2 * i + k, src.at[k], dst.at[k]) for k in range(2)])
-    first = [load(8, dq_hbm, dq_land), load(9, gq_hbm, gq_land), load(10, go_hbm, go_land), load(11, wqkv_hbm, wqkv)]
+    first = [load(8, dnorm_hbm, dnorm), load(9, gq_hbm, gq_land), load(10, go_hbm, go_land), load(11, wqkv_hbm, wqkv)]
     rest = [load(12, tok_hbm, tok), load(13, gres_hbm, gres)]
     me = lax.axis_index("dp")
-    for i in range(1, 4):
-        s = lax.rem(me + i, 4)
-        rest.append(load(12 + 2 * i, wfirst.at[s], w.at[s, pl.ds(0, half)]))
-        rest.append(load(13 + 2 * i, wsecond.at[s], w.at[s, pl.ds(half, half)]))
-    rest.append(load(20, wqkv_hbm, w.at[me]))
 
     def tile_copy(stage, out, base, k, t):
         at = pl.ds(pl.multiple_of(t * TILE, TILE), TILE)
@@ -1114,7 +1130,6 @@
     for s in range(8):
         for i in range(3):
             at = pl.ds(i * width + s * 128, 128)
-            dqkv[:, at] = dq_land[s, :, pl.ds(i * 128, 128)]
             gqkv[:, at] = gq_land[s, pl.ds(i * shard, shard), :].astype(F32)
         gout[:, pl.ds(s * 128, 128)] = go_land[s].astype(F32)
     stores = [
@@ -1125,8 +1140,6 @@
         cp.start()
     for cp in rest:
         cp.wait()
-    for s in range(4):
-        dnorm[:, pl.ds(s * shard, shard)] = lax.dot_general(dqkv[...], w[s], NT, preferred_element_type=F32)
     gain = jnp.concatenate([gain_col[s : s + 1, :] for s in range(4)], axis=1)
 
     def norm_rows(t, c):
@@ -1165,7 +1178,7 @@
             tile_copy(tile_out, geout, 2, k, t).wait()
 
 
-def final_block(dq_land, wfirst, wsecond, tokens, gain_col, grad_resid, gq_land, go_land, qkv_weight, gc_land, gain_part, n, h, df, du):
+def final_block(dnorm, tokens, gain_col, grad_resid, gq_land, go_land, qkv_weight, gc_land, gain_part, n, h, df, du):
     rows, width = tokens.shape
     shard = width // 4
     hidden = h.shape[2]
@@ -1180,20 +1193,20 @@
             S((rows, width), F32), S((shard, 3 * width), F32), S((shard, width), F32), S((1, shard), F32),
             S((8, shard), F32), S((2, shard), F32), S((2, hidden, width), F32), S((2, hidden, width), F32),
         ),
-        in_specs=[any_spec] * 4 + [vmem_spec] + [any_spec] * 4 + [vmem_spec] * 2 + [any_spec] * 4,
+        in_specs=[any_spec] * 2 + [vmem_spec] + [any_spec] * 4 + [vmem_spec] * 2 + [any_spec] * 4,
         out_specs=(any_spec,) * 3 + (vmem_spec,) * 3 + (any_spec,) * 2,
         scratch_shapes=[V(n.shape, BF), V(h.shape, BF), V(df.shape, BF), V(du.shape, BF)]
         + [V((2, hidden, width), F32)] * 2
         + [
-            V(dq_land.shape, BF), V((4, shard, 3 * width), BF), V((rows, width), BF), V((rows, width), F32),
+            V((rows, width), F32), V((rows, width), BF), V((rows, width), F32),
             V(gq_land.shape, BF), V(go_land.shape, BF), V((shard, 3 * width), BF),
-            V((rows, 3 * width), BF), V((rows, width), F32), V((rows, width), F32),
+            V((rows, width), F32),
             V((shard, 3 * width), F32), V((shard, width), F32), V((shard, 128), F32),
-            D((21,)), D((16,)), D((3,)),
+            D((14,)), D((16,)), D((3,)),
         ],
         compiler_params=pltpu.CompilerParams(vmem_limit_bytes=58 * 1024 * 1024),
         name="final_block",
-    )(dq_land, wfirst, wsecond, tokens, gain_col, grad_resid, gq_land, go_land, qkv_weight, gc_land, gain_part, n, h, df, du)
+    )(dnorm, tokens, gain_col, grad_resid, gq_land, go_land, qkv_weight, gc_land, gain_part, n, h, df, du)
 
 
 def on_device_split(
@@ -1245,12 +1258,12 @@
     grad_resid = grad_out + grad_logit[:, None] * centroid_rows + back_rows
     grad_attended = grad_resid.astype(BF)
     grad_mixed = lax.dot_general(grad_attended, wout_full, NT, preferred_element_type=F32).astype(BF)
-    dq_land, gq_land, go_land, gc_land, wsecond = back_block(
+    dnormed, gq_land, go_land, gc_land = back_block(
         grad_mixed, grad_attended, qkv, mixed, lse_rows, normed_all,
-        olow_full.reshape(experts * rows, width), grad_centroid[:, None, :], qkv_weight,
+        olow_full.reshape(experts * rows, width), grad_centroid[:, None, :], qkv_weight, wfirst,
     )
     grad_tokens, grad_qkv, grad_out_weight, grad_norm_gain, grad_centroids, grad_gain, grad_expert_in, grad_expert_out = final_block(
-        dq_land, wfirst, wsecond, tokens, gain_col, grad_resid, gq_land, go_land, qkv_weight, gc_land, gain_part,
+        dnormed, tokens, gain_col, grad_resid, gq_land, go_land, qkv_weight, gc_land, gain_part,
         n_rows, h_rows, df_rows, du_rows,
     )
     return (

time: 242 us -> 239 us (0.988)
  Pallas kernels: 226 us -> 223 us
    pallas_call x1, Pallas kernels: 19.2 us -> 16.5 us  [final_block(): pl.pallas_call(final_kernel, out_shape=(S((rows, width), F32), S((shard,...]
where the time goes in v6:
time: 239 us
  Pallas kernels  223 us (93%)
  matrix products  10.8 us (5%)
  local copies, waits for them, and re-layouts  2.82 us (1%)
    pallas_call x1, Pallas kernels, expert_block(): pl.pallas_call(expert_kernel, out_shape=(S(zslots.shape, BF), S(zslots.sh...  91.5 us
    pallas_call x1, Pallas kernels, back_block(): pl.pallas_call(back_kernel, out_shape=(S((rows, width), F32), S((8, 3 * s...  66.7 us
    pallas_call x1, Pallas kernels, front_block(): pl.pallas_call(front_kernel, out_shape=(S((rows, width), BF), S((seq, wid...  48.5 us
    pallas_call x1, Pallas kernels, final_block(): pl.pallas_call(final_kernel, out_shape=(S((rows, width), F32), S((shard,...  16.5 us

profile of v6, /device:TPU:0, one launch (start us, length us, event | category | flops | bytes accessed | tf_op | source)
XLA Modules:
  0.0 238.6 jit_solution(5961785906765573267)
XLA Ops:
  0.6 0.0 copy-start.1
  0.7 0.0 copy-start.4
  0.7 1.0 fusion
  1.6 0.7 convert_add_fusion.1
  2.3 1.2 broadcast_in_dim.29.norm_gain
  3.5 48.5 %front_block.1 = (bf16[128,1024]{1,0:T(8,128)(2,1)}, bf16[1024,1024]{1,0:T(8,128)(2,1)}, bf16[1024,384]{1,0:T(8,128)(2,1)}, f32[1024,128]{1,0:T(8,128)}, bf16[10...) custom-call(bf16[128,1024]{1,0:T(8,128)(2,1)} %tok_hbm.1, ...), custom_call_target="tpu_custom_call" | custom-call | tf_op jit(solution)/shard_map/front_block/pallas_call | solution.py:444
  52.1 0.0 copy-done.4
  52.1 1.0 fusion.19
  53.1 0.0 copy-done.1
  53.1 0.0 copy-start.3
  53.1 2.3 fusion.27
  55.4 0.1 fusion.1
  55.5 0.4 convolution_convert_fusion
  55.9 0.9 fusion.26
  56.8 91.5 %expert_block.1 = (bf16[8,24,1024]{2,1,0:T(8,128)(2,1)}, bf16[8,24,1024]{2,1,0:T(8,128)(2,1)}, bf16[8,128,1024]{2,1,0:T(8,128)(2,1)}, f32[2,256]{1,0:T(2,128)}, ...) custom-call(bf16[8,24,1024]{2,1,0:T(8,128)(2,1)} %bitcast.20, ...), custom_call_target="tpu_custom_call" | custom-call | tf_op jit(solution)/shard_map/expert_block/pallas_call | solution.py:805
  148.4 0.0 copy-start
  148.4 2.2 fusion.2
  150.6 0.4 fusion.6
  151.0 0.6 broadcast_in_dim.32.cent
  151.6 2.1 fusion.28
  153.7 0.0 copy-done
  153.7 1.6 convolution_convert_fusion.1.gmix
  155.3 66.7 %back_block.1 = (f32[128,1024]{1,0:T(8,128)}, bf16[8,768,128]{2,1,0:T(8,128)(2,1)}, bf16[8,256,128]{2,1,0:T(8,128)(2,1)}, f32[8,1,256]{2,1,0:T(1,128)}) custom-call(bf16[128,1024]{1,0:T(8,128)(2,1)} %convolution_convert_fusion.1.gmix, bf16[128,1024]{1,0:T(8,128)(2,1)} %copy-done.2, bf16[1024,384]{1,0:T(8,128)(2,1)} %get-tuple-element.45.qkv_hbm, ...), custom_call_target="tpu_custom_call" | custom-call | tf_op jit(solution)/shard_map/back_block/pallas_call | solution.py:1062
  222.0 16.5 %final_block.1 = (f32[128,1024]{1,0:T(8,128)}, f32[256,3072]{1,0:T(8,128)}, f32[256,1024]{1,0:T(8,128)}, f32[1,256]{1,0:T(1,128)}, f32[8,256]{1,0:T(8,128)}, /*i...) custom-call(f32[128,1024]{1,0:T(8,128)} %get-tuple-element.51.dnorm_hbm, ...), custom_call_target="tpu_custom_call" | custom-call | tf_op jit(solution)/shard_map/final_block/pallas_call | solution.py:1190
  (6 shorter events, 0.0 us)
Async XLA Ops:
  0.6 52.4 %copy-start.1 = (bf16[128,1024]{1,0:T(8,128)(2,1)S(1)}, bf16[128,1024]{1,0:T(8,128)(2,1)}, u32[]{:S(2)}) copy-start(bf16[128,1024]{1,0:T(8,128)(2,1)} %tok_hbm.1) | copy-start | bytes 786436
  0.7 51.4 %copy-start.4 = (s32[128,1]{0,1:T(1,128)S(1)}, s32[128,1]{0,1:T(1,128)}, u32[]{:S(2)}) copy-start(s32[128,1]{0,1:T(1,128)} %param.18) | copy-start | bytes 1540
  53.1 2.3 copy-start.3
  148.4 5.4 %copy-start = (bf16[1024,1024]{1,0:T(8,128)(2,1)S(1)}, bf16[1024,1024]{1,0:T(8,128)(2,1)}, u32[]{:S(2)}) copy-start(bf16[1024,1024]{1,0:T(8,128)(2,1)} %get-tuple-element.40) | copy-start | bytes 6291460
  153.7 1.6 copy-start.2

commit v7 on v6

--- a/solution.py
+++ b/solution.py
@@ -829,12 +829,13 @@
 
 
 def back_kernel(
-    gmix, gatt, qkv_hbm, mixed_hbm, lse_rows, normed_hbm, olow_hbm, cent, wqkv, wfirst_hbm,
-    dnorm_hbm, gq_land, go_land, gc_land,
+    gmix, gatt, qkv_hbm, mixed_hbm, lse_rows, normed_hbm, olow_hbm, cent, wqkv, wfirst_hbm, n_hbm, h_hbm, df_hbm, du_hbm,
+    dnorm_hbm, gq_land, go_land, gc_land, grads_hbm,
     dom, dam, qkv, mixed, normed, olow, delta, dq_acc, dqkv,
     part, f1, f3, ssum, rf1, rf3, rss, gq_own, go_own, cland, csum, cdp,
     h_send, h_recv, d_send, d_recv, p_send, p_recv, gq_send, gq_recv, go_send, go_recv, c_send, c_recv, copy_sem, q_send, q_recv,
     dq_land, wfirst, wsecond, dq_rows, dnorm, n_sem,
+    lefts, rights, grads, m_sem, t_sem,
 ):
     j, sibling, across, diagonal = dp_peers()
     e, zpos, xpos, beside, zs = expert_peers()
@@ -856,10 +857,35 @@
     for i in range(1, 4):
         s = lax.rem(j + i, 4)
         weights.append(pltpu.make_async_copy(wfirst_hbm.at[s], wfirst.at[s], n_sem.at[1 + i]))
-    for cp in weights:
+    operands = []
+    for i in range(4):
+        k = i % 2
+        left, right = (du_hbm, n_hbm) if i < 2 else (h_hbm, df_hbm)
+        operands.append(pltpu.make_async_copy(left.at[k], lefts.at[i], m_sem.at[2 * i]))
+        operands.append(pltpu.make_async_copy(right.at[k], rights.at[i], m_sem.at[2 * i + 1]))
+    for cp in operands + weights:
         cp.start()
     peers = others(8, e)
     greet([{"expert": p} for p in peers] + [{"dp": p} for p in (sibling, across, diagonal)])
+
+    tiles = width // TILE
+
+    def grad_copy(i):
+        at = pl.ds(pl.multiple_of(i % tiles * TILE, TILE), TILE)
+        return pltpu.make_async_copy(grads.at[i // tiles, at], grads_hbm.at[i // tiles, at], t_sem.at[i])
+
+    def grad_tiles(first, last):
+        for cp in operands[2 * ((first + tiles - 1) // tiles) : 2 * ((last + tiles - 1) // tiles)]:
+            cp.wait()
+
+        def tile(i, c):
+            at = pl.ds(pl.multiple_of(i % tiles * TILE, TILE), TILE)
+            res = lax.dot_general(lefts[i // tiles, :, at], rights[i // tiles], TN, preferred_element_type=F32)
+            grads[i // tiles, at, :] = res.astype(BF)
+            grad_copy(i).start()
+            return c
+
+        lax.fori_loop(first, last, tile, 0)
 
     def cols_of(s):
         return pl.ds(pl.multiple_of(s * lanes, lanes), lanes)
@@ -913,6 +939,7 @@
 
     for cp in loads[:2]:
         cp.wait()
+    grad_tiles(0, 6)
     for source in peers:
         head_arrival(gmix, dom, 0, source).wait_recv()
     left_row = lax.broadcasted_iota(jnp.int32, (8, 128), 1) < HEAD
@@ -1002,14 +1029,17 @@
             dp_sum_cross(g)
     dp_sum_cross(3)
     gos.step(1)
+    grad_tiles(6, 9)
     for g in range(3):
         gq_own[pl.ds(g * shard, shard), :] = dp_sum_end(g + 1)
         gqs.start_chunk(g)
     own_gq = pltpu.make_async_copy(gq_own, gq_land.at[e], copy_sem.at[7])
     own_gq.start()
     gos.step(2)
+    grad_tiles(9, 12)
     gqs.step(1)
     gos.step(3)
+    grad_tiles(12, 16)
     later.drain()
     for cp in weights:
         cp.wait()
@@ -1032,6 +1062,8 @@
     gos.drain()
     gqs.drain()
     own_dnorm.wait()
+    for i in range(4 * tiles):
+        grad_copy(i).wait()
     for source in range(8):
         @pl.when(source != e)
         def _():
@@ -1050,7 +1082,7 @@
         cp.wait()
 
 
-def back_block(gmix, gatt, qkv, mixed, lse_rows, normed, olow_full, cent, qkv_weight, wfirst):
+def back_block(gmix, gatt, qkv, mixed, lse_rows, normed, olow_full, cent, qkv_weight, wfirst, n, h, df, du):
     rows, width = gmix.shape
     seq = 8 * rows
     shard = width // 4
@@ -1063,9 +1095,10 @@
         back_kernel,
         out_shape=(
             S((rows, width), F32), S((8, 3 * shard, 128), BF), S((8, shard, 128), BF), S((8, 1, shard), F32),
+            S((4, width, width), BF),
         ),
-        in_specs=[vmem_spec, vmem_spec, any_spec, any_spec, vmem_spec, any_spec, any_spec, vmem_spec, any_spec, any_spec],
-        out_specs=(any_spec,) * 4,
+        in_specs=[vmem_spec, vmem_spec, any_spec, any_spec, vmem_spec, any_spec, any_spec, vmem_spec] + [any_spec] * 6,
+        out_specs=(any_spec,) * 5,
         scratch_shapes=[
             V((seq, 128), BF), V((seq, 128), BF), V((seq, 384), BF), V((seq, 128), F32), V((seq, width), BF), V((seq, width), BF),
             V((8, seq), F32), V((seq, 128), F32), V((seq, 384), BF),
@@ -1077,17 +1110,18 @@
             D((16,)), D((16,)), D((8,)), D((8,)), D((12,)), D((12,)), D((33,)), D((24,)), D((11,)), D((8,)), D((20,)), D((20,)), D((9,)), D((3,)), D((4,)),
             V((8, rows, 384), BF), V((4, shard // 2, 3 * width), BF), V((4, shard // 2, 3 * width), BF),
             V((rows, 3 * width), BF), V((rows, width), F32), D((5,)),
+            V((4,) + h.shape[1:], BF), V((4,) + n.shape[1:], BF), V((4, width, width), BF), D((8,)), D((16,)),
         ],
         compiler_params=pltpu.CompilerParams(collective_id=3, has_side_effects=True, vmem_limit_bytes=56 * 1024 * 1024),
         name="back_block",
-    )(gmix, gatt, qkv, mixed, lse_rows, normed, olow_full, cent, qkv_weight, wfirst)
+    )(gmix, gatt, qkv, mixed, lse_rows, normed, olow_full, cent, qkv_weight, wfirst, n, h, df, du)
 
 
 def final_kernel(
     dnorm_hbm, tok_hbm, gain_col, gres_hbm, gq_hbm, go_hbm, wqkv_hbm, gc_land, gain_part,
-    n_hbm, h_hbm, df_hbm, du_hbm,
+    grads_hbm,
     gtok_hbm, gqkv_hbm, gout_hbm, gnorm, gcent, ggain, gein, geout,
-    n, h, df, du, tile_in, tile_out, dnorm, tok, gres, gq_land, go_land, wqkv,
+    grads, wide, dnorm, tok, gres, gq_land, go_land, wqkv,
     gtok, gqkv, gout, small_sum,
     load_sem, tile_sem, store_sem,
 ):
@@ -1100,31 +1134,26 @@
         cp.start()
         return cp
 
-    pairs = []
-    for i, (src, dst) in enumerate([(du_hbm, du), (n_hbm, n), (h_hbm, h), (df_hbm, df)]):
-        pairs.append([load(2 * i + k, src.at[k], dst.at[k]) for k in range(2)])
+    parts = [load(i, grads_hbm.at[i], grads.at[i]) for i in range(4)]
     first = [load(8, dnorm_hbm, dnorm), load(9, gq_hbm, gq_land), load(10, go_hbm, go_land), load(11, wqkv_hbm, wqkv)]
     rest = [load(12, tok_hbm, tok), load(13, gres_hbm, gres)]
     me = lax.axis_index("dp")
 
-    def tile_copy(stage, out, base, k, t):
+    def grad_copy(i, t):
+        out = gein if i < 2 else geout
         at = pl.ds(pl.multiple_of(t * TILE, TILE), TILE)
-        return pltpu.make_async_copy(stage.at[k, at], out.at[k, at], tile_sem.at[(base + k) * tiles + t])
-
-    for base, left, right, stage, out, waits in (
-        (0, du, n, tile_in, gein, pairs[:2]), (2, h, df, tile_out, geout, pairs[2:]),
-    ):
-        for k in range(2):
-            for pair in waits:
-                pair[k].wait()
-
-            def tile(t, c):
-                at = pl.ds(pl.multiple_of(t * TILE, TILE), TILE)
-                stage[k, at, :] = lax.dot_general(left[k, :, at], right[k], TN, preferred_element_type=F32)
-                tile_copy(stage, out, base, k, t).start()
-                return c
-
-            lax.fori_loop(0, tiles, tile, 0)
+        return pltpu.make_async_copy(wide.at[i, at], out.at[i % 2, at], tile_sem.at[i * tiles + t])
+
+    for i in range(4):
+        parts[i].wait()
+
+        def tile(t, c):
+            at = pl.ds(pl.multiple_of(t * TILE, TILE), TILE)
+            wide[i, at, :] = grads[i, at, :].astype(F32)
+            grad_copy(i, t).start()
+            return c
+
+        lax.fori_loop(0, tiles, tile, 0)
     for cp in first:
         cp.wait()
     for s in range(8):
@@ -1172,16 +1201,15 @@
     ggain[...] = gain_part[...]
     for cp in stores:
         cp.wait()
-    for k in range(2):
+    for i in range(4):
         for t in range(tiles):
-            tile_copy(tile_in, gein, 0, k, t).wait()
-            tile_copy(tile_out, geout, 2, k, t).wait()
-
-
-def final_block(dnorm, tokens, gain_col, grad_resid, gq_land, go_land, qkv_weight, gc_land, gain_part, n, h, df, du):
+            grad_copy(i, t).wait()
+
+
+def final_block(dnorm, tokens, gain_col, grad_resid, gq_land, go_land, qkv_weight, gc_land, gain_part, grads):
     rows, width = tokens.shape
     shard = width // 4
-    hidden = h.shape[2]
+    hidden = grads.shape[1]
     any_spec = pl.BlockSpec(memory_space=pl.ANY)
     vmem_spec = pl.BlockSpec(memory_space=pltpu.VMEM)
     S = jax.ShapeDtypeStruct
@@ -1193,11 +1221,10 @@
             S((rows, width), F32), S((shard, 3 * width), F32), S((shard, width), F32), S((1, shard), F32),
             S((8, shard), F32), S((2, shard), F32), S((2, hidden, width), F32), S((2, hidden, width), F32),
         ),
-        in_specs=[any_spec] * 2 + [vmem_spec] + [any_spec] * 4 + [vmem_spec] * 2 + [any_spec] * 4,
+        in_specs=[any_spec] * 2 + [vmem_spec] + [any_spec] * 4 + [vmem_spec] * 2 + [any_spec],
         out_specs=(any_spec,) * 3 + (vmem_spec,) * 3 + (any_spec,) * 2,
-        scratch_shapes=[V(n.shape, BF), V(h.shape, BF), V(df.shape, BF), V(du.shape, BF)]
-        + [V((2, hidden, width), F32)] * 2
-        + [
+        scratch_shapes=[
+            V(grads.shape, BF), V(grads.shape, F32),
             V((rows, width), F32), V((rows, width), BF), V((rows, width), F32),
             V(gq_land.shape, BF), V(go_land.shape, BF), V((shard, 3 * width), BF),
             V((rows, width), F32),
@@ -1206,7 +1233,7 @@
         ],
         compiler_params=pltpu.CompilerParams(vmem_limit_bytes=58 * 1024 * 1024),
         name="final_block",
-    )(dnorm, tokens, gain_col, grad_resid, gq_land, go_land, qkv_weight, gc_land, gain_part, n, h, df, du)
+    )(dnorm, tokens, gain_col, grad_resid, gq_land, go_land, qkv_weight, gc_land, gain_part, grads)
 
 
 def on_device_split(
@@ -1258,13 +1285,14 @@
     grad_resid = grad_out + grad_logit[:, None] * centroid_rows + back_rows
     grad_attended = grad_resid.astype(BF)
     grad_mixed = lax.dot_general(grad_attended, wout_full, NT, preferred_element_type=F32).astype(BF)
-    dnormed, gq_land, go_land, gc_land = back_block(
+    dnormed, gq_land, go_land, gc_land, expert_grads = back_block(
         grad_mixed, grad_attended, qkv, mixed, lse_rows, normed_all,
         olow_full.reshape(experts * rows, width), grad_centroid[:, None, :], qkv_weight, wfirst,
+        n_rows, h_rows, df_rows, du_rows,
     )
     grad_tokens, grad_qkv, grad_out_weight, grad_norm_gain, grad_centroids, grad_gain, grad_expert_in, grad_expert_out = final_block(
         dnormed, tokens, gain_col, grad_resid, gq_land, go_land, qkv_weight, gc_land, gain_part,
-        n_rows, h_rows, df_rows, du_rows,
+        expert_grads,
     )
     return (
         block_out,

time: 239 us -> 236 us (0.987)
    pallas_call x1, Pallas kernels: 16.5 us -> 13.6 us  [final_block(): pl.pallas_call(final_kernel, out_shape=(S((rows, width), F32), S((shard,...]
where the time goes in v7:
time: 236 us
  Pallas kernels  221 us (94%)
  matrix products  10.8 us (5%)
  local copies, waits for them, and re-layouts  2.82 us (1%)
    pallas_call x1, Pallas kernels, expert_block(): pl.pallas_call(expert_kernel, out_shape=(S(zslots.shape, BF), S(zslots.sh...  91.5 us
    pallas_call x1, Pallas kernels, back_block(): pl.pallas_call(back_kernel, out_shape=(S((rows, width), F32), S((8, 3 * s...  67 us
    pallas_call x1, Pallas kernels, front_block(): pl.pallas_call(front_kernel, out_shape=(S((rows, width), BF), S((seq, wid...  48.6 us
    pallas_call x1, Pallas kernels, final_block(): pl.pallas_call(final_kernel, out_shape=(S((rows, width), F32), S((shard,...  13.6 us

profile of v7, /device:TPU:0, one launch (start us, length us, event | category | flops | bytes accessed | tf_op | source)
XLA Modules:
  0.0 236.0 jit_solution(454280091211558830)
XLA Ops:
  0.6 0.0 copy-start.3
  0.7 0.0 copy-start.4
  0.7 1.0 fusion
  1.6 0.7 convert_add_fusion.1
  2.3 1.2 broadcast_in_dim.29.norm_gain
  3.5 48.6 %front_block.1 = (bf16[128,1024]{1,0:T(8,128)(2,1)}, bf16[1024,1024]{1,0:T(8,128)(2,1)}, bf16[1024,384]{1,0:T(8,128)(2,1)}, f32[1024,128]{1,0:T(8,128)}, bf16[10...) custom-call(bf16[128,1024]{1,0:T(8,128)(2,1)} %tok_hbm.1, ...), custom_call_target="tpu_custom_call" | custom-call | tf_op jit(solution)/shard_map/front_block/pallas_call | solution.py:444
  52.1 0.0 copy-done.4
  52.1 1.0 fusion.19
  53.1 0.0 copy-done.3
  53.1 0.0 copy-start.2
  53.1 2.3 fusion.27
  55.4 0.0 copy-done.2
  55.4 0.1 fusion.1
  55.5 0.4 convolution_convert_fusion
  55.9 0.9 fusion.26
  56.8 91.5 %expert_block.1 = (bf16[8,24,1024]{2,1,0:T(8,128)(2,1)}, bf16[8,24,1024]{2,1,0:T(8,128)(2,1)}, bf16[8,128,1024]{2,1,0:T(8,128)(2,1)}, f32[2,256]{1,0:T(2,128)}, ...) custom-call(bf16[8,24,1024]{2,1,0:T(8,128)(2,1)} %bitcast.20, ...), custom_call_target="tpu_custom_call" | custom-call | tf_op jit(solution)/shard_map/expert_block/pallas_call | solution.py:805
  148.3 0.0 copy-start
  148.3 2.2 fusion.2
  150.6 0.4 fusion.6
  151.0 0.6 broadcast_in_dim.32.cent
  151.6 2.1 fusion.28
  153.7 1.6 convolution_convert_fusion.1.gmix
  155.3 67.0 %back_block.1 = (f32[128,1024]{1,0:T(8,128)}, bf16[8,768,128]{2,1,0:T(8,128)(2,1)}, bf16[8,256,128]{2,1,0:T(8,128)(2,1)}, f32[8,1,256]{2,1,0:T(1,128)}, bf16[4,1024,1024]{2,1,0:T(8,128)(2,1)}) custom-call(bf16[128,1024]{1,0:T(8,128)(2,1)} %convolution_convert_fusion.1.gmix, bf16[128,1024]{1,0:T(8,128)(2,1)} %copy-done.1, ...), custom_call_target="tpu_custom_call" | custom-call | tf_op jit(solution)/shard_map/back_block/pallas_call | solution.py:1094
  222.3 13.6 %final_block.1 = (f32[128,1024]{1,0:T(8,128)}, f32[256,3072]{1,0:T(8,128)}, f32[256,1024]{1,0:T(8,128)}, f32[1,256]{1,0:T(1,128)}, f32[8,256]{1,0:T(8,128)}, /*i...) custom-call(f32[128,1024]{1,0:T(8,128)} %get-tuple-element.56.dnorm_hbm, ...), custom_call_target="tpu_custom_call" | custom-call | tf_op jit(solution)/shard_map/final_block/pallas_call | solution.py:1218
  (6 shorter events, 0.0 us)
Async XLA Ops:
  0.6 52.5 %copy-start.3 = (bf16[128,1024]{1,0:T(8,128)(2,1)S(1)}, bf16[128,1024]{1,0:T(8,128)(2,1)}, u32[]{:S(2)}) copy-start(bf16[128,1024]{1,0:T(8,128)(2,1)} %tok_hbm.1) | copy-start | bytes 786436
  0.7 51.4 %copy-start.4 = (s32[128,1]{0,1:T(1,128)S(1)}, s32[128,1]{0,1:T(1,128)}, u32[]{:S(2)}) copy-start(s32[128,1]{0,1:T(1,128)} %param.18) | copy-start | bytes 1540
  53.1 2.3 copy-start.2
  148.3 5.4 %copy-start = (bf16[1024,1024]{1,0:T(8,128)(2,1)S(1)}, bf16[1024,1024]{1,0:T(8,128)(2,1)}, u32[]{:S(2)}) copy-start(bf16[1024,1024]{1,0:T(8,128)(2,1)} %get-tuple-element.41) | copy-start | bytes 6291460
  153.7 1.6 copy-start.1
